TPU v7x, 32 devices: a whole 2x2x4 slice. The times are simulated.
32 devices in a mesh: dp: 8 (over y, x, core), expert: 4 (over z).
Axes of the slice: x: 2, y: 2, z: 4, core: 2. Of those that a mesh axis runs over, the one named last changes fastest.
Arguments:
- tokens: bfloat16 [4096, 1536], P(('dp', 'expert')), may hold values from -6 to 6
- segment_ids: int32 [32, 128], P(('dp', 'expert')), may hold values from 0 to 3, never falling along the last dimension, each value on 1 to 64 neighbouring positions
- routes: int32 [4096, 8], P(('dp', 'expert')), may hold values from 0 to 19, as said below
- cotangent: bfloat16 [4096, 1536], P(('dp', 'expert')), may hold values from -6 to 6
- query_weight: bfloat16 [1536, 1536], P('dp'), may hold values from -0.15625 to 0.15625
- key_weight: bfloat16 [1536, 512], P('dp'), may hold values from -0.15625 to 0.15625
- value_matrix: bfloat16 [1536, 512], P('dp'), may hold values from -0.15625 to 0.15625
- out_weight: bfloat16 [1536, 1536], P('dp'), may hold values from -1.25 to 1.25
- first_gain: bfloat16 [1536], P('dp'), may hold values from 0.5 to 1.5
- second_gain: bfloat16 [1536], P('dp'), may hold values from 0.5 to 1.5
- router_weight: bfloat16 [1536, 20], P('dp'), may hold values from -0.078125 to 0.078125
- gate_weight: bfloat16 [20, 1536, 512], P('expert'), may hold values from -0.15625 to 0.15625
- up_weight: bfloat16 [20, 1536, 512], P('expert'), may hold values from -0.15625 to 0.15625
- down_weight: bfloat16 [20, 512, 1536], P('expert'), may hold values from -0.5 to 0.5
Outputs:
- layer_out: bfloat16 [4096, 1536], P(('dp', 'expert'))
- input_grad: float32 [4096, 1536], P(('dp', 'expert'))
- query_grad: float32 [1536, 1536], P('dp')
- key_grad: float32 [1536, 512], P('dp')
- value_grad: float32 [1536, 512], P('dp')
- out_grad: float32 [1536, 1536], P('dp')
- first_grad: float32 [1536], P('dp')
- second_grad: float32 [1536], P('dp')
- router_grad: float32 [1536, 20], P('dp')
- gate_grad: float32 [20, 1536, 512], P('expert', 'dp')
- up_grad: float32 [20, 1536, 512], P('expert', 'dp')
- down_grad: float32 [20, 512, 1536], P('expert', 'dp')
Inputs may be any that keep to these rules, and one draw needn't show every extreme that they name: `segment_ids`: within each row the segment ids start at 0, never fall and take 4 values; a sequence has at most 64 tokens and some sequence has exactly that many. `routes`: each token names 8 different experts. Among the 128 tokens of one device no expert is named more than 96 times; in every such block between four and eight experts are named exactly 96 times.
All inputs are finite; a program needn't handle non-finite values.
Results may differ from a plain program's by a relative error of at most 0.012.
Values may be sent and summed in bfloat16 or wider, within the bound.
No kernel may reach another device: no remote copies, remote signals or barrier semaphores. Data moves between devices by JAX's collectives and lax.ppermute only.
A program may use at most 256 MiB of HBM per device.

v0:
```python
import jax
import jax.numpy as jnp
from jax import lax
from jax.sharding import PartitionSpec as P

HEAD_SIZE = 64
CAP = 96


EPSILON = 1e-06
ROTARY_BASE = 10000.0
SCORE_FACTOR = 0.015625
HIGHEST = lax.Precision.HIGHEST


def rope_tables(positions, width):
    half = width // 2
    freq = ROTARY_BASE ** (-jnp.arange(half, dtype=jnp.float32) * 2.0 / width)
    angle = positions.astype(jnp.float32)[:, None] * freq[None, :]
    return (jnp.cos(angle)[:, None, :], jnp.sin(angle)[:, None, :])


def rotate(field, cosine, sine):
    half = field.shape[-1] // 2
    first, second = (field[..., :half], field[..., half:])
    return jnp.concatenate(
        [first * cosine - second * sine, second * cosine + first * sine], axis=-1
    )


def rotate_back(grad, cosine, sine):
    half = grad.shape[-1] // 2
    first, second = (grad[..., :half], grad[..., half:])
    return jnp.concatenate(
        [first * cosine + second * sine, second * cosine - first * sine], axis=-1
    )


def positions_of(segments):
    count = segments.shape[0]
    earlier = jnp.sum((segments[None, :] < segments[:, None]).astype(jnp.int32), axis=1)
    return jnp.arange(count, dtype=jnp.int32) - earlier


def attention_mask(segments):
    count = segments.shape[0]
    index = jnp.arange(count, dtype=jnp.int32)
    return (segments[:, None] == segments[None, :]) & (index[None, :] <= index[:, None])


def rms_forward(field, gain):
    inverse = lax.rsqrt(jnp.mean(field * field, axis=-1, keepdims=True) + EPSILON)
    return (inverse, field * inverse * gain.astype(jnp.float32))


def rms_backward(field, inverse, gain, grad):
    scaled = grad * gain.astype(jnp.float32)
    inner = jnp.mean(scaled * field, axis=-1, keepdims=True)
    return (inverse * scaled - field * inverse**3 * inner, jnp.sum(grad * field * inverse, axis=0))


def score_block(query_rows, key_rows, mask):
    score_matrix = (
        jnp.einsum("qean,wen->eaqw", query_rows, key_rows, preferred_element_type=jnp.float32)
        * SCORE_FACTOR
    )
    return jnp.where(mask[None, None], score_matrix, -1e30)


def expert_front(arrived, gate_weight, up_weight):
    gate_pre = jnp.einsum("erd,edh->erh", arrived, gate_weight, preferred_element_type=jnp.float32)
    up_pre = jnp.einsum("erd,edh->erh", arrived, up_weight, preferred_element_type=jnp.float32)
    hidden = (jax.nn.silu(gate_pre) * up_pre).astype(jnp.bfloat16)
    return (gate_pre, up_pre, hidden)


def local(
    tokens,
    segment_ids,
    routes,
    cotangent,
    query_weight,
    key_weight,
    value_matrix,
    out_weight,
    first_gain,
    second_gain,
    router_weight,
    gate_weight,
    up_weight,
    down_weight,
):
    gathered = (
        lax.all_gather(query_weight, "dp", axis=0, tiled=True),
        lax.all_gather(key_weight, "dp", axis=0, tiled=True),
        lax.all_gather(value_matrix, "dp", axis=0, tiled=True),
        lax.all_gather(out_weight, "dp", axis=0, tiled=True),
        lax.all_gather(first_gain, "dp", axis=0, tiled=True),
        lax.all_gather(second_gain, "dp", axis=0, tiled=True),
        lax.all_gather(router_weight, "dp", axis=0, tiled=True),
    )
    query_full, key_full, value_full, out_full, gain_one, gain_two, router_full = gathered
    token_rows, width = tokens.shape
    query_head_rows = query_full.shape[1] // HEAD_SIZE
    key_heads = key_full.shape[1] // HEAD_SIZE
    head_group = query_head_rows // key_heads
    experts = router_full.shape[1]
    choices_per = routes.shape[1]
    segments = segment_ids[0]
    mask = attention_mask(segments)
    cosine, sine = rope_tables(positions_of(segments), HEAD_SIZE)
    inputs = tokens.astype(jnp.float32)
    first_inverse, normed1 = rms_forward(inputs, gain_one)
    normed1 = normed1.astype(jnp.bfloat16)
    query_rows = rotate(
        jnp.dot(normed1, query_full, preferred_element_type=jnp.float32).reshape(
            token_rows, query_head_rows, HEAD_SIZE
        ),
        cosine,
        sine,
    )
    query_rows = query_rows.astype(jnp.bfloat16).reshape(
        token_rows, key_heads, head_group, HEAD_SIZE
    )
    key_rows = rotate(
        jnp.dot(normed1, key_full, preferred_element_type=jnp.float32).reshape(
            token_rows, key_heads, HEAD_SIZE
        ),
        cosine,
        sine,
    ).astype(jnp.bfloat16)
    value_rows = (
        jnp.dot(normed1, value_full, preferred_element_type=jnp.float32)
        .astype(jnp.bfloat16)
        .reshape(token_rows, key_heads, HEAD_SIZE)
    )
    score_matrix = score_block(query_rows, key_rows, mask)
    peak = jnp.max(score_matrix, axis=-1, keepdims=True)
    logsum = peak + jnp.log(jnp.sum(jnp.exp(score_matrix - peak), axis=-1, keepdims=True))
    probabilities = jnp.exp(score_matrix - logsum).astype(jnp.bfloat16)
    mixed_values = jnp.einsum(
        "wmik,kwy->iwmy", probabilities, value_rows, preferred_element_type=jnp.float32
    )
    mixed_values = mixed_values.astype(jnp.bfloat16).reshape(
        token_rows, query_head_rows * HEAD_SIZE
    )
    resid = inputs + jnp.dot(mixed_values, out_full, preferred_element_type=jnp.float32)
    second_inverse, normed2 = rms_forward(resid, gain_two)
    normed2 = normed2.astype(jnp.bfloat16)
    logits = jnp.dot(normed2, router_full, preferred_element_type=jnp.float32)
    choose = (routes[:, :, None] == jnp.arange(experts, dtype=jnp.int32)[None, None, :]).astype(
        jnp.float32
    )
    chosen = jnp.sum(choose * logits[:, None, :], axis=-1)
    top = jnp.max(chosen, axis=-1, keepdims=True)
    raised = jnp.exp(chosen - top)
    gates = raised / jnp.sum(raised, axis=-1, keepdims=True)
    flat = routes.reshape(-1)
    hits = (flat[:, None] == jnp.arange(experts, dtype=jnp.int32)[None, :]).astype(jnp.int32)
    slots = jnp.sum((jnp.cumsum(hits, axis=0) - hits) * hits, axis=1)
    empty = jnp.zeros((experts, CAP, width), jnp.bfloat16)
    outgoing = empty.at[flat, slots].set(jnp.repeat(normed2, choices_per, axis=0))
    arrived = lax.all_to_all(outgoing, "expert", split_axis=0, concat_axis=1, tiled=True)
    gate_pre, up_pre, hidden = expert_front(arrived, gate_weight, up_weight)
    produced = jnp.einsum(
        "erh,ehd->erd", hidden, down_weight, preferred_element_type=jnp.float32
    ).astype(jnp.bfloat16)
    returned = lax.all_to_all(produced, "expert", split_axis=1, concat_axis=0, tiled=True)
    picked = returned[flat, slots].reshape(token_rows, choices_per, width)
    combined = jnp.einsum("tk,tkd->td", gates, picked.astype(jnp.float32), precision=HIGHEST)
    layer_out = (resid + combined).astype(jnp.bfloat16)
    grad_out = cotangent.astype(jnp.float32)
    gate_back = jnp.einsum("td,tkd->tk", cotangent, picked, preferred_element_type=jnp.float32)
    chosen_back = gates * (gate_back - jnp.sum(gates * gate_back, axis=-1, keepdims=True))
    logit_back = jnp.sum(choose * chosen_back[:, :, None], axis=1)
    router_part = jnp.dot(normed2.astype(jnp.float32).T, logit_back, precision=HIGHEST)
    normed2_back = jnp.dot(logit_back, router_full.astype(jnp.float32).T, precision=HIGHEST)
    row_grads = (
        (gates[:, :, None] * grad_out[:, None, :])
        .astype(jnp.bfloat16)
        .reshape(token_rows * choices_per, width)
    )
    leaving = empty.at[flat, slots].set(row_grads)
    incoming = lax.all_to_all(leaving, "expert", split_axis=0, concat_axis=1, tiled=True)
    landed, gate_again, up_again, hidden_again = (arrived, gate_pre, up_pre, hidden)
    hidden_back = jnp.einsum(
        "erd,ehd->erh", incoming, down_weight, preferred_element_type=jnp.float32
    )
    sigma = jax.nn.sigmoid(gate_again)
    gate_rows = (hidden_back * up_again * sigma * (1.0 + gate_again * (1.0 - sigma))).astype(
        jnp.bfloat16
    )
    up_rows = (hidden_back * gate_again * sigma).astype(jnp.bfloat16)
    down_part = jnp.einsum(
        "erh,erd->ehd", hidden_again, incoming, preferred_element_type=jnp.float32
    )
    gate_part = jnp.einsum("erd,erh->edh", landed, gate_rows, preferred_element_type=jnp.float32)
    up_part = jnp.einsum("erd,erh->edh", landed, up_rows, preferred_element_type=jnp.float32)
    rows_back = jnp.einsum(
        "erh,edh->erd", gate_rows, gate_weight, preferred_element_type=jnp.float32
    )
    rows_back = (
        rows_back
        + jnp.einsum("erh,edh->erd", up_rows, up_weight, preferred_element_type=jnp.float32)
    ).astype(jnp.bfloat16)
    expert_sums = (gate_part, up_part, down_part)
    coming_back = lax.all_to_all(rows_back, "expert", split_axis=1, concat_axis=0, tiled=True)
    normed2_back = normed2_back + jnp.sum(
        coming_back[flat, slots].reshape(token_rows, choices_per, width).astype(jnp.float32), axis=1
    )
    resid_part, second_part = rms_backward(resid, second_inverse, gain_two, normed2_back)
    resid_back = grad_out + resid_part
    attended_back = resid_back.astype(jnp.bfloat16)
    out_part = jnp.dot(mixed_values.T, attended_back, preferred_element_type=jnp.float32)
    mixed_values_gradient = jnp.dot(
        attended_back, out_full.T, preferred_element_type=jnp.float32
    ).astype(jnp.bfloat16)
    mixed_values_gradient = mixed_values_gradient.reshape(
        token_rows, key_heads, head_group, HEAD_SIZE
    )
    second_pass = jnp.exp(score_block(query_rows, key_rows, mask) - logsum)
    value_rows_gradient = jnp.einsum(
        "kjal,akjx->lkx",
        second_pass.astype(jnp.bfloat16),
        mixed_values_gradient,
        preferred_element_type=jnp.float32,
    )
    probability_gradient = jnp.einsum(
        "qean,wen->eaqw", mixed_values_gradient, value_rows, preferred_element_type=jnp.float32
    )
    delta = jnp.sum(second_pass * probability_gradient, axis=-1, keepdims=True)
    score_gradient = (second_pass * (probability_gradient - delta) * SCORE_FACTOR).astype(
        jnp.bfloat16
    )
    query_rows_gradient = jnp.einsum(
        "wmik,kwy->iwmy", score_gradient, key_rows, preferred_element_type=jnp.float32
    ).reshape(token_rows, query_head_rows, HEAD_SIZE)
    key_rows_gradient = jnp.einsum(
        "kjal,akjx->lkx", score_gradient, query_rows, preferred_element_type=jnp.float32
    )
    query_rows_gradient = (
        rotate_back(query_rows_gradient, cosine, sine)
        .astype(jnp.bfloat16)
        .reshape(token_rows, query_head_rows * HEAD_SIZE)
    )
    key_rows_gradient = (
        rotate_back(key_rows_gradient, cosine, sine)
        .astype(jnp.bfloat16)
        .reshape(token_rows, key_heads * HEAD_SIZE)
    )
    value_rows_gradient = value_rows_gradient.astype(jnp.bfloat16).reshape(
        token_rows, key_heads * HEAD_SIZE
    )
    query_part = jnp.dot(normed1.T, query_rows_gradient, preferred_element_type=jnp.float32)
    key_part = jnp.dot(normed1.T, key_rows_gradient, preferred_element_type=jnp.float32)
    value_part = jnp.dot(normed1.T, value_rows_gradient, preferred_element_type=jnp.float32)
    normed1_back = jnp.dot(query_rows_gradient, query_full.T, preferred_element_type=jnp.float32)
    normed1_back = normed1_back + jnp.dot(
        key_rows_gradient, key_full.T, preferred_element_type=jnp.float32
    )
    normed1_back = normed1_back + jnp.dot(
        value_rows_gradient, value_full.T, preferred_element_type=jnp.float32
    )
    input_part, first_part = rms_backward(inputs, first_inverse, gain_one, normed1_back)
    input_grad = resid_back + input_part
    partial_sums = (
        lax.psum_scatter(query_part, "dp", scatter_dimension=0, tiled=True),
        lax.psum_scatter(key_part, "dp", scatter_dimension=0, tiled=True),
        lax.psum_scatter(value_part, "dp", scatter_dimension=0, tiled=True),
        lax.psum_scatter(out_part, "dp", scatter_dimension=0, tiled=True),
        lax.psum_scatter(first_part, "dp", scatter_dimension=0, tiled=True),
        lax.psum_scatter(second_part, "dp", scatter_dimension=0, tiled=True),
        lax.psum_scatter(router_part, "dp", scatter_dimension=0, tiled=True),
    )
    totals = lax.psum(
        (
            partial_sums[0],
            partial_sums[1],
            partial_sums[2],
            partial_sums[3],
            partial_sums[4],
            partial_sums[5],
            partial_sums[6],
        ),
        "expert",
    )
    expert_sums = (
        lax.psum_scatter(gate_part, "dp", scatter_dimension=1, tiled=True),
        lax.psum_scatter(up_part, "dp", scatter_dimension=1, tiled=True),
        lax.psum_scatter(down_part, "dp", scatter_dimension=1, tiled=True),
    )
    return (
        layer_out,
        input_grad,
        totals[0],
        totals[1],
        totals[2],
        totals[3],
        totals[4],
        totals[5],
        totals[6],
        expert_sums[0],
        expert_sums[1],
        expert_sums[2],
    )


def solution(mesh):
    return jax.shard_map(
        local,
        mesh=mesh,
        in_specs=(
            P(("dp", "expert"), None),
            P(("dp", "expert"), None),
            P(("dp", "expert"), None),
            P(("dp", "expert"), None),
            P("dp", None),
            P("dp", None),
            P("dp", None),
            P("dp", None),
            P("dp"),
            P("dp"),
            P("dp", None),
            P("expert", None, None),
            P("expert", None, None),
            P("expert", None, None),
        ),
        out_specs=(
            P(("dp", "expert"), None),
            P(("dp", "expert"), None),
            P("dp", None),
            P("dp", None),
            P("dp", None),
            P("dp", None),
            P("dp"),
            P("dp"),
            P("dp", None),
            P("expert", "dp", None),
            P("expert", "dp", None),
            P("expert", "dp", None),
        ),
        check_vma=False,
    )
```

profile of v0, /device:TPU:0, one launch (start us, length us, event | category | flops | bytes accessed | tf_op | source)
XLA Modules:
  0.0 1799.6 jit_solution(2375361750178085493)
XLA Ops:
  14.8 15.5 all-reduce.7
  40.5 25.7 %all-gather.8.cloned.1.call-done = bf16[1536,512]{1,0:T(8,128)(2,1)} async-done(((bf16[192,512]{1,0:T(8,128)(2,1)}), bf16[1536,512]{1,0:T(8,128)(2,1)}) %all-gather.8.cloned.1.call-update) | async-done | bytes 1572880 | tf_op jit(solution)/shard_map/all_gather | solution.py:95
  68.4 38.6 %all-gather.10.cloned.1.call-done = bf16[1536,1536]{1,0:T(8,128)(2,1)} async-done(((bf16[192,1536]{1,0:T(8,128)(2,1)}), bf16[1536,1536]{1,0:T(8,128)(2,1)}) %all-gather.10.cloned.1.call-update) | async-done | bytes 4718608 | tf_op jit(solution)/shard_map/all_gather | solution.py:94
  114.2 33.5 %all-gather.12.cloned.1.call-done = bf16[1536,1536]{1,0:T(8,128)(2,1)} async-done(((bf16[192,1536]{1,0:T(8,128)(2,1)}), bf16[1536,1536]{1,0:T(8,128)(2,1)}) %all-gather.12.cloned.1.call-update) | async-done | bytes 4718608 | tf_op jit(solution)/shard_map/all_gather | solution.py:97
  152.0 9.2 scatter_custom_fusion
  161.2 134.7 %all_to_all.72 = bf16[20,96,1536]{2,1,0:T(8,128)(2,1)S(1)} all-to-all(bf16[20,96,1536]{2,1,0:T(8,128)(2,1)} %bitcast.191), channel_id=1, replica_groups=mesh['dp'=8,'expert'=4] {'expert'}, dimensions={0} | all-to-all | bytes 11796480 | tf_op jit(solution)/shard_map/all_to_all | solution.py:163
  296.4 10.8 fusion.76
  322.8 10.0 copy.108
  338.8 9.4 all-gather
  350.2 193.8 %all-to-all-done.1 = bf16[5,384,1536]{2,0,1:T(8,128)(2,1)} async-done(((bf16[5,384,1536]{2,0,1:T(8,128)(2,1)}), bf16[5,384,1536]{2,0,1:T(8,128)(2,1)}, u32[]{:S(2)}, u32[]{:S(2)}) %all-to-all-start.1) | async-done | bytes 5898272 | tf_op jit(solution)/shard_map/all_to_all | solution.py:168
  552.4 17.8 gather_fusion
  576.3 9.6 scatter_custom_fusion.1
  585.9 133.6 %all_to_all.73 = bf16[20,96,1536]{2,1,0:T(8,128)(2,1)S(1)} all-to-all(bf16[20,96,1536]{2,1,0:T(8,128)(2,1)} %bitcast.188), channel_id=1, replica_groups=mesh['dp'=8,'expert'=4] {'expert'}, dimensions={0} | all-to-all | bytes 11796480 | tf_op jit(solution)/shard_map/all_to_all | solution.py:184
  722.6 12.6 multiply_convert_fusion
  735.2 11.2 fusion.77
  746.4 13.0 add_convert_fusion
  759.4 10.0 copy.112
  781.1 198.8 %all-to-all-done.3 = bf16[5,384,1536]{2,0,1:T(8,128)(2,1)} async-done(((bf16[5,384,1536]{2,0,1:T(8,128)(2,1)}), bf16[5,384,1536]{2,0,1:T(8,128)(2,1)}, u32[]{:S(2)}, u32[]{:S(2)}) %all-to-all-start.3) | async-done | bytes 5898272 | tf_op jit(solution)/shard_map/all_to_all | solution.py:207
  988.4 23.3 %gather_fusion.1 = bf16[1024,1536]{1,0:T(8,128)(2,1)} fusion(bf16[20,96,1536]{2,1,0:T(8,128)(2,1)} %bitcast.181, s32[1024]{0:T(1024)S(1)} %bitcast.179), kind=kCustom, calls=%fused_computation.1 | custom fusion | bytes 6299648 | tf_op jit(solution)/shard_map/gather | solution.py:209
  1060.2 13.1 fusion.83
  1073.6 13.9 fusion.82
  1087.6 11.3 fusion.81
  1099.0 24.6 %reduce-scatter.13.cloned.1.call-done = f32[192,512]{1,0:T(8,128)} async-done(((f32[1536,512]{1,0:T(8,128)}), f32[192,512]{1,0:T(8,128)}) %reduce-scatter.13.cloned.1.call-update) | async-done | bytes 393232 | tf_op jit(solution)/shard_map/reduce_scatter | solution.py:268
  1123.6 80.0 %reduce-scatter.17.cloned.1.call-done = f32[192,1536]{1,0:T(8,128)} async-done(((f32[1536,1536]{1,0:T(8,128)}), f32[192,1536]{1,0:T(8,128)}) %reduce-scatter.17.cloned.1.call-update) | async-done | bytes 1179664 | tf_op jit(solution)/shard_map/reduce_scatter | solution.py:270
  1203.6 80.0 %reduce-scatter.11.cloned.1.call-done = f32[192,1536]{1,0:T(8,128)} async-done(((f32[1536,1536]{1,0:T(8,128)}), f32[192,1536]{1,0:T(8,128)}) %reduce-scatter.11.cloned.1.call-update) | async-done | bytes 1179664 | tf_op jit(solution)/shard_map/reduce_scatter | solution.py:267
  1284.4 37.9 %reduce-scatter.25.cloned.1.call-done = f32[192,20]{1,0:T(8,128)} async-done(((f32[1536,20]{1,0:T(8,128)}), f32[192,20]{1,0:T(8,128)}) %reduce-scatter.25.cloned.1.call-update) | async-done | bytes 15376
  1329.1 22.8 %all-reduce.4 = (f32[1536]{0:T(1024)S(1)}, f32[1536]{0:T(1024)S(1)}) all-reduce(f32[1536]{0:T(1024)S(1)} %get-tuple-element.14, f32[1536]{0:T(1024)S(1)} %copy-done.47), channel_id=6, replica_groups=mesh['dp'=8,'expert'=4] {'dp'}, use_global_device_ids=true, to_apply=%region_28.29.clone | all-reduce | flops 3072 | bytes 24576
  1352.0 19.6 %all-reduce.5 = (f32[192]{0:T(256)}, f32[192]{0:T(256)}, f32[192,20]{0,1:T(8,128)}) all-reduce(f32[192]{0:T(256)S(1)} %dynamic-slice.3, f32[192]{0:T(256)S(1)} %dynamic-slice.5, f32[192,20]{0,1:T(8,128)S(1)} %copy.139), channel_id=1, replica_groups=mesh['dp'=8,'expert'=4] {'expert'}, use_global_device_ids=true, to_apply=%region_29.30 | all-reduce | flops 4224 | bytes 33792 | tf_op jit(solution)/shard_map/psum | solution.py:275
  1372.8 62.7 %reduce-scatter.23.cloned.1.call-done = f32[5,64,1536]{2,1,0:T(8,128)} async-done(((f32[5,512,1536]{2,1,0:T(8,128)}), f32[5,64,1536]{2,1,0:T(8,128)}) %reduce-scatter.23.cloned.1.call-update) | async-done | bytes 1966096 | tf_op jit(solution)/shard_map/reduce_scatter | solution.py:290
  1435.4 113.3 %reduce-scatter.21.cloned.1.call-done = f32[5,192,512]{2,1,0:T(8,128)} async-done(((f32[5,1536,512]{2,1,0:T(8,128)}), f32[5,192,512]{2,1,0:T(8,128)}) %reduce-scatter.21.cloned.1.call-update) | async-done | bytes 1966096 | tf_op jit(solution)/shard_map/reduce_scatter | solution.py:289
  1548.7 113.1 %reduce-scatter.19.cloned.1.call-done = f32[5,192,512]{2,1,0:T(8,128)} async-done(((f32[5,1536,512]{2,1,0:T(8,128)}), f32[5,192,512]{2,1,0:T(8,128)}) %reduce-scatter.19.cloned.1.call-update) | async-done | bytes 1966096 | tf_op jit(solution)/shard_map/reduce_scatter | solution.py:288
  1661.9 124.8 %all-reduce.10.cloned.1.call-done = (f32[192,1536]{1,0:T(8,128)}, f32[192,512]{1,0:T(8,128)}, f32[192,512]{1,0:T(8,128)}, f32[192,1536]{1,0:T(8,128)}) async-done(((f32[192,1536]{1,0:T(8,128)}, f32[192,512]{1,0:T(8,128)}, f32[192,512]{1,0:T(8,128)}, f32[192,1536]{1,0:T(8,128)}), (f32[192,1536]{1,0:T(8,128)}, f32[192,512]{1,0:T(8,128)}, f32[192,512]{1,0:T(8,128)}, ...) | async-done | bytes 3145744 | tf_op jit(solution)/shard_map/psum | solution.py:275
  (254 shorter events, 155.0 us)
Async XLA Ops:
  7.2 31.3 %all-gather.6.cloned.1.call-start = ((), (), s32[]{:S(2)}) async-start(), calls=%async_computation.12 | async-start | bytes 1769472 | tf_op jit(solution)/shard_map/all_gather | solution.py:96
  8.0 58.2 %all-gather.8.cloned.1.call-start = ((), (), s32[]{:S(2)}) async-start(), calls=%async_computation.13 | async-start | bytes 1769472 | tf_op jit(solution)/shard_map/all_gather | solution.py:95
  8.7 98.3 %all-gather.10.cloned.1.call-start = ((), (), s32[]{:S(2)}) async-start(), calls=%async_computation.14 | async-start | bytes 5308416 | tf_op jit(solution)/shard_map/all_gather | solution.py:94
  9.4 138.2 %all-gather.12.cloned.1.call-start = ((), (), s32[]{:S(2)}) async-start(), calls=%async_computation.15 | async-start | bytes 5308416 | tf_op jit(solution)/shard_map/all_gather | solution.py:97
  30.4 121.1 %copy-start.37 = (f32[1536]{0:T(1024)}, f32[1536]{0:T(1024)S(1)}, u32[]{:S(2)}) copy-start(f32[1536]{0:T(1024)S(1)} %convert_element_type.119) | copy-start | bytes 18436
  37.7 73.7 %copy-start.48 = (f32[128]{0:T(128)}, f32[128]{0:T(128)S(1)}, u32[]{:S(2)}) copy-start(f32[128]{0:T(128)S(1)} %get-tuple-element.49) | copy-start | bytes 1540
  37.7 114.3 %copy-start.54 = (s32[1024]{0:T(1024)}, s32[1024]{0:T(1024)S(1)}, u32[]{:S(2)}) copy-start(s32[1024]{0:T(1024)S(1)} %broadcast_select_fusion) | copy-start | bytes 12292
  37.9 73.5 %copy-start.26 = (f32[128,32]{0,1:T(8,128)}, f32[128,32]{0,1:T(8,128)S(1)}, u32[]{:S(2)}) copy-start(f32[128,32]{0,1:T(8,128)S(1)} %get-tuple-element.44) | copy-start | bytes 49156
  37.9 73.5 %copy-start.29 = (f32[128,32]{0,1:T(8,128)}, f32[128,32]{0,1:T(8,128)S(1)}, u32[]{:S(2)}) copy-start(f32[128,32]{0,1:T(8,128)S(1)} %get-tuple-element.45) | copy-start | bytes 49156
  40.5 72.5 %copy-start.20 = (bf16[128,512]{0,1:T(8,128)(2,1)}, bf16[128,512]{0,1:T(8,128)(2,1)S(1)}, u32[]{:S(2)}) copy-start(bf16[128,512]{0,1:T(8,128)(2,1)S(1)} %copy.97) | copy-start | bytes 393220
  68.4 43.1 %copy-start.40 = (bf16[128,8,32]{0,2,1:T(8,128)(2,1)}, bf16[128,8,32]{0,2,1:T(8,128)(2,1)S(1)}, u32[]{:S(2)}) copy-start(bf16[128,8,32]{0,2,1:T(8,128)(2,1)S(1)} %get-tuple-element.39) | copy-start | bytes 196612
  68.4 43.1 %copy-start.42 = (bf16[128,8,32]{0,2,1:T(8,128)(2,1)}, bf16[128,8,32]{0,2,1:T(8,128)(2,1)S(1)}, u32[]{:S(2)}) copy-start(bf16[128,8,32]{0,2,1:T(8,128)(2,1)S(1)} %get-tuple-element.40) | copy-start | bytes 196612
  114.2 36.7 %copy-start.9 = (bf16[8,64,3,128]{3,1,2,0:T(8,128)(2,1)}, bf16[8,64,3,128]{3,1,2,0:T(8,128)(2,1)S(1)}, u32[]{:S(2)}) copy-start(bf16[8,64,3,128]{3,1,2,0:T(8,128)(2,1)S(1)} %convolution_convert_fusion.2) | copy-start | bytes 1179652
  152.0 197.4 %copy-start.7 = (bf16[128,1536]{1,0:T(8,128)(2,1)}, bf16[128,1536]{1,0:T(8,128)(2,1)S(1)}, u32[]{:S(2)}) copy-start(bf16[128,1536]{1,0:T(8,128)(2,1)S(1)} %multiply_convert_fusion.3) | copy-start | bytes 1179652
  332.8 211.1 %all-to-all-start.1 = ((bf16[5,384,1536]{2,0,1:T(8,128)(2,1)}), bf16[5,384,1536]{2,0,1:T(8,128)(2,1)}, u32[]{:S(2)}, u32[]{:S(2)}) async-start(bf16[5,384,1536]{2,0,1:T(8,128)(2,1)} %copy.108), calls=%async_computation.1 | async-start | bytes 18874368 | tf_op jit(solution)/shard_map/all_to_all | solution.py:168
  348.4 204.1 %copy-start.24 = (bf16[1536,20]{0,1:T(8,128)(2,1)}, bf16[1536,20]{0,1:T(8,128)(2,1)S(1)}, u32[]{:S(2)}) copy-start(bf16[1536,20]{0,1:T(8,128)(2,1)S(1)} %reshape.368) | copy-start | bytes 184324
  349.6 202.8 %copy-start.53 = (f32[128]{0:T(128)}, f32[128]{0:T(128)S(1)}, u32[]{:S(2)}) copy-start(f32[128]{0:T(128)S(1)} %reduce_max.19) | copy-start | bytes 1540
  769.4 210.6 %all-to-all-start.3 = ((bf16[5,384,1536]{2,0,1:T(8,128)(2,1)}), bf16[5,384,1536]{2,0,1:T(8,128)(2,1)}, u32[]{:S(2)}, u32[]{:S(2)}) async-start(bf16[5,384,1536]{2,0,1:T(8,128)(2,1)} %copy.112), calls=%async_computation.3 | async-start | bytes 18874368 | tf_op jit(solution)/shard_map/all_to_all | solution.py:207
  775.3 323.7 %reduce-scatter.15.cloned.1.call-start = ((), (), s32[]{:S(2)}) async-start(), calls=%async_computation.18 | async-start | bytes 3538944 | tf_op jit(solution)/shard_map/reduce_scatter | solution.py:269
  775.7 240.2 %copy-start.39 = (f32[128,20]{0,1:T(8,128)}, f32[128,20]{0,1:T(8,128)S(1)}, u32[]{:S(2)}) copy-start(f32[128,20]{0,1:T(8,128)S(1)} %select_reduce_fusion) | copy-start | bytes 30724
  1029.2 94.4 %reduce-scatter.13.cloned.1.call-start = ((), (), s32[]{:S(2)}) async-start(), calls=%async_computation.17 | async-start | bytes 3538944 | tf_op jit(solution)/shard_map/reduce_scatter | solution.py:268
  1039.4 164.2 %reduce-scatter.17.cloned.1.call-start = ((), (), s32[]{:S(2)}) async-start(), calls=%async_computation.19 | async-start | bytes 10616832 | tf_op jit(solution)/shard_map/reduce_scatter | solution.py:270
  1044.5 239.2 %reduce-scatter.11.cloned.1.call-start = ((), (), s32[]{:S(2)}) async-start(), calls=%async_computation.16 | async-start | bytes 10616832 | tf_op jit(solution)/shard_map/reduce_scatter | solution.py:267
  1057.1 265.3 %reduce-scatter.25.cloned.1.call-start = ((), (), s32[]{:S(2)}) async-start(), calls=%async_computation.23 | async-start | bytes 884736
  1060.2 375.3 %reduce-scatter.23.cloned.1.call-start = ((), (), s32[]{:S(2)}) async-start(), calls=%async_computation.22 | async-start | bytes 17694720 | tf_op jit(solution)/shard_map/reduce_scatter | solution.py:290
  1073.3 475.4 %reduce-scatter.21.cloned.1.call-start = ((), (), s32[]{:S(2)}) async-start(), calls=%async_computation.21 | async-start | bytes 17694720 | tf_op jit(solution)/shard_map/reduce_scatter | solution.py:289
  1087.5 574.4 %reduce-scatter.19.cloned.1.call-start = ((), (), s32[]{:S(2)}) async-start(), calls=%async_computation.20 | async-start | bytes 17694720 | tf_op jit(solution)/shard_map/reduce_scatter | solution.py:288
  1098.9 224.4 %copy-start.12 = (bf16[128,24,64]{0,2,1:T(8,128)(2,1)S(1)}, bf16[128,24,64]{0,2,1:T(8,128)(2,1)}, u32[]{:S(2)}) copy-start(bf16[128,24,64]{0,2,1:T(8,128)(2,1)} %copy-done.11) | copy-start | bytes 1179652
  1098.9 687.7 %all-reduce.10.cloned.1.call-start = ((), (), s32[]{:S(2)}) async-start(), calls=%async_computation.24 | async-start | bytes 6291456 | tf_op jit(solution)/shard_map/psum | solution.py:275
  1283.6 43.9 %copy-start.6 = (bf16[1536,512]{1,0:T(8,128)(2,1)S(1)}, bf16[1536,512]{1,0:T(8,128)(2,1)}, u32[]{:S(2)}) copy-start(bf16[1536,512]{1,0:T(8,128)(2,1)} %all-gather.8.cloned.1.call-done) | copy-start | bytes 4718596
  1283.6 43.9 %copy-start.22 = (bf16[128,8,64]{0,2,1:T(8,128)(2,1)S(1)}, bf16[128,8,64]{0,2,1:T(8,128)(2,1)}, u32[]{:S(2)}) copy-start(bf16[128,8,64]{0,2,1:T(8,128)(2,1)} %copy-done.21) | copy-start | bytes 393220
  1327.6 44.0 %copy-start.59 = (f32[128]{0:T(128)S(1)}, f32[128]{0:T(128)}, u32[]{:S(2)}) copy-start(f32[128]{0:T(128)} %get-tuple-element.48) | copy-start | bytes 1540
  (45 other events, 319.1 us)
Sparse Core Ops, SparseCore 0:
  9.9 28.5 all-gather.5
  40.4 25.7 all-gather.7
  68.0 38.9 all-gather.9
  108.7 38.9 all-gather.11
  1029.3 44.3 reduce-scatter.14
  1077.4 46.2 reduce-scatter.12
  1127.1 76.4 reduce-scatter.16
  1207.1 76.4 reduce-scatter.10
  1287.3 34.9 reduce-scatter.24
  1326.3 109.1 reduce-scatter.22
  1439.5 109.1 reduce-scatter.20
  1552.7 109.1 reduce-scatter.18
  1664.5 122.1 all-reduce.9
where the time goes:
time: 1810 us; the launch traced here: 1800 us
  waiting for transfers between devices  1130 us (62%)
  blocking collectives  336 us (19%)
  matrix products  165 us (9%)
  local copies, waits for them, and re-layouts  111 us (6%)
  other arithmetic  27.9 us (2%)
    all_to_all x1, waiting for transfers between devices, local(): lax.all_to_all(rows_back, 'expert', split_axis=1, concat_axis=0, tiled=True)  199 us
    all_to_all x1, waiting for transfers between devices, local(): lax.all_to_all(produced, 'expert', split_axis=1, concat_axis=0, tiled=True)  194 us
    all_to_all x1, blocking collectives, local(): lax.all_to_all(outgoing, 'expert', split_axis=0, concat_axis=1, tiled=True)  135 us
    all_to_all x1, blocking collectives, local(): lax.all_to_all(leaving, 'expert', split_axis=0, concat_axis=1, tiled=True)  134 us
    psum x1, waiting for transfers between devices, local(): lax.psum((partial_sums[0], partial_sums[1], partial_sums[2], partial_sums...  125 us
    reduce_scatter x1, waiting for transfers between devices, local(): lax.psum_scatter(up_part, 'dp', scatter_dimension=1, tiled=True)  113 us
    reduce_scatter x1, waiting for transfers between devices, local(): lax.psum_scatter(gate_part, 'dp', scatter_dimension=1, tiled=True)  113 us
    reduce_scatter x1, waiting for transfers between devices, local(): lax.psum_scatter(out_part, 'dp', scatter_dimension=0, tiled=True)  80 us
  transfers between devices with their start and end apart: 15, of which 14 were waited for; matrix products, arithmetic and copies ran while one was open for 6% of the time, Pallas kernels for 0%

commit v1 on v0

v1 whole, which is shorter than its diff:
```python
import functools
import jax, jax.numpy as jnp
from jax import lax
from jax.experimental import pallas as pl
from jax.experimental.pallas import tpu as pltpu

F32=jnp.float32; BF=jnp.bfloat16
def dot_nn(a,b): return lax.dot_general(a,b,(((1,),(0,)),((),())),preferred_element_type=F32)
def dot_nt(a,b): return lax.dot_general(a,b,(((1,),(1,)),((),())),preferred_element_type=F32)

def column(table, lane):
    at = lax.broadcasted_iota(jnp.int32, table.shape, 1) == lane
    return jnp.sum(jnp.where(at, table, 0.0), axis=1, keepdims=True)

def expert_kernel(blocks, where_ref, *refs):
    n2_refs, refs = refs[:blocks], refs[blocks:]
    cot_refs, refs = refs[:blocks], refs[blocks:]
    route_refs, refs = refs[:blocks], refs[blocks:]
    (router_ref, gate_ref, up_ref, down_ref,
     comb_ref, rows_ref, aux_ref, gates_ref, n2t_ref, hid_ref, grow_ref, urow_ref,
     n2, cot, comb, rows) = refs
    e = pl.program_id(0)
    own = where_ref[0]; dev = where_ref[1]
    experts_here = pl.num_programs(0)
    T = n2_refs[0].shape[0]; W = n2_refs[0].shape[1]; H = gate_ref.shape[2]
    C = 512
    n_dp = n2t_ref.shape[0] * n2t_ref.shape[1]; R = W // n_dp; D = H // n_dp

    @pl.when(e == 0)
    def _():
        for b in range(blocks):
            n2[b * T:(b + 1) * T, :] = n2_refs[b][...]
            cot[b * T:(b + 1) * T, :] = cot_refs[b][...]
            logits = dot_nn(n2_refs[b][...], router_ref[...])
            lane = lax.broadcasted_iota(jnp.int32, logits.shape, 1)
            named = lane < 0
            for k in range(route_refs[b].shape[1]):
                named = named | (lane == route_refs[b][:, k:k + 1])
            logits = jnp.where(named, logits, -1e30)
            top = jnp.max(logits, axis=1, keepdims=True)
            raised = jnp.where(named, jnp.exp(logits - top), 0.0)
            gates_ref[b * T:(b + 1) * T, :] = raised / jnp.sum(raised, axis=1, keepdims=True)
        aux_ref[...] = jnp.zeros_like(aux_ref)
        comb[...] = jnp.zeros_like(comb)
        rows[...] = jnp.zeros_like(rows)
        for r in range(n_dp):
            at = (r ^ dev) * R if False else None
        turned = n2[...].T
        for d in range(n_dp):
            r = d ^ dev
            n2t_ref[lax.rem(r, 2), lax.div(r, 2), :, :] = turned[d * R:(d + 1) * R, :]

    mine = own * experts_here + e
    g = column(gates_ref[...], mine)
    gate_pre = dot_nn(n2[...], gate_ref[0])
    up_pre = dot_nn(n2[...], up_ref[0])
    sig = 1.0 / (1.0 + jnp.exp(-gate_pre))
    silu = gate_pre * sig
    hidden = (silu * up_pre).astype(BF)
    turned = hidden.T
    for d in range(n_dp):
        r = d ^ dev
        hid_ref[0, lax.rem(r, 2), lax.div(r, 2), :, :] = turned[d * D:(d + 1) * D, :]
    back = jnp.zeros((blocks * T, 1), F32)
    hid_back = jnp.zeros((blocks * T, H), F32)
    for j in range(W // C):
        cols = slice(j * C, (j + 1) * C)
        made = dot_nn(hidden, down_ref[0, :, cols]).astype(BF).astype(F32)
        cj = cot[:, cols].astype(F32)
        back = back + jnp.sum(cj * made, axis=1, keepdims=True)
        comb[:, cols] += g * made
        hid_back = hid_back + dot_nt((g * cj).astype(BF), down_ref[0, :, cols])
    lane = lax.broadcasted_iota(jnp.int32, aux_ref.shape, 1)
    aux_ref[...] = jnp.where(lane == mine, back, aux_ref[...])
    grow = (hid_back * up_pre * sig * (1.0 + gate_pre * (1.0 - sig))).astype(BF)
    urow = (hid_back * silu).astype(BF)
    grow_ref[0] = grow
    urow_ref[0] = urow
    for j in range(W // C):
        cols = slice(j * C, (j + 1) * C)
        rows[:, cols] += dot_nt(grow, gate_ref[0, cols, :]) + dot_nt(urow, up_ref[0, cols, :])

    @pl.when(e == experts_here - 1)
    def _():
        comb_ref[...] = comb[...].astype(BF)
        rows_ref[...] = rows[...].astype(BF)

def expert_rows(where, n2s, cots, routes, router, gate_w, up_w, down_w, n_dp):
    blocks = len(n2s); T, W = n2s[0].shape; E, _, H = gate_w.shape
    R, D = W // n_dp, H // n_dp; A = blocks * T
    once = lambda s: pl.BlockSpec(s, lambda e, w: (0,) * len(s), pipeline_mode=pl.Buffered(1))
    out1 = lambda s: pl.BlockSpec(s, lambda e, w: (0,) * len(s))
    per = lambda s: pl.BlockSpec((1,) + s, lambda e, w: (e,) + (0,) * len(s))
    S = jax.ShapeDtypeStruct
    return pl.pallas_call(
        functools.partial(expert_kernel, blocks),
        out_shape=(S((A, W), BF), S((A, W), BF), S((A, 128), F32), S((A, 128), F32),
                   S((2, n_dp // 2, R, A), BF), S((E, 2, n_dp // 2, D, A), BF),
                   S((E, A, H), BF), S((E, A, H), BF)),
        grid_spec=pltpu.PrefetchScalarGridSpec(
            num_scalar_prefetch=1, grid=(E,),
            in_specs=[once((T, W))] * (2 * blocks) + [once((T, routes[0].shape[1]))] * blocks
            + [once((W, 128)), per((W, H)), per((W, H)), per((H, W))],
            out_specs=[out1((A, W)), out1((A, W)), out1((A, 128)), out1((A, 128)),
                       out1((2, n_dp // 2, R, A)), per((2, n_dp // 2, D, A)), per((A, H)), per((A, H))],
            scratch_shapes=[pltpu.VMEM((A, W), BF), pltpu.VMEM((A, W), BF),
                            pltpu.VMEM((A, W), F32), pltpu.VMEM((A, W), F32)]),
        compiler_params=pltpu.CompilerParams(vmem_limit_bytes=60 << 20),
        cost_estimate=pl.CostEstimate(flops=12 * A * W * H * E, bytes_accessed=6 * E * W * H + 12 * A * W, transcendentals=A * H * E),
    )(where, *n2s, *cots, *routes, router, gate_w, up_w, down_w)

def grad_kernel(blocks, first, where_ref, *refs):
    cot_refs, refs = refs[:blocks], refs[blocks:]
    gates_ref, n2t_ref, hid_ref, grow_ref, urow_ref, keep_ref, send_ref = refs
    T = cot_refs[0].shape[0]
    e = pl.program_id(0) + first
    experts_here = where_ref[2]
    half, R = n2t_ref.shape[1], n2t_ref.shape[2]; D = hid_ref.shape[3]; A = n2t_ref.shape[3]
    W = cot_refs[0].shape[1]; C = grow_ref.shape[2]
    g = column(gates_ref[...], where_ref[0] * experts_here + e)
    grow, urow = grow_ref[0], urow_ref[0]
    for s, out in ((1, send_ref), (0, keep_ref)):
        left = n2t_ref[s].reshape(half * R, A)
        out[0, :, 0:R, :] = dot_nn(left, grow).astype(BF).reshape(half, R, C)
        out[0, :, R:2 * R, :] = dot_nn(left, urow).astype(BF).reshape(half, R, C)
    for j in range(W // C):
        cols = slice(j * C, (j + 1) * C)
        rb = jnp.concatenate([(g[b * T:(b + 1) * T] * cot_refs[b][:, cols].astype(F32)).astype(BF) for b in range(blocks)], axis=0)
        for s, out in ((1, send_ref), (0, keep_ref)):
            left = hid_ref[0, s].reshape(half * D, A)
            out[0, :, 2 * R + j * D:2 * R + (j + 1) * D, :] = dot_nn(left, rb).astype(BF).reshape(half, D, C)

def expert_grads(first, count, where, cots, gates, n2t, hid, grow, urow):
    blocks = len(cots); T, W = cots[0].shape; E, A, H = grow.shape
    half, R = n2t.shape[1:3]; D = hid.shape[3]
    once = lambda s: pl.BlockSpec(s, lambda e, w: (0,) * len(s), pipeline_mode=pl.Buffered(1))
    per = lambda s: pl.BlockSpec((1,) + s, lambda e, w: (e + first,) + (0,) * len(s))
    S = jax.ShapeDtypeStruct
    P_ = 2 * R + (W // H) * D
    o = pl.BlockSpec((1, half, P_, H), lambda e, w: (e, 0, 0, 0))
    return pl.pallas_call(
        functools.partial(grad_kernel, blocks, first),
        out_shape=(S((count, half, P_, H), BF),) * 2,
        grid_spec=pltpu.PrefetchScalarGridSpec(
            num_scalar_prefetch=1, grid=(count,),
            in_specs=[once((T, W))] * blocks + [once((A, 128)), once((2, half, R, A)), per((2, half, D, A)), per((A, H)), per((A, H))],
            out_specs=[o, o]),
        compiler_params=pltpu.CompilerParams(vmem_limit_bytes=60 << 20),
        cost_estimate=pl.CostEstimate(flops=6 * A * W * H * count, bytes_accessed=6 * count * W * H + 6 * A * W, transcendentals=0),
    )(where, *cots, gates, n2t, hid, grow, urow)


from jax.sharding import PartitionSpec as P

HEAD_SIZE = 64
EPSILON = 1e-06
ROTARY_BASE = 10000.0
SCORE_FACTOR = 0.015625
HIGHEST = lax.Precision.HIGHEST
GROUPS = ((0, 2), (2, 2), (4, 1))


def attn_grad_kernel(blocks, dev_ref, *refs):
    n1_refs, refs = refs[:blocks], refs[blocks:]
    mix_refs, refs = refs[:blocks], refs[blocks:]
    qkv_refs, refs = refs[:blocks], refs[blocks:]
    att_refs, refs = refs[:blocks], refs[blocks:]
    keep_ref, send_ref, left = refs
    dev = dev_ref[0]
    T, W = n1_refs[0].shape
    half, R, C = keep_ref.shape
    n_dp = 2 * half
    at = 0
    for lefts, rights in ((n1_refs, qkv_refs), (mix_refs, att_refs)):
        width = rights[0].shape[1]
        for b in range(blocks):
            turned = lefts[b][...].T
            for d in range(n_dp):
                r = d ^ dev
                left[lax.rem(r, 2), lax.div(r, 2), :, b * T:(b + 1) * T] = turned[d * R:(d + 1) * R, :]
        right = jnp.concatenate([ref[...] for ref in rights], axis=0)
        for s, out in ((1, send_ref), (0, keep_ref)):
            out[:, :, at:at + width] = dot_nn(left[s].reshape(half * R, blocks * T), right).astype(BF).reshape(half, R, width)
        at += width


def attn_grads(dev, n1s, mixs, qkvs, atts, n_dp):
    blocks = len(n1s); T, W = n1s[0].shape
    C = qkvs[0].shape[1] + atts[0].shape[1]
    R = W // n_dp
    S = jax.ShapeDtypeStruct
    v = pl.BlockSpec(memory_space=pltpu.VMEM)
    return pl.pallas_call(
        functools.partial(attn_grad_kernel, blocks),
        out_shape=(S((n_dp // 2, R, C), BF),) * 2,
        in_specs=[pl.BlockSpec(memory_space=pltpu.SMEM)] + [v] * (4 * blocks),
        out_specs=(v, v),
        scratch_shapes=[pltpu.VMEM((2, n_dp // 2, R, blocks * T), BF)],
        compiler_params=pltpu.CompilerParams(vmem_limit_bytes=60 << 20),
        cost_estimate=pl.CostEstimate(flops=2 * blocks * T * W * C, bytes_accessed=4 * W * C, transcendentals=0),
    )(dev, *n1s, *mixs, *qkvs, *atts)


def rope_tables(positions, width):
    half = width // 2
    freq = ROTARY_BASE ** (-jnp.arange(half, dtype=F32) * 2.0 / width)
    angle = positions.astype(F32)[:, None] * freq[None, :]
    return (jnp.cos(angle)[:, None, :], jnp.sin(angle)[:, None, :])


def rotate(field, cosine, sine):
    half = field.shape[-1] // 2
    first, second = (field[..., :half], field[..., half:])
    return jnp.concatenate([first * cosine - second * sine, second * cosine + first * sine], axis=-1)


def rotate_back(grad, cosine, sine):
    half = grad.shape[-1] // 2
    first, second = (grad[..., :half], grad[..., half:])
    return jnp.concatenate([first * cosine + second * sine, second * cosine - first * sine], axis=-1)


def positions_of(segments):
    count = segments.shape[0]
    earlier = jnp.sum((segments[None, :] < segments[:, None]).astype(jnp.int32), axis=1)
    return jnp.arange(count, dtype=jnp.int32) - earlier


def attention_mask(segments):
    index = jnp.arange(segments.shape[0], dtype=jnp.int32)
    return (segments[:, None] == segments[None, :]) & (index[None, :] <= index[:, None])


def rms_forward(field, gain):
    inverse = lax.rsqrt(jnp.mean(field * field, axis=-1, keepdims=True) + EPSILON)
    return (inverse, field * inverse * gain)


def rms_backward(field, inverse, gain, grad):
    scaled = grad * gain
    inner = jnp.mean(scaled * field, axis=-1, keepdims=True)
    return (inverse * scaled - field * inverse**3 * inner, jnp.sum(grad * field * inverse, axis=0))


def score_block(query_rows, key_rows, mask):
    score_matrix = jnp.einsum("qean,wen->eaqw", query_rows, key_rows, preferred_element_type=F32) * SCORE_FACTOR
    return jnp.where(mask[None, None], score_matrix, -1e30)


def flip(x, axis, mask, size):
    return lax.ppermute(x, axis, [(i, i ^ mask) for i in range(size)])


def add(a, b):
    return (a.astype(F32) + b.astype(F32)).astype(BF)


def scatter_dp(keep, send, n_dp):
    bits = n_dp.bit_length() - 1
    whole = add(keep, flip(send, "dp", 1, n_dp))
    group, _, rows, cols = whole.shape
    parts = []
    for lo, hi, order in ((0, rows // 2, range(1, bits)), (rows // 2, rows, range(bits - 1, 0, -1))):
        part = whole.reshape((group,) + (2,) * (bits - 1) + (rows, cols))[..., lo:hi, :]
        left = list(range(bits - 1, 0, -1))
        for bit in order:
            axis = 1 + left.index(bit)
            mine = lax.index_in_dim(part, 0, axis, keepdims=False)
            theirs = flip(lax.index_in_dim(part, 1, axis, keepdims=False), "dp", 1 << bit, n_dp)
            left.remove(bit)
            part = add(mine, theirs) if left else mine.astype(F32) + theirs.astype(F32)
        parts.append(part)
    return jnp.concatenate(parts, axis=1)


def reorder(stack, index, size):
    bit = 1
    shape = stack.shape
    while bit < size:
        split = stack.reshape((size // (2 * bit), 2, bit) + shape[1:])
        stack = jnp.where((index & bit) != 0, split[:, ::-1], split).reshape(shape)
        bit *= 2
    return stack


def butterfly(x, n_dp, ne):
    for axis, size in (("dp", n_dp), ("expert", ne)):
        bit = 1
        while bit < size:
            x = x + flip(x, axis, bit, size)
            bit *= 2
    return x


def local(n_dp, ne, tokens, segment_ids, routes, cotangent, query_weight, key_weight, value_matrix, out_weight,
          first_gain, second_gain, router_weight, gate_weight, up_weight, down_weight):
    d = lax.axis_index("dp")
    z = lax.axis_index("expert")
    zx = lambda x, k: x if k == 0 else flip(x, "expert", k, ne)
    ks = range(ne)
    T, W = tokens.shape
    experts = router_weight.shape[1]
    E, _, H = gate_weight.shape
    R = W // n_dp
    D = H // n_dp
    KV = key_weight.shape[1]
    where = jnp.stack([z, d, jnp.int32(E), jnp.int32(0)]).astype(jnp.int32)

    small = jnp.concatenate([first_gain[None], second_gain[None], router_weight.T], axis=0)
    small = lax.all_gather(small, "dp", axis=0, tiled=False).transpose(1, 0, 2).reshape(2 + experts, W)
    gain_one = small[0].astype(F32)
    gain_two = small[1].astype(F32)
    router_t = small[2:]
    router_pad = jnp.pad(router_t.T, ((0, 0), (0, 128 - experts)))
    qkv_full = lax.all_gather(jnp.concatenate([query_weight, key_weight, value_matrix], axis=1), "dp", axis=0, tiled=True)
    out_full = lax.all_gather(out_weight, "dp", axis=0, tiled=True)
    cots = [zx(cotangent, k) for k in ks]
    picks = [zx(routes, k) for k in ks]

    key_heads = KV // HEAD_SIZE
    query_heads = query_weight.shape[1] // HEAD_SIZE
    head_group = query_heads // key_heads
    segments = segment_ids[0]
    mask = attention_mask(segments)
    cosine, sine = rope_tables(positions_of(segments), HEAD_SIZE)
    inputs = tokens.astype(F32)
    first_inverse, normed1 = rms_forward(inputs, gain_one)
    normed1 = normed1.astype(BF)
    qkv = jnp.dot(normed1, qkv_full, preferred_element_type=F32)
    query_rows = rotate(qkv[:, :W].reshape(T, query_heads, HEAD_SIZE), cosine, sine)
    query_rows = query_rows.astype(BF).reshape(T, key_heads, head_group, HEAD_SIZE)
    key_rows = rotate(qkv[:, W:W + KV].reshape(T, key_heads, HEAD_SIZE), cosine, sine).astype(BF)
    value_rows = qkv[:, W + KV:].astype(BF).reshape(T, key_heads, HEAD_SIZE)
    score_matrix = score_block(query_rows, key_rows, mask)
    peak = jnp.max(score_matrix, axis=-1, keepdims=True)
    logsum = peak + jnp.log(jnp.sum(jnp.exp(score_matrix - peak), axis=-1, keepdims=True))
    probabilities = jnp.exp(score_matrix - logsum).astype(BF)
    mixed = jnp.einsum("wmik,kwy->iwmy", probabilities, value_rows, preferred_element_type=F32)
    mixed = mixed.astype(BF).reshape(T, W)
    resid = inputs + jnp.dot(mixed, out_full, preferred_element_type=F32)
    second_inverse, normed2 = rms_forward(resid, gain_two)
    normed2 = normed2.astype(BF)

    n2s = [zx(normed2, k) for k in ks]
    comb, rows, aux, gates, n2t, hid, grow, urow = expert_rows(
        where, n2s, cots, picks, router_pad, gate_weight, up_weight, down_weight, n_dp)
    cut = lambda x, k: x[k * T:(k + 1) * T]
    back = sum(zx(cut(aux, k), k) for k in ks)
    rows_in = [zx(cut(rows, k), k) for k in ks]
    pieces = []
    for first, count in GROUPS:
        keep, send = expert_grads(first, count, where, cots, gates, n2t, hid, grow, urow)
        pieces.append(scatter_dp(keep, send, n_dp))
    comb_in = [zx(cut(comb, k), k) for k in ks]

    gates_own = gates[:T]
    logit_back = gates_own * (back - jnp.sum(gates_own * back, axis=1, keepdims=True))
    logit_back = logit_back[:, :experts]
    grad_out = cotangent.astype(F32)
    router_part = lax.dot_general(logit_back, normed2.astype(F32), (((0,), (0,)), ((), ())), precision=HIGHEST)
    normed2_back = jnp.dot(logit_back, router_t.astype(F32), precision=HIGHEST)
    normed2_back = normed2_back + sum(r.astype(F32) for r in rows_in)
    resid_part, second_part = rms_backward(resid, second_inverse, gain_two, normed2_back)
    resid_back = grad_out + resid_part
    attended_back = resid_back.astype(BF)
    layer_out = (resid + sum(c.astype(F32) for c in comb_in)).astype(BF)
    mixed_back = lax.dot_general(attended_back, out_full, (((1,), (1,)), ((), ())), preferred_element_type=F32).astype(BF)
    mixed_back = mixed_back.reshape(T, key_heads, head_group, HEAD_SIZE)
    second_pass = jnp.exp(score_matrix - logsum)
    value_back = jnp.einsum("kjal,akjx->lkx", second_pass.astype(BF), mixed_back, preferred_element_type=F32)
    prob_back = jnp.einsum("qean,wen->eaqw", mixed_back, value_rows, preferred_element_type=F32)
    delta = jnp.sum(second_pass * prob_back, axis=-1, keepdims=True)
    score_back = (second_pass * (prob_back - delta) * SCORE_FACTOR).astype(BF)
    query_back = jnp.einsum("wmik,kwy->iwmy", score_back, key_rows, preferred_element_type=F32).reshape(T, query_heads, HEAD_SIZE)
    key_back = jnp.einsum("kjal,akjx->lkx", score_back, query_rows, preferred_element_type=F32)
    query_back = rotate_back(query_back, cosine, sine).astype(BF).reshape(T, W)
    key_back = rotate_back(key_back, cosine, sine).astype(BF).reshape(T, KV)
    value_back = value_back.astype(BF).reshape(T, KV)

    def columns(x, k):
        width = x.shape[1] // ne
        return lax.dynamic_slice_in_dim(x, (z ^ k) * width, width, axis=1)

    n1s = [zx(normed1, k) for k in ks]
    mixs = [zx(mixed, k) for k in ks]
    atts = [zx(columns(attended_back, k), k) for k in ks]
    qkvs = [zx(jnp.concatenate([columns(query_back, k), columns(key_back, k), columns(value_back, k)], axis=1), k) for k in ks]
    keep, send = attn_grads(d.reshape(1).astype(jnp.int32), n1s, mixs, qkvs, atts, n_dp)
    part = scatter_dp(keep[None], send[None], n_dp)[0].astype(BF)
    full = reorder(jnp.stack([zx(part, k) for k in ks]), z, ne).astype(F32)
    edges = [0, W // ne, (W + KV) // ne, (W + 2 * KV) // ne, (2 * W + 2 * KV) // ne]
    query_grad, key_grad, value_grad, out_grad = [
        full[:, :, a:b].transpose(1, 0, 2).reshape(R, -1) for a, b in zip(edges[:-1], edges[1:])]

    back_qkv = jnp.concatenate([query_back, key_back, value_back], axis=1)
    normed1_back = lax.dot_general(back_qkv, qkv_full, (((1,), (1,)), ((), ())), preferred_element_type=F32)
    input_part, first_part = rms_backward(inputs, first_inverse, gain_one, normed1_back)
    input_grad = resid_back + input_part
    early = butterfly(jnp.concatenate([second_part[None], router_part], axis=0), n_dp, ne)
    late = butterfly(first_part[None], n_dp, ne)
    own = lambda x: lax.dynamic_slice_in_dim(x, d * R, R, axis=1)
    early, late = own(early), own(late)
    packed = jnp.concatenate(pieces, axis=0)
    gate_grad, up_grad = packed[:, :R], packed[:, R:2 * R]
    down_grad = packed[:, 2 * R:].reshape(E, W // H, D, H).transpose(0, 2, 1, 3).reshape(E, D, W)
    return (layer_out, input_grad, query_grad, key_grad, value_grad, out_grad, late[0], early[0], early[1:].T,
            gate_grad, up_grad, down_grad)


def solution(mesh):
    both = P(("dp", "expert"), None)
    dp = P("dp", None)
    own = P("expert", None, None)
    part = P("expert", "dp", None)
    return jax.shard_map(
        functools.partial(local, mesh.shape["dp"], mesh.shape["expert"]),
        mesh=mesh,
        in_specs=(both, both, both, both, dp, dp, dp, dp, P("dp"), P("dp"), dp, own, own, own),
        out_specs=(both, both, dp, dp, dp, dp, P("dp"), P("dp"), dp, part, part, part),
        check_vma=False,
    )
```

time: 1810 us -> 619 us (0.34)
  waiting for transfers between devices: 1130 us -> 310 us
  blocking collectives: 336 us -> 9.52 us
  matrix products: 165 us -> 31.2 us
  starting transfers between devices: 13.1 us -> 114 us
  local copies, waits for them, and re-layouts: 111 us -> 30.3 us
  Pallas kernels: 0 us -> 74 us
    reduce_scatter x7 -> x0, waiting for transfers between devices: 474 us -> none  [the longest x1 113 us: local(): lax.psum_scatter(up_part, 'dp', scatter_dimension=1, tiled=True)]
    all_to_all x2 -> x0, waiting for transfers between devices: 393 us -> none  [the longest x1 199 us: local(): lax.all_to_all(rows_back, 'expert', split_axis=1, concat_axis=0, tiled=True)]
    all_to_all x2 -> x0, blocking collectives: 268 us -> none  [the longest x1 135 us: local(): lax.all_to_all(outgoing, 'expert', split_axis=0, concat_axis=1, tiled=True)]
    ppermute x0 -> x63, waiting for transfers between devices: none -> 242 us  [flip(): return lax.ppermute(x, axis, [(i, i ^ mask) for i in range(size)])]
    dot_general x29 -> x10, matrix products: 162 us -> 30.4 us  [the longest x1 6.11 us: local(): lax.dot_general(back_qkv, qkv_full, (((1,), (1,)), ((), ())), preferred_e...]
    psum x1 -> x0, waiting for transfers between devices: 125 us -> none  [local(): lax.psum((partial_sums[0], partial_sums[1], partial_sums[2], partial_sums...]
    ppermute x0 -> x63, starting transfers between devices: none -> 114 us  [flip(): return lax.ppermute(x, axis, [(i, i ^ mask) for i in range(size)])]
    pallas_call x0 -> x5, Pallas kernels: none -> 74 us  [the longest x1 38.4 us: expert_rows(): pl.pallas_call(functools.partial(expert_kernel, blocks), out_shape=(S((A,...]
  transfers between devices with their start and end apart: 15 -> 65, of which waited for: 14 -> 23; matrix products, arithmetic and copies ran while one was open for 6% -> 13% of each run, Pallas kernels for 0% -> 12%
where the time goes in v1:
time: 619 us; the launch traced here: 614 us
  waiting for transfers between devices  310 us (50%)
  starting transfers between devices  114 us (18%)
  Pallas kernels  74 us (12%)
  matrix products  31.2 us (5%)
  local copies, waits for them, and re-layouts  30.3 us (5%)
  other arithmetic  29.1 us (5%)
  between operations  15.6 us (3%)
  blocking collectives  9.52 us (2%)
    ppermute x63, waiting for transfers between devices, flip(): return lax.ppermute(x, axis, [(i, i ^ mask) for i in range(size)])  242 us
    ppermute x63, starting transfers between devices, flip(): return lax.ppermute(x, axis, [(i, i ^ mask) for i in range(size)])  114 us
    pallas_call x1, Pallas kernels, expert_rows(): pl.pallas_call(functools.partial(expert_kernel, blocks), out_shape=(S((A,...  38.4 us
    all_gather x1, waiting for transfers between devices, local(): out_full = lax.all_gather(out_weight, 'dp', axis=0, tiled=True)  34.1 us
    all_gather x1, waiting for transfers between devices, local(): lax.all_gather(jnp.concatenate([query_weight, key_weight, value_matrix],...  32.7 us
    pallas_call x3, Pallas kernels, expert_grads(): pl.pallas_call(functools.partial(grad_kernel, blocks, first), out_shape=(...  29.4 us
  transfers between devices with their start and end apart: 65, of which 23 were waited for; matrix products, arithmetic and copies ran while one was open for 13% of the time, Pallas kernels for 12%

profile of v1, /device:TPU:0, one launch (start us, length us, event | category | flops | bytes accessed | tf_op | source)
XLA Modules:
  0.0 613.5 jit_solution(8417331962788405751)
XLA Ops:
  17.3 3.9 collective-permute-start.8
  21.2 9.5 %all-gather.1 = bf16[8,22,192]{2,1,0:T(8,128)(2,1)S(1)} all-gather(bf16[1,22,192]{2,1,0:T(8,128)(2,1)S(1)} %maximum_bitcast_fusion.3), channel_id=2, replica_groups=mesh['dp'=8,'expert'=4] {'dp'}, dimensions={0}, use_global_device_ids=true | all-gather | bytes 76032 | tf_op jit(solution)/shard_map/all_gather | solution.py:310
  32.9 32.7 %all-gather.5.cloned.1.call-done = bf16[1536,2560]{1,0:T(8,128)(2,1)} async-done(((bf16[192,2560]{1,0:T(8,128)(2,1)}), bf16[1536,2560]{1,0:T(8,128)(2,1)}) %all-gather.5.cloned.1.call-update) | async-done | bytes 7864336 | tf_op jit(solution)/shard_map/all_gather | solution.py:315
  65.6 4.6 fusion.69
  72.3 34.1 %all-gather.7.cloned.1.call-done = bf16[1536,1536]{1,0:T(8,128)(2,1)} async-done(((bf16[192,1536]{1,0:T(8,128)(2,1)}), bf16[1536,1536]{1,0:T(8,128)(2,1)}) %all-gather.7.cloned.1.call-update) | async-done | bytes 4718608 | tf_op jit(solution)/shard_map/all_gather | solution.py:316
  125.2 8.9 %collective-permute-start.19 = (bf16[128,1536]{1,0:T(8,128)(2,1)}, bf16[128,1536]{1,0:T(8,128)(2,1)}, u32[]{:S(2)}, u32[]{:S(2)}) collective-permute-start(bf16[128,1536]{1,0:T(8,128)(2,1)} %fusion.20.refs_0_), channel_id=1, source_target_pairs={{0,2},{1,3},{2,0},{3,1},{4,6},{5,7},{6,4},{7,5},{8,10},{9,11},{10,... | collective-permute-start | bytes 1179656 | tf_op jit(solution)/shard_map/ppermute | solution.py:251
  134.2 24.2 %collective-permute-done.1.refs_2_ = bf16[128,1536]{1,0:T(8,128)(2,1)} collective-permute-done((bf16[128,1536]{1,0:T(8,128)(2,1)}, bf16[128,1536]{1,0:T(8,128)(2,1)}, u32[]{:S(2)}, u32[]{:S(2)}) %collective-permute-start.1) | collective-permute-done | bytes 393248 | tf_op jit(solution)/shard_map/ppermute | solution.py:251
  158.4 38.4 %shard_map.229 = (bf16[512,1536]{1,0:T(8,128)(2,1)}, bf16[512,1536]{1,0:T(8,128)(2,1)}, f32[512,128]{1,0:T(8,128)}, f32[512,128]{1,0:T(8,128)}, bf16[2,4,192,512...) custom-call(s32[4]{0:T(128)} %pad_add_fusion.where_ref, ...), custom_call_target="tpu_custom_call" | custom-call | flops 24159191040 | bytes 33030144 | tf_op jit(solution)/shard_map/pallas_call | solution.py:95
  201.9 16.5 %collective-permute-start.13 = (f32[128,128]{1,0:T(8,128)}, f32[128,128]{1,0:T(8,128)S(1)}, u32[]{:S(2)}, u32[]{:S(2)}) collective-permute-start(f32[128,128]{1,0:T(8,128)} %get-tuple-element.99), channel_id=1, source_target_pairs={{0,2},{1,3},{2,0},{3,1},{4,6},{5,7},{6,4},{7,5},{8,10},{9,11},{10,... | collective-permute-start | bytes 196616 | tf_op jit(solution)/shard_map/ppermute | solution.py:251
  219.4 11.1 %shard_map.232 = (bf16[2,4,576,512]{3,2,1,0:T(8,128)(2,1)}, bf16[2,4,576,512]{3,2,1,0:T(8,128)(2,1)}) custom-call(s32[4]{0:T(128)} %pad_add_fusion.where_ref, bf16[128,1536]{1,0:T(8,128)(2,1)} %refs_0_.5, bf16[128,1536]{1,0:T(8,128)(2,1)} %collective-permute-done.3.refs_5_.refs_1_, bf16[128,1536]{1,0:T(8,128)(2,1)} %collective-permute-done.4.refs_6_.refs_2_, ...), custom_call_target="tpu_custom_call" | custom-call | flops 4831838208 | bytes 14155776 | tf_op jit(solution)/shard_map/pallas_call | solution.py:141
  230.5 7.7 %shard_map.233 = (bf16[1,4,576,512]{3,2,1,0:T(8,128)(2,1)}, bf16[1,4,576,512]{3,2,1,0:T(8,128)(2,1)}) custom-call(s32[4]{0:T(128)} %pad_add_fusion.where_ref, bf16[128,1536]{1,0:T(8,128)(2,1)} %refs_0_.5, bf16[128,1536]{1,0:T(8,128)(2,1)} %collective-permute-done.3.refs_5_.refs_1_, bf16[128,1536]{1,0:T(8,128)(2,1)} %collective-permute-done.4.refs_6_.refs_2_, ...), custom_call_target="tpu_custom_call" | custom-call | flops 2415919104 | bytes 9437184 | tf_op jit(solution)/shard_map/pallas_call | solution.py:141
  246.3 6.1 collective-permute-done.17
  254.7 28.6 %collective-permute-done.16 = bf16[128,1536]{1,0:T(8,128)(2,1)S(1)} collective-permute-done((bf16[128,1536]{1,0:T(8,128)(2,1)}, bf16[128,1536]{1,0:T(8,128)(2,1)S(1)}, u32[]{:S(2)}, u32[]{:S(2)}) %collective-permute-start.16) | collective-permute-done | bytes 393248 | tf_op jit(solution)/shard_map/ppermute | solution.py:251
  290.2 26.8 %collective-permute-done.10 = bf16[128,1536]{1,0:T(8,128)(2,1)S(1)} collective-permute-done((bf16[128,1536]{1,0:T(8,128)(2,1)}, bf16[128,1536]{1,0:T(8,128)(2,1)S(1)}, u32[]{:S(2)}, u32[]{:S(2)}) %collective-permute-start.10) | collective-permute-done | bytes 393248 | tf_op jit(solution)/shard_map/ppermute | solution.py:251
  319.6 4.0 convolution_convert_fusion
  334.6 6.1 fusion.26
  352.6 19.8 %collective-permute-done.22.refs_6_ = bf16[128,1536]{1,0:T(8,128)(2,1)} collective-permute-done((bf16[128,1536]{1,0:T(8,128)(2,1)}, bf16[128,1536]{1,0:T(8,128)(2,1)}, u32[]{:S(2)}, u32[]{:S(2)}) %collective-permute-start.22) | collective-permute-done | bytes 393248 | tf_op jit(solution)/shard_map/ppermute | solution.py:251
  374.6 15.2 %collective-permute-start.28 = (bf16[128,384]{1,0:T(8,128)(2,1)S(1)}, bf16[128,384]{1,0:T(8,128)(2,1)S(1)}, u32[]{:S(2)}, u32[]{:S(2)}) collective-permute-start(bf16[128,384]{1,0:T(8,128)(2,1)S(1)} %get-tuple-element.85), channel_id=1, source_target_pairs={{0,2},{1,3},{2,0},{3,1},{4,6},{5,7},{6,4},{7,5},{8,10},{9,11},{10,... | collective-permute-start | bytes 294920 | tf_op jit(solution)/shard_map/ppermute | solution.py:251
  392.1 9.1 %collective-permute-done.28.refs_14_ = bf16[128,384]{1,0:T(8,128)(2,1)S(1)} collective-permute-done((bf16[128,384]{1,0:T(8,128)(2,1)S(1)}, bf16[128,384]{1,0:T(8,128)(2,1)S(1)}, u32[]{:S(2)}, u32[]{:S(2)}) %collective-permute-start.28) | collective-permute-done | bytes 98336 | tf_op jit(solution)/shard_map/ppermute | solution.py:251
  404.5 6.2 %shard_map.230 = (bf16[4,192,1024]{2,1,0:T(8,128)(2,1)}, bf16[4,192,1024]{2,1,0:T(8,128)(2,1)}) custom-call(s32[1]{0:T(128)} %bitcast.17.dev_ref, bf16[128,1536]{1,0:T(8,128)(2,1)} %fusion.20.refs_0_, bf16[128,1536]{1,0:T(8,128)(2,1)} %collective-permute-done.18.refs_1_, bf16[128,1536]{1,0:T(8,128)(2,1)} %collective-permute-done.19.refs_2_, ...), custom_call_target="tpu_custom_call" | custom-call | flops 1610612736 | bytes 6291456 | tf_op jit(solution)/shard_map/pallas_call | solution.py:193
  412.3 10.6 %shard_map.231 = (bf16[2,4,576,512]{3,2,1,0:T(8,128)(2,1)}, bf16[2,4,576,512]{3,2,1,0:T(8,128)(2,1)}) custom-call(s32[4]{0:T(128)} %pad_add_fusion.where_ref, bf16[128,1536]{1,0:T(8,128)(2,1)} %refs_0_.5, bf16[128,1536]{1,0:T(8,128)(2,1)} %collective-permute-done.3.refs_5_.refs_1_, bf16[128,1536]{1,0:T(8,128)(2,1)} %collective-permute-done.4.refs_6_.refs_2_, ...), custom_call_target="tpu_custom_call" | custom-call | flops 4831838208 | bytes 14155776 | tf_op jit(solution)/shard_map/pallas_call | solution.py:141
  433.7 5.8 collective-permute-done.47
  446.8 6.8 %collective-permute-done.31 = bf16[1,2,96,1024]{3,2,1,0:T(8,128)(2,1)S(1)} collective-permute-done((bf16[1,2,96,1024]{3,2,1,0:T(8,128)(2,1)S(1)}, bf16[1,2,96,1024]{3,2,1,0:T(8,128)(2,1)S(1)}, u32[]{:S(2)}, u32[]{:S(2)}) %collective-permute-start.31) | collective-permute-done | bytes 393248 | tf_op jit(solution)/shard_map/ppermute | solution.py:251
  455.8 13.5 %collective-permute-done.34 = bf16[1,96,1024]{2,1,0:T(8,128)(2,1)S(1)} collective-permute-done((bf16[1,96,1024]{2,1,0:T(8,128)(2,1)S(1)}, bf16[1,96,1024]{2,1,0:T(8,128)(2,1)S(1)}, u32[]{:S(2)}, u32[]{:S(2)}) %collective-permute-start.34) | collective-permute-done | bytes 196640 | tf_op jit(solution)/shard_map/ppermute | solution.py:251
  470.0 5.2 collective-permute-done.32
  480.2 9.0 %collective-permute-done.37 = bf16[192,1024]{1,0:T(8,128)(2,1)S(1)} collective-permute-done((bf16[192,1024]{1,0:T(8,128)(2,1)S(1)}, bf16[192,1024]{1,0:T(8,128)(2,1)S(1)}, u32[]{:S(2)}, u32[]{:S(2)}) %collective-permute-start.37) | collective-permute-done | bytes 393248 | tf_op jit(solution)/shard_map/ppermute | solution.py:251
  489.9 18.1 %collective-permute-done.36 = bf16[192,1024]{1,0:T(8,128)(2,1)S(1)} collective-permute-done((bf16[192,1024]{1,0:T(8,128)(2,1)S(1)}, bf16[192,1024]{1,0:T(8,128)(2,1)S(1)}, u32[]{:S(2)}, u32[]{:S(2)}) %collective-permute-start.36) | collective-permute-done | bytes 393248 | tf_op jit(solution)/shard_map/ppermute | solution.py:251
  516.3 3.8 add_convert_fusion
  529.0 21.6 %collective-permute-done.56 = bf16[2,2,288,512]{3,2,0,1:T(8,128)(2,1)} collective-permute-done((bf16[2,2,288,512]{3,2,0,1:T(8,128)(2,1)}, bf16[2,2,288,512]{3,2,0,1:T(8,128)(2,1)}, u32[]{:S(2)}, u32[]{:S(2)}) %collective-permute-start.56) | collective-permute-done | bytes 1179680 | tf_op jit(solution)/shard_map/ppermute | solution.py:251
  555.1 20.6 %collective-permute-done.51 = bf16[2,2,288,512]{3,2,0,1:T(8,128)(2,1)S(1)} collective-permute-done((bf16[2,2,288,512]{3,2,0,1:T(8,128)(2,1)S(1)}, bf16[2,2,288,512]{3,2,0,1:T(8,128)(2,1)S(1)}, u32[]{:S(2)}, u32[]{:S(2)}) %collective-permute-start.51) | collective-permute-done | bytes 1179680 | tf_op jit(solution)/shard_map/ppermute | solution.py:251
  579.5 11.6 %collective-permute-done.57 = bf16[2,288,512]{2,1,0:T(8,128)(2,1)S(1)} collective-permute-done((bf16[2,288,512]{2,1,0:T(8,128)(2,1)S(1)}, bf16[2,288,512]{2,1,0:T(8,128)(2,1)S(1)}, u32[]{:S(2)}, u32[]{:S(2)}) %collective-permute-start.57) | collective-permute-done | bytes 589856 | tf_op jit(solution)/shard_map/ppermute | solution.py:251
  591.5 7.5 %collective-permute-done.52 = bf16[2,288,512]{2,1,0:T(8,128)(2,1)S(1)} collective-permute-done((bf16[2,288,512]{2,1,0:T(8,128)(2,1)S(1)}, bf16[2,288,512]{2,1,0:T(8,128)(2,1)S(1)}, u32[]{:S(2)}, u32[]{:S(2)}) %collective-permute-start.52) | collective-permute-done | bytes 589856 | tf_op jit(solution)/shard_map/ppermute | solution.py:251
  (354 shorter events, 150.2 us)
Async XLA Ops:
  7.2 58.4 %all-gather.5.cloned.1.call-start = ((), (), s32[]{:S(2)}) async-start(), calls=%async_computation | async-start | bytes 8847360 | tf_op jit(solution)/shard_map/all_gather | solution.py:315
  9.6 96.8 %all-gather.7.cloned.1.call-start = ((), (), s32[]{:S(2)}) async-start(), calls=%async_computation.1 | async-start | bytes 5308416 | tf_op jit(solution)/shard_map/all_gather | solution.py:316
  10.4 105.1 %collective-permute-start.3 = (bf16[128,1536]{1,0:T(8,128)(2,1)}, bf16[128,1536]{1,0:T(8,128)(2,1)}, u32[]{:S(2)}, u32[]{:S(2)}) collective-permute-start(bf16[128,1536]{1,0:T(8,128)(2,1)} %refs_0_.5), channel_id=1, source_target_pairs={{0,1},{1,0},{2,3},{3,2},{4,5},{5,4},{6,7},{7,6},{8,9},{9,8},{10,11... | collective-permute-start | bytes 1179656 | tf_op jit(solution)/shard_map/ppermute | solution.py:251
  13.5 109.5 %collective-permute-start.4 = (bf16[128,1536]{1,0:T(8,128)(2,1)}, bf16[128,1536]{1,0:T(8,128)(2,1)}, u32[]{:S(2)}, u32[]{:S(2)}) collective-permute-start(bf16[128,1536]{1,0:T(8,128)(2,1)} %refs_0_.5), channel_id=1, source_target_pairs={{0,2},{1,3},{2,0},{3,1},{4,6},{5,7},{6,4},{7,5},{8,10},{9,11},{10,... | collective-permute-start | bytes 1179656 | tf_op jit(solution)/shard_map/ppermute | solution.py:251
  16.8 94.3 %collective-permute-start.6 = (s32[128,8]{1,0:T(8,128)}, s32[128,8]{1,0:T(8,128)}, u32[]{:S(2)}, u32[]{:S(2)}) collective-permute-start(s32[128,8]{1,0:T(8,128)} %copy.113.refs_8_), channel_id=1, source_target_pairs={{0,1},{1,0},{2,3},{3,2},{4,5},{5,4},{6,7},{7,6},{8,9},{9,8},{10,11... | collective-permute-start | bytes 12296 | tf_op jit(solution)/shard_map/ppermute | solution.py:251
  17.3 97.2 %collective-permute-start.7 = (s32[128,8]{1,0:T(8,128)}, s32[128,8]{1,0:T(8,128)}, u32[]{:S(2)}, u32[]{:S(2)}) collective-permute-start(s32[128,8]{1,0:T(8,128)} %copy.113.refs_8_), channel_id=1, source_target_pairs={{0,2},{1,3},{2,0},{3,1},{4,6},{5,7},{6,4},{7,5},{8,10},{9,11},{10,... | collective-permute-start | bytes 12296 | tf_op jit(solution)/shard_map/ppermute | solution.py:251
  17.3 97.2 %collective-permute-start.8 = (s32[128,8]{1,0:T(8,128)}, s32[128,8]{1,0:T(8,128)}, u32[]{:S(2)}, u32[]{:S(2)}) collective-permute-start(s32[128,8]{1,0:T(8,128)} %copy.113.refs_8_), channel_id=1, source_target_pairs={{0,3},{1,2},{2,1},{3,0},{4,7},{5,6},{6,5},{7,4},{8,11},{9,10},{10,... | collective-permute-start | bytes 12296 | tf_op jit(solution)/shard_map/ppermute | solution.py:251
  114.4 43.9 %collective-permute-start.1 = (bf16[128,1536]{1,0:T(8,128)(2,1)}, bf16[128,1536]{1,0:T(8,128)(2,1)}, u32[]{:S(2)}, u32[]{:S(2)}) collective-permute-start(bf16[128,1536]{1,0:T(8,128)(2,1)} %multiply_convert_fusion.refs_0_), channel_id=1, source_target_pairs={{0,2},{1,3},{2,0},{3,1},{4,6},{5,7},{6,4},{7,5},{8,10},{9,11},{10,... | collective-permute-start | bytes 1179656 | tf_op jit(solution)/shard_map/ppermute | solution.py:251
  115.5 42.9 %collective-permute-start.2 = (bf16[128,1536]{1,0:T(8,128)(2,1)}, bf16[128,1536]{1,0:T(8,128)(2,1)}, u32[]{:S(2)}, u32[]{:S(2)}) collective-permute-start(bf16[128,1536]{1,0:T(8,128)(2,1)} %multiply_convert_fusion.refs_0_), channel_id=1, source_target_pairs={{0,3},{1,2},{2,1},{3,0},{4,7},{5,6},{6,5},{7,4},{8,11},{9,10},{10,... | collective-permute-start | bytes 1179656 | tf_op jit(solution)/shard_map/ppermute | solution.py:251
  123.0 219.2 %collective-permute-start.18 = (bf16[128,1536]{1,0:T(8,128)(2,1)}, bf16[128,1536]{1,0:T(8,128)(2,1)}, u32[]{:S(2)}, u32[]{:S(2)}) collective-permute-start(bf16[128,1536]{1,0:T(8,128)(2,1)} %fusion.20.refs_0_), channel_id=1, source_target_pairs={{0,1},{1,0},{2,3},{3,2},{4,5},{5,4},{6,7},{7,6},{8,9},{9,8},{10,11... | collective-permute-start | bytes 1179656 | tf_op jit(solution)/shard_map/ppermute | solution.py:251
  125.2 221.4 %collective-permute-start.19 = (bf16[128,1536]{1,0:T(8,128)(2,1)}, bf16[128,1536]{1,0:T(8,128)(2,1)}, u32[]{:S(2)}, u32[]{:S(2)}) collective-permute-start(bf16[128,1536]{1,0:T(8,128)(2,1)} %fusion.20.refs_0_), channel_id=1, source_target_pairs={{0,2},{1,3},{2,0},{3,1},{4,6},{5,7},{6,4},{7,5},{8,10},{9,11},{10,... | collective-permute-start | bytes 1179656 | tf_op jit(solution)/shard_map/ppermute | solution.py:251
  199.9 38.3 %collective-permute-start.14 = (f32[128,128]{1,0:T(8,128)}, f32[128,128]{1,0:T(8,128)S(1)}, u32[]{:S(2)}, u32[]{:S(2)}) collective-permute-start(f32[128,128]{1,0:T(8,128)} %get-tuple-element.98), channel_id=1, source_target_pairs={{0,3},{1,2},{2,1},{3,0},{4,7},{5,6},{6,5},{7,4},{8,11},{9,10},{10,... | collective-permute-start | bytes 196616 | tf_op jit(solution)/shard_map/ppermute | solution.py:251
  201.9 38.6 %collective-permute-start.13 = (f32[128,128]{1,0:T(8,128)}, f32[128,128]{1,0:T(8,128)S(1)}, u32[]{:S(2)}, u32[]{:S(2)}) collective-permute-start(f32[128,128]{1,0:T(8,128)} %get-tuple-element.99), channel_id=1, source_target_pairs={{0,2},{1,3},{2,0},{3,1},{4,6},{5,7},{6,4},{7,5},{8,10},{9,11},{10,... | collective-permute-start | bytes 196616 | tf_op jit(solution)/shard_map/ppermute | solution.py:251
  240.6 42.8 %collective-permute-start.16 = (bf16[128,1536]{1,0:T(8,128)(2,1)}, bf16[128,1536]{1,0:T(8,128)(2,1)S(1)}, u32[]{:S(2)}, u32[]{:S(2)}) collective-permute-start(bf16[128,1536]{1,0:T(8,128)(2,1)} %get-tuple-element.75), channel_id=1, source_target_pairs={{0,2},{1,3},{2,0},{3,1},{4,6},{5,7},{6,4},{7,5},{8,10},{9,11},{10,... | collective-permute-start | bytes 1179656 | tf_op jit(solution)/shard_map/ppermute | solution.py:251
  242.3 41.0 %collective-permute-start.15 = (bf16[128,1536]{1,0:T(8,128)(2,1)}, bf16[128,1536]{1,0:T(8,128)(2,1)S(1)}, u32[]{:S(2)}, u32[]{:S(2)}) collective-permute-start(bf16[128,1536]{1,0:T(8,128)(2,1)} %get-tuple-element.73), channel_id=1, source_target_pairs={{0,1},{1,0},{2,3},{3,2},{4,5},{5,4},{6,7},{7,6},{8,9},{9,8},{10,11... | collective-permute-start | bytes 1179656 | tf_op jit(solution)/shard_map/ppermute | solution.py:251
  252.4 36.4 %collective-permute-start.11 = (bf16[128,1536]{1,0:T(8,128)(2,1)}, bf16[128,1536]{1,0:T(8,128)(2,1)S(1)}, u32[]{:S(2)}, u32[]{:S(2)}) collective-permute-start(bf16[128,1536]{1,0:T(8,128)(2,1)} %get-tuple-element.77), channel_id=1, source_target_pairs={{0,3},{1,2},{2,1},{3,0},{4,7},{5,6},{6,5},{7,4},{8,11},{9,10},{10,... | collective-permute-start | bytes 1179656 | tf_op jit(solution)/shard_map/ppermute | solution.py:251
  283.3 33.7 %collective-permute-start.10 = (bf16[128,1536]{1,0:T(8,128)(2,1)}, bf16[128,1536]{1,0:T(8,128)(2,1)S(1)}, u32[]{:S(2)}, u32[]{:S(2)}) collective-permute-start(bf16[128,1536]{1,0:T(8,128)(2,1)} %get-tuple-element.78), channel_id=1, source_target_pairs={{0,2},{1,3},{2,0},{3,1},{4,6},{5,7},{6,4},{7,5},{8,10},{9,11},{10,... | collective-permute-start | bytes 1179656 | tf_op jit(solution)/shard_map/ppermute | solution.py:251
  283.3 33.7 %collective-permute-start.9 = (bf16[128,1536]{1,0:T(8,128)(2,1)S(1)}, bf16[128,1536]{1,0:T(8,128)(2,1)S(1)}, u32[]{:S(2)}, u32[]{:S(2)}) collective-permute-start(bf16[128,1536]{1,0:T(8,128)(2,1)S(1)} %get-tuple-element.76), channel_id=1, source_target_pairs={{0,1},{1,0},{2,3},{3,2},{4,5},{5,4},{6,7},{7,6},{8,9},{9,8},{10,11... | collective-permute-start | bytes 1179656 | tf_op jit(solution)/shard_map/ppermute | solution.py:251
  288.8 57.9 %collective-permute-start.20 = (bf16[128,1536]{1,0:T(8,128)(2,1)}, bf16[128,1536]{1,0:T(8,128)(2,1)}, u32[]{:S(2)}, u32[]{:S(2)}) collective-permute-start(bf16[128,1536]{1,0:T(8,128)(2,1)} %fusion.20.refs_0_), channel_id=1, source_target_pairs={{0,3},{1,2},{2,1},{3,0},{4,7},{5,6},{6,5},{7,4},{8,11},{9,10},{10,... | collective-permute-start | bytes 1179656 | tf_op jit(solution)/shard_map/ppermute | solution.py:251
  317.0 33.4 %collective-permute-start.21 = (bf16[128,1536]{1,0:T(8,128)(2,1)}, bf16[128,1536]{1,0:T(8,128)(2,1)}, u32[]{:S(2)}, u32[]{:S(2)}) collective-permute-start(bf16[128,1536]{1,0:T(8,128)(2,1)} %copy.133.refs_4_), channel_id=1, source_target_pairs={{0,1},{1,0},{2,3},{3,2},{4,5},{5,4},{6,7},{7,6},{8,9},{9,8},{10,11... | collective-permute-start | bytes 1179656 | tf_op jit(solution)/shard_map/ppermute | solution.py:251
  346.6 43.2 %collective-permute-start.43 = (f32[21,1536]{1,0:T(8,128)S(1)}, f32[21,1536]{1,0:T(8,128)S(1)}, u32[]{:S(2)}, u32[]{:S(2)}) collective-permute-start(f32[21,1536]{1,0:T(8,128)S(1)} %pad_maximum_fusion.10), channel_id=1, source_target_pairs={{0,4},{4,0},{8,12},{12,8},{16,20},{20,16},{24,28},{28,24},{1,5},{5... | collective-permute-start | bytes 387080 | tf_op jit(solution)/shard_map/ppermute | solution.py:251
  350.5 51.3 %collective-permute-start.24 = (bf16[128,640]{1,0:T(8,128)(2,1)S(1)}, bf16[128,640]{1,0:T(8,128)(2,1)S(1)}, u32[]{:S(2)}, u32[]{:S(2)}) collective-permute-start(bf16[128,640]{1,0:T(8,128)(2,1)S(1)} %pad_maximum_fusion.7), channel_id=1, source_target_pairs={{0,1},{1,0},{2,3},{3,2},{4,5},{5,4},{6,7},{7,6},{8,9},{9,8},{10,11... | collective-permute-start | bytes 491528 | tf_op jit(solution)/shard_map/ppermute | solution.py:251
  372.4 31.4 %collective-permute-start.26 = (bf16[128,640]{1,0:T(8,128)(2,1)S(1)}, bf16[128,640]{1,0:T(8,128)(2,1)S(1)}, u32[]{:S(2)}, u32[]{:S(2)}) collective-permute-start(bf16[128,640]{1,0:T(8,128)(2,1)S(1)} %pad_maximum_fusion.9), channel_id=1, source_target_pairs={{0,3},{1,2},{2,1},{3,0},{4,7},{5,6},{6,5},{7,4},{8,11},{9,10},{10,... | collective-permute-start | bytes 491528 | tf_op jit(solution)/shard_map/ppermute | solution.py:251
  401.3 42.2 %collective-permute-start.58 = (bf16[1,4,576,512]{3,2,1,0:T(8,128)(2,1)}, bf16[1,4,576,512]{3,2,1,0:T(8,128)(2,1)}, u32[]{:S(2)}, u32[]{:S(2)}) collective-permute-start(bf16[1,4,576,512]{3,2,1,0:T(8,128)(2,1)} %get-tuple-element.43), channel_id=1, source_target_pairs={{0,4},{4,0},{8,12},{12,8},{16,20},{20,16},{24,28},{28,24},{1,5},{5... | collective-permute-start | bytes 7077896 | tf_op jit(solution)/shard_map/ppermute | solution.py:251
  401.3 115.0 %collective-permute-start.53 = (bf16[2,4,576,512]{3,2,1,0:T(8,128)(2,1)}, bf16[2,4,576,512]{3,2,1,0:T(8,128)(2,1)}, u32[]{:S(2)}, u32[]{:S(2)}) collective-permute-start(bf16[2,4,576,512]{3,2,1,0:T(8,128)(2,1)} %get-tuple-element.41), channel_id=1, source_target_pairs={{0,4},{4,0},{8,12},{12,8},{16,20},{20,16},{24,28},{28,24},{1,5},{5... | collective-permute-start | bytes 14155784 | tf_op jit(solution)/shard_map/ppermute | solution.py:251
  433.1 91.9 %collective-permute-start.48 = (bf16[2,4,576,512]{3,2,1,0:T(8,128)(2,1)}, bf16[2,4,576,512]{3,2,1,0:T(8,128)(2,1)S(1)}, u32[]{:S(2)}, u32[]{:S(2)}) collective-permute-start(bf16[2,4,576,512]{3,2,1,0:T(8,128)(2,1)} %get-tuple-element.39), channel_id=1, source_target_pairs={{0,4},{4,0},{8,12},{12,8},{16,20},{20,16},{24,28},{28,24},{1,5},{5... | collective-permute-start | bytes 14155784 | tf_op jit(solution)/shard_map/ppermute | solution.py:251
  445.9 31.4 %collective-permute-start.59 = (bf16[1,2,288,512]{3,2,1,0:T(8,128)(2,1)S(1)}, bf16[1,2,288,512]{3,2,1,0:T(8,128)(2,1)S(1)}, u32[]{:S(2)}, u32[]{:S(2)}) collective-permute-start(bf16[1,2,288,512]{3,2,1,0:T(8,128)(2,1)S(1)} %slice_bitcast_fusion.2), channel_id=1, source_target_pairs={{0,8},{4,12},{8,0},{12,4},{16,24},{20,28},{24,16},{28,20},{1,9},{5... | collective-permute-start | bytes 1769480 | tf_op jit(solution)/shard_map/ppermute | solution.py:251
  477.4 31.1 %collective-permute-start.35 = (bf16[192,1024]{1,0:T(8,128)(2,1)S(1)}, bf16[192,1024]{1,0:T(8,128)(2,1)S(1)}, u32[]{:S(2)}, u32[]{:S(2)}) collective-permute-start(bf16[192,1024]{1,0:T(8,128)(2,1)S(1)} %fusion.68), channel_id=1, source_target_pairs={{0,1},{1,0},{2,3},{3,2},{4,5},{5,4},{6,7},{7,6},{8,9},{9,8},{10,11... | collective-permute-start | bytes 1179656 | tf_op jit(solution)/shard_map/ppermute | solution.py:251
  526.9 48.8 %collective-permute-start.51 = (bf16[2,2,288,512]{3,2,0,1:T(8,128)(2,1)S(1)}, bf16[2,2,288,512]{3,2,0,1:T(8,128)(2,1)S(1)}, u32[]{:S(2)}, u32[]{:S(2)}) collective-permute-start(bf16[2,2,288,512]{3,2,0,1:T(8,128)(2,1)S(1)} %bitcast.288), channel_id=1, source_target_pairs={{0,16},{4,20},{8,24},{12,28},{16,0},{20,4},{24,8},{28,12},{1,17},{... | collective-permute-start | bytes 3538952 | tf_op jit(solution)/shard_map/ppermute | solution.py:251
  528.2 50.4 %collective-permute-start.49 = (bf16[2,2,288,512]{3,2,0,1:T(8,128)(2,1)S(1)}, bf16[2,2,288,512]{3,2,0,1:T(8,128)(2,1)S(1)}, u32[]{:S(2)}, u32[]{:S(2)}) collective-permute-start(bf16[2,2,288,512]{3,2,0,1:T(8,128)(2,1)S(1)} %bitcast.287), channel_id=1, source_target_pairs={{0,8},{4,12},{8,0},{12,4},{16,24},{20,28},{24,16},{28,20},{1,9},{5... | collective-permute-start | bytes 3538952 | tf_op jit(solution)/shard_map/ppermute | solution.py:251
  552.3 38.9 %collective-permute-start.57 = (bf16[2,288,512]{2,1,0:T(8,128)(2,1)S(1)}, bf16[2,288,512]{2,1,0:T(8,128)(2,1)S(1)}, u32[]{:S(2)}, u32[]{:S(2)}) collective-permute-start(bf16[2,288,512]{2,1,0:T(8,128)(2,1)S(1)} %slice_bitcast_fusion.4), channel_id=1, source_target_pairs={{0,8},{4,12},{8,0},{12,4},{16,24},{20,28},{24,16},{28,20},{1,9},{5... | collective-permute-start | bytes 1769480 | tf_op jit(solution)/shard_map/ppermute | solution.py:251
  554.0 37.4 %collective-permute-start.55 = (bf16[2,288,512]{2,1,0:T(8,128)(2,1)S(1)}, bf16[2,288,512]{2,1,0:T(8,128)(2,1)S(1)}, u32[]{:S(2)}, u32[]{:S(2)}) collective-permute-start(bf16[2,288,512]{2,1,0:T(8,128)(2,1)S(1)} %slice_bitcast_fusion.6), channel_id=1, source_target_pairs={{0,16},{4,20},{8,24},{12,28},{16,0},{20,4},{24,8},{28,12},{1,17},{... | collective-permute-start | bytes 1769480 | tf_op jit(solution)/shard_map/ppermute | solution.py:251
  (81 other events, 1244.1 us)
Sparse Core Ops, SparseCore 0:
  10.5 55.0 all-gather.4
  67.5 38.9 all-gather.6

commit v2 on v1

v2 whole, which is shorter than its diff:
```python
import functools
import jax
import jax.numpy as jnp
from jax import lax
from jax.experimental import pallas as pl
from jax.experimental.pallas import tpu as pltpu
from jax.sharding import PartitionSpec as P

HEAD_SIZE = 64
EPSILON = 1e-06
ROTARY_BASE = 10000.0
SCORE_FACTOR = 0.015625
F32=jnp.float32; BF=jnp.bfloat16
def dot_nn(a,b): return lax.dot_general(a,b,(((1,),(0,)),((),())),preferred_element_type=F32)
def dot_nt(a,b): return lax.dot_general(a,b,(((1,),(1,)),((),())),preferred_element_type=F32)

def column(table, lane):
    at = lax.broadcasted_iota(jnp.int32, table.shape, 1) == lane
    return jnp.sum(jnp.where(at, table, 0.0), axis=1, keepdims=True)

def expert_kernel(blocks, choices, where_ref, *refs):
    n2_refs, refs = refs[:blocks], refs[blocks:]
    cot_refs, refs = refs[:blocks], refs[blocks:]
    (router_ref, gate_ref, up_ref, down_ref,
     comb_ref, rows_ref, gates_ref, n2t_ref, hid_ref, grow_ref, urow_ref,
     n2, cot, comb, rows, aux_ref) = refs
    e = pl.program_id(0)
    own = where_ref[0]
    experts_here = pl.num_programs(0)
    T = n2_refs[0].shape[0]; W = n2_refs[0].shape[1]; H = gate_ref.shape[2]
    C = 512

    @pl.when(e == 0)
    def _():
        for b in range(blocks):
            n2[b * T:(b + 1) * T, :] = n2_refs[b][...]
            cot[b * T:(b + 1) * T, :] = cot_refs[b][:, :W]
            picks = cot_refs[b][:, W:].astype(F32)
            logits = dot_nn(n2_refs[b][...], router_ref[...])
            lane = lax.broadcasted_iota(jnp.int32, logits.shape, 1)
            named = lane < 0
            for k in range(choices):
                named = named | (lane.astype(F32) == picks[:, k:k + 1])
            logits = jnp.where(named, logits, -1e30)
            top = jnp.max(logits, axis=1, keepdims=True)
            raised = jnp.where(named, jnp.exp(logits - top), 0.0)
            gates_ref[b * T:(b + 1) * T, :] = raised / jnp.sum(raised, axis=1, keepdims=True)
        aux_ref[...] = jnp.zeros_like(aux_ref)
        comb[...] = jnp.zeros_like(comb)
        rows[...] = jnp.zeros_like(rows)
        n2t_ref[...] = n2[...].T

    mine = own * experts_here + e
    g = column(gates_ref[...], mine)
    gate_pre = dot_nn(n2[...], gate_ref[0])
    up_pre = dot_nn(n2[...], up_ref[0])
    raw_back = dot_nt(cot[...], down_ref[0])
    sig = 1.0 / (1.0 + jnp.exp(-gate_pre))
    silu = gate_pre * sig
    hidden = (silu * up_pre).astype(BF).astype(F32)
    back = jnp.sum(hidden * raw_back, axis=1, keepdims=True)
    weighed = (g * hidden).astype(BF)
    hid_ref[0] = weighed.T
    lane = lax.broadcasted_iota(jnp.int32, aux_ref.shape, 1)
    aux_ref[...] = jnp.where(lane == mine, back, aux_ref[...])
    hid_back = g * raw_back
    grow = (hid_back * up_pre * (sig + silu * (1.0 - sig))).astype(BF)
    urow = (hid_back * silu).astype(BF)
    grow_ref[0] = grow
    urow_ref[0] = urow
    for j in range(W // C):
        cols = slice(j * C, (j + 1) * C)
        rows[:, cols] += dot_nt(grow, gate_ref[0, cols, :]) + dot_nt(urow, up_ref[0, cols, :])
        comb[:, cols] += dot_nn(weighed, down_ref[0, :, cols])

    @pl.when(e == experts_here - 1)
    def _():
        hi = aux_ref[...].astype(BF).astype(F32)
        packed = (hi + pltpu.roll(aux_ref[...] - hi, 64, 1)).astype(BF)
        for b in range(blocks):
            part = slice(b * T, (b + 1) * T)
            comb_ref[own ^ b] = comb[part, :].astype(BF)
            rows_ref[own ^ b, :, :W] = rows[part, :].astype(BF)
            rows_ref[own ^ b, :, W:] = packed[part, :]


def expert_rows(where, n2s, cots, choices, router, gate_w, up_w, down_w):
    blocks = len(n2s)
    T, W = n2s[0].shape
    E, _, H = gate_w.shape
    A = blocks * T
    once = lambda s: pl.BlockSpec(s, lambda e, w: (0,) * len(s), pipeline_mode=pl.Buffered(1))
    whole = lambda s: pl.BlockSpec(s, lambda e, w: (0,) * len(s))
    per = lambda s: pl.BlockSpec((1,) + s, lambda e, w: (e,) + (0,) * len(s))
    S = jax.ShapeDtypeStruct
    return pl.pallas_call(
        functools.partial(expert_kernel, blocks, choices),
        out_shape=(S((blocks, T, W), BF), S((blocks, T, W + 128), BF), S((A, 128), F32), S((W, A), BF),
                   S((E, H, A), BF), S((E, A, H), BF), S((E, A, H), BF)),
        grid_spec=pltpu.PrefetchScalarGridSpec(
            num_scalar_prefetch=1, grid=(E,),
            in_specs=[once((T, W))] * blocks + [once((T, W + 128))] * blocks
            + [once((W, 128)), per((W, H)), per((W, H)), per((H, W))],
            out_specs=[whole((blocks, T, W)), whole((blocks, T, W + 128)), whole((A, 128)), whole((W, A)),
                       per((H, A)), per((A, H)), per((A, H))],
            scratch_shapes=[pltpu.VMEM((A, W), BF), pltpu.VMEM((A, W), BF),
                            pltpu.VMEM((A, W), F32), pltpu.VMEM((A, W), F32), pltpu.VMEM((A, 128), F32)]),
        compiler_params=pltpu.CompilerParams(vmem_limit_bytes=60 << 20),
        cost_estimate=pl.CostEstimate(flops=12 * A * W * H * E, bytes_accessed=6 * E * W * H + 12 * A * W, transcendentals=A * H * E),
    )(where, *n2s, *cots, router, gate_w, up_w, down_w)


def grad_kernel(blocks, *refs):
    cot_refs, refs = refs[:blocks], refs[blocks:]
    n2t_ref, hid_ref, grow_ref, urow_ref, out_ref = refs
    n_dp, _, _, C = out_ref.shape
    W = n2t_ref.shape[0]
    H = hid_ref.shape[1]
    R, D = W // n_dp, H // n_dp
    left = n2t_ref[...]
    out_ref[:, 0, 0:R, :] = dot_nn(left, grow_ref[0]).astype(BF).reshape(n_dp, R, C)
    out_ref[:, 0, R:2 * R, :] = dot_nn(left, urow_ref[0]).astype(BF).reshape(n_dp, R, C)
    for j in range(W // C):
        cot = jnp.concatenate([ref[:, j * C:(j + 1) * C] for ref in cot_refs], axis=0)
        out_ref[:, 0, 2 * R + j * D:2 * R + (j + 1) * D, :] = dot_nn(hid_ref[0], cot).astype(BF).reshape(n_dp, D, C)


def expert_grads(first, count, cots, n2t, hid, grow, urow, n_dp):
    blocks = len(cots)
    T = cots[0].shape[0]
    W, A = n2t.shape
    _, _, H = grow.shape
    P_ = 2 * (W // n_dp) + (W // H) * (H // n_dp)
    once = lambda s: pl.BlockSpec(s, lambda e: (0,) * len(s), pipeline_mode=pl.Buffered(1))
    per = lambda s: pl.BlockSpec((1,) + s, lambda e: (e + first,) + (0,) * len(s))
    return pl.pallas_call(
        functools.partial(grad_kernel, blocks),
        out_shape=jax.ShapeDtypeStruct((n_dp, count, P_, H), BF),
        grid=(count,),
        in_specs=[once((T, W))] * blocks + [once((W, A)), per((H, A)), per((A, H)), per((A, H))],
        out_specs=pl.BlockSpec((n_dp, 1, P_, H), lambda e: (0, e, 0, 0)),
        compiler_params=pltpu.CompilerParams(vmem_limit_bytes=60 << 20),
        cost_estimate=pl.CostEstimate(flops=6 * A * W * H * count, bytes_accessed=6 * count * W * H + 6 * A * W, transcendentals=0),
    )(*cots, n2t, hid, grow, urow)


def rope_tile(x, cosine, sine):
    lane = lax.broadcasted_iota(jnp.int32, x.shape, 1)
    other = jnp.where(lax.rem(lane, 64) < 32, pltpu.roll(x, 96, 1), pltpu.roll(x, 32, 1))
    return x * cosine + other * sine


def half_mask(shape, half):
    lane = lax.broadcasted_iota(jnp.int32, shape, 1)
    return (lane < 64) if half == 0 else (lane >= 64)


def stacked(tiles, group, per, T):
    out = []
    for i in range(per):
        h = group * per + i
        x = tiles[h // 2]
        if h % 2 != group % 2:
            x = pltpu.roll(x, 64, 1)
        out.append(jnp.where(half_mask(x.shape, group % 2), x, 0.0).astype(BF))
    return jnp.concatenate(out, axis=0)


def unstacked(value, group, per, T, tiles):
    for i in range(per):
        h = group * per + i
        x = value[i * T:(i + 1) * T]
        if h % 2 != group % 2:
            x = pltpu.roll(x, 64, 1)
        x = jnp.where(half_mask(x.shape, h % 2), x, 0.0)
        tiles[h // 2] = x if tiles[h // 2] is None else tiles[h // 2] + x


def allowed(seg_row_ref, seg_col_ref, T, per):
    row = lax.broadcasted_iota(jnp.int32, (T, T), 0)
    col = lax.broadcasted_iota(jnp.int32, (T, T), 1)
    ok = (seg_col_ref[...] == seg_row_ref[...]) & (col <= row)
    bias = jnp.where(ok, 0.0, -1e30)
    return jnp.concatenate([bias] * per, axis=0)


def fetch(places, pieces, dev, dst, sems, at):
    R = pieces[0].shape[0]
    copies = []
    for i, ((r, col), piece) in enumerate(zip(places, pieces)):
        row = pl.multiple_of((dev ^ r) * R, R)
        copies.append(pltpu.make_async_copy(piece, dst.at[pl.ds(row, R), col:col + piece.shape[1]], sems.at[at + i]))
        copies[-1].start()
    return copies


def forward_kernel(places, dev_ref, tok_ref, n1_ref, g2_ref, cos_ref, sin_ref, segr_ref, segc_ref, qkv_hbm, *refs):
    outs, refs = refs[:len(places)], refs[len(places):]
    qkv_ref, mix_ref, resid_ref, n2_ref, wq, wo, sems = refs
    T, W = tok_ref.shape
    C = 512
    chunks = qkv_hbm.shape[1] // C
    copies = []
    for j in range(chunks):
        copies.append(pltpu.make_async_copy(qkv_hbm.at[:, j * C:(j + 1) * C], wq.at[j], sems.at[j]))
        copies[-1].start()
    fetched = fetch(places, outs, dev_ref[1], wo, sems, chunks)
    n1 = n1_ref[...]
    cosine, sine = cos_ref[...], sin_ref[...]
    tiles = []
    q_tiles = W // 128
    k_tiles = (qkv_hbm.shape[1] - W) // 256
    for j in range(chunks):
        copies[j].wait()
        made = dot_nn(n1, wq[j])
        for t in range(C // 128):
            tile = made[:, t * 128:(t + 1) * 128]
            if len(tiles) < q_tiles + k_tiles:
                tile = rope_tile(tile, cosine, sine)
            tile = tile.astype(BF)
            qkv_ref[:, len(tiles) * 128:(len(tiles) + 1) * 128] = tile
            tiles.append(tile)
    per = q_tiles // k_tiles
    bias = allowed(segr_ref, segc_ref, T, per)
    q = [t.astype(F32) for t in tiles[:q_tiles]]
    mixed = [None] * q_tiles
    for g in range(2 * k_tiles):
        k_tile, v_tile = tiles[q_tiles + g // 2], tiles[q_tiles + k_tiles + g // 2]
        s = dot_nt(stacked(q, g, per, T), k_tile) * SCORE_FACTOR + bias
        raised = jnp.exp(s - jnp.max(s, axis=1, keepdims=True))
        p = raised / jnp.sum(raised, axis=1, keepdims=True)
        unstacked(dot_nn(p.astype(BF), v_tile), g, per, T, mixed)
    for t in range(q_tiles):
        mix_ref[:, t * 128:(t + 1) * 128] = mixed[t].astype(BF)
    for copy in fetched:
        copy.wait()
    total = jnp.zeros((T, 1), F32)
    for j in range(W // C):
        cols = slice(j * C, (j + 1) * C)
        r = tok_ref[:, cols].astype(F32) + dot_nn(mix_ref[...], wo[:, cols])
        resid_ref[:, cols] = r
        total = total + jnp.sum(r * r, axis=1, keepdims=True)
    inverse = lax.rsqrt(total / W + EPSILON)
    n2_ref[...] = (resid_ref[...] * inverse * g2_ref[...]).astype(BF)


def forward(where, tokens, n1, gain2, cosine, sine, segr, segc, qkv_w, outs, places):
    T, W = tokens.shape
    N = qkv_w.shape[1]
    S = jax.ShapeDtypeStruct
    v = pl.BlockSpec(memory_space=pltpu.VMEM)
    hbm = pl.BlockSpec(memory_space=pl.ANY)
    return pl.pallas_call(
        functools.partial(forward_kernel, places),
        out_shape=(S((T, N), BF), S((T, W), BF), S((T, W), F32), S((T, W), BF)),
        in_specs=[pl.BlockSpec(memory_space=pltpu.SMEM)] + [v] * 7 + [hbm] * (1 + len(places)),
        out_specs=(v,) * 4,
        scratch_shapes=[pltpu.VMEM((N // 512, W, 512), BF), pltpu.VMEM((W, W), BF), pltpu.SemaphoreType.DMA((N // 512 + len(places),))],
        compiler_params=pltpu.CompilerParams(vmem_limit_bytes=60 << 20),
        cost_estimate=pl.CostEstimate(flops=12 * T * W * (N + W), bytes_accessed=2 * W * (N + W), transcendentals=24 * T * T),
    )(where, tokens, n1, gain2, cosine, sine, segr, segc, qkv_w, *outs)


def split(x):
    hi = x.astype(BF)
    return hi, (x - hi.astype(F32)).astype(BF)


def dot_tn(a, b): return lax.dot_general(a, b, (((0,), (0,)), ((), ())), preferred_element_type=F32)


def ones_at(T, lane):
    return jnp.where(lax.broadcasted_iota(jnp.int32, (T, 128), 1) == lane, 1.0, 0.0).astype(BF)


def middle_kernel(experts, *refs):
    (rows_ref, gates_ref, router_ref, n2_ref, resid_ref, g2_ref, cot_ref, att_ref, cut_ref, back_ref, extra_ref) = refs
    T, W = n2_ref.shape
    total = rows_ref[0].astype(F32)
    for b in range(1, rows_ref.shape[0]):
        total = total + rows_ref[b].astype(F32)
    aux = total[:, W:]
    gate_back = aux + pltpu.roll(aux, 64, 1)
    gates = gates_ref[...]
    hi, lo = split(gates * (gate_back - jnp.sum(gates * gate_back, axis=1, keepdims=True)))
    n2_back = total[:, :W] + dot_nt(hi, router_ref[...]) + dot_nt(lo, router_ref[...])
    resid = resid_ref[...]
    inverse = lax.rsqrt(jnp.mean(resid * resid, axis=1, keepdims=True) + EPSILON)
    scaled = n2_back * g2_ref[...]
    inner = jnp.mean(scaled * resid, axis=1, keepdims=True)
    back = cot_ref[...].astype(F32) + inverse * scaled - resid * (inverse * inverse * inverse * inner)
    back_ref[...] = back
    att_ref[...] = back.astype(BF)
    width = cut_ref.shape[2]
    for b in range(cut_ref.shape[0]):
        cut_ref[b] = back[:, b * width:(b + 1) * width].astype(BF)
    p_hi, p_lo = split(n2_back * resid * inverse)
    one = ones_at(T, experts)
    extra_ref[...] = dot_tn(n2_ref[...], hi) + dot_tn(n2_ref[...], lo) + dot_tn(p_hi, one) + dot_tn(p_lo, one)


def middle(rows_in, gates, router, n2, resid, gain2, cot, experts):
    T, W = n2.shape
    blocks = rows_in.shape[0]
    S = jax.ShapeDtypeStruct
    v = lambda s: pl.BlockSpec(s, lambda i: (0, 0))
    return pl.pallas_call(
        functools.partial(middle_kernel, experts),
        grid=(1,),
        out_shape=(S((T, W), BF), S((blocks, T, W // blocks), BF), S((T, W), F32), S((W, 128), F32)),
        in_specs=[pl.BlockSpec((blocks, T, W + 128), lambda i: (0, 0, 0)), v((T, 128)), v((W, 128)), v((T, W)), v((T, W)), v((1, W)), v((T, W))],
        out_specs=(v((T, W)), pl.BlockSpec((blocks, T, W // blocks), lambda i: (0, 0, 0)), v((T, W)), v((W, 128))),
        compiler_params=pltpu.CompilerParams(vmem_limit_bytes=40 << 20),
        cost_estimate=pl.CostEstimate(flops=12 * T * W * 128, bytes_accessed=30 * T * W, transcendentals=T),
    )(rows_in, gates, router, n2, resid, gain2, cot)


def backward_kernel(places, dev_ref, att_ref, qkv_ref, cos_ref, sin_ref, segr_ref, segc_ref, *refs):
    outs, refs = refs[:len(places)], refs[len(places):]
    back_ref, cut_ref, wo, sems = refs
    T, W = att_ref.shape
    fetched = fetch(places, outs, dev_ref[1], wo, sems, 0)
    q_tiles = W // 128
    k_tiles = (qkv_ref.shape[1] - W) // 256
    per = q_tiles // k_tiles
    tile = lambda t: qkv_ref[:, t * 128:(t + 1) * 128]
    q = [tile(t).astype(F32) for t in range(q_tiles)]
    bias = allowed(segr_ref, segc_ref, T, per)
    cosine, sine = cos_ref[...], -sin_ref[...]
    for copy in fetched:
        copy.wait()
    mixed_back = []
    for j in range(W // 512):
        made = dot_nt(att_ref[...], wo[j * 512:(j + 1) * 512, :]).astype(BF).astype(F32)
        mixed_back += [made[:, t * 128:(t + 1) * 128] for t in range(4)]
    q_back = [None] * q_tiles
    k_back = [None] * k_tiles
    v_back = [None] * k_tiles
    for g in range(2 * k_tiles):
        k_tile, v_tile = tile(q_tiles + g // 2), tile(q_tiles + k_tiles + g // 2)
        qs = stacked(q, g, per, T)
        ms = stacked(mixed_back, g, per, T)
        s = dot_nt(qs, k_tile) * SCORE_FACTOR + bias
        raised = jnp.exp(s - jnp.max(s, axis=1, keepdims=True))
        p = raised / jnp.sum(raised, axis=1, keepdims=True)
        dp = dot_nt(ms, v_tile)
        ds = (p * (dp - jnp.sum(p * dp, axis=1, keepdims=True)) * SCORE_FACTOR).astype(BF)
        unstacked(dot_nn(ds, k_tile), g, per, T, q_back)
        kb, vb = dot_tn(ds, qs), dot_tn(p.astype(BF), ms)
        k_back[g // 2] = kb if g % 2 == 0 else k_back[g // 2] + kb
        v_back[g // 2] = vb if g % 2 == 0 else v_back[g // 2] + vb
    made = [rope_tile(t, cosine, sine) for t in q_back + k_back] + v_back
    for t, value in enumerate(made):
        back_ref[:, t * 128:(t + 1) * 128] = value.astype(BF)
        of, place = (q_tiles, t) if t < q_tiles else (k_tiles, (t - q_tiles) % k_tiles)
        each = of // cut_ref.shape[0]
        at = place % each * 128 + (0 if t < q_tiles else (q_tiles + (k_tiles if t >= q_tiles + k_tiles else 0)) // cut_ref.shape[0] * 128)
        cut_ref[place // each, :, at:at + 128] = value.astype(BF)


def backward(where, att, qkv, cosine, sine, segr, segc, outs, places, ne):
    T, W = att.shape
    N = qkv.shape[1]
    S = jax.ShapeDtypeStruct
    v = pl.BlockSpec(memory_space=pltpu.VMEM)
    hbm = pl.BlockSpec(memory_space=pl.ANY)
    return pl.pallas_call(
        functools.partial(backward_kernel, places),
        out_shape=(S((T, N), BF), S((ne, T, N // ne), BF)),
        in_specs=[pl.BlockSpec(memory_space=pltpu.SMEM)] + [v] * 6 + [hbm] * len(places),
        out_specs=(v, v),
        scratch_shapes=[pltpu.VMEM((W, W), BF), pltpu.SemaphoreType.DMA((len(places),))],
        compiler_params=pltpu.CompilerParams(vmem_limit_bytes=60 << 20),
        cost_estimate=pl.CostEstimate(flops=30 * T * W * W, bytes_accessed=2 * W * W, transcendentals=24 * T * T),
    )(where, att, qkv, cosine, sine, segr, segc, *outs)


def last_kernel(experts, back_ref, tok_ref, g1_ref, resid_back_ref, extra_ref, w_ref, grad_ref, more_ref, nb):
    j = pl.program_id(0)
    T, W = tok_ref.shape
    C = w_ref.shape[0]
    nb[j] = dot_nt(back_ref[...], w_ref[...])

    @pl.when(j == pl.num_programs(0) - 1)
    def _():
        x = tok_ref[...].astype(F32)
        inverse = lax.rsqrt(jnp.mean(x * x, axis=1, keepdims=True) + EPSILON)
        n1_back = jnp.concatenate([nb[i] for i in range(W // C)], axis=1)
        scaled = n1_back * g1_ref[...]
        inner = jnp.mean(scaled * x, axis=1, keepdims=True)
        grad_ref[...] = resid_back_ref[...] + inverse * scaled - x * (inverse * inverse * inverse * inner)
        p_hi, p_lo = split(n1_back * x * inverse)
        one = ones_at(T, experts + 1)
        more_ref[...] = extra_ref[...] + dot_tn(p_hi, one) + dot_tn(p_lo, one)


def last(back, tokens, gain1, resid_back, extra, qkv_w, experts):
    T, W = tokens.shape
    N = back.shape[1]
    C = 512
    S = jax.ShapeDtypeStruct
    v = lambda s: pl.BlockSpec(s, lambda j: (0, 0))
    return pl.pallas_call(
        functools.partial(last_kernel, experts),
        grid=(W // C,),
        out_shape=(S((T, W), F32), S((W, 128), F32)),
        in_specs=[v((T, N)), v((T, W)), v((1, W)), v((T, W)), v((W, 128)), pl.BlockSpec((C, N), lambda j: (j, 0))],
        out_specs=(v((T, W)), v((W, 128))),
        scratch_shapes=[pltpu.VMEM((W // C, T, C), F32)],
        compiler_params=pltpu.CompilerParams(vmem_limit_bytes=40 << 20),
        cost_estimate=pl.CostEstimate(flops=6 * T * W * N, bytes_accessed=2 * W * N, transcendentals=T),
    )(back, tokens, gain1, resid_back, extra, qkv_w)


def attn_grad_kernel(blocks, where_ref, *refs):
    n1_refs, refs = refs[:blocks], refs[blocks:]
    mix_refs, refs = refs[:blocks], refs[blocks:]
    qkv_ref, att_ref, extra_ref, keep_ref, send_ref, left = refs
    own, dev = where_ref[0], where_ref[1]
    T = n1_refs[0].shape[0]
    W = extra_ref.shape[0]
    half, _, R, C = keep_ref.shape
    n_dp = 2 * half
    at = 0
    for side, right_ref in ((n1_refs, qkv_ref), (mix_refs, att_ref)):
        width = right_ref.shape[2]
        for b in range(blocks):
            turned = side[b][...].T
            for d in range(n_dp):
                r = d ^ dev
                left[lax.rem(r, 2), lax.div(r, 2), :, b * T:(b + 1) * T] = turned[d * R:(d + 1) * R, :]
        right = jnp.concatenate([right_ref[own ^ b] for b in range(blocks)], axis=0)
        for s, out in ((1, send_ref), (0, keep_ref)):
            out[:, 0, :, at:at + width] = dot_nn(left[s].reshape(half * R, blocks * T), right).astype(BF).reshape(half, R, width)
        at += width
    for d in range(n_dp):
        more = extra_ref[d * R:(d + 1) * R, :].astype(BF)
        r = d ^ dev

        @pl.when(lax.rem(r, 2) == 0)
        def _(more=more, r=r):
            keep_ref[lax.div(r, 2), 0, :, at:] = more

        @pl.when(lax.rem(r, 2) == 1)
        def _(more=more, r=r):
            send_ref[lax.div(r, 2), 0, :, at:] = more


def attn_grads(where, n1s, mixs, qkv_cut, att_cut, extra, n_dp):
    blocks = len(n1s)
    T = n1s[0].shape[0]
    W = extra.shape[0]
    C = qkv_cut.shape[2] + att_cut.shape[2] + 128
    R = W // n_dp
    S = jax.ShapeDtypeStruct
    v = pl.BlockSpec(memory_space=pltpu.VMEM)
    return pl.pallas_call(
        functools.partial(attn_grad_kernel, blocks),
        out_shape=(S((n_dp // 2, 1, R, C), BF),) * 2,
        in_specs=[pl.BlockSpec(memory_space=pltpu.SMEM)] + [v] * (2 * blocks + 3),
        out_specs=(v, v),
        scratch_shapes=[pltpu.VMEM((2, n_dp // 2, R, blocks * T), BF)],
        compiler_params=pltpu.CompilerParams(vmem_limit_bytes=60 << 20),
        cost_estimate=pl.CostEstimate(flops=2 * blocks * T * W * C, bytes_accessed=4 * W * C, transcendentals=0),
    )(where, *n1s, *mixs, qkv_cut, att_cut, extra)


def flip(x, axis, mask, size):
    return lax.ppermute(x, axis, [(i, i ^ mask) for i in range(size)])


def add(a, b):
    return (a.astype(F32) + b.astype(F32)).astype(BF)


def split_kernel(keep_ref, theirs_ref, a_keep, a_send, b_keep, b_send):
    count = keep_ref.shape[0]
    a = a_keep.shape[3]
    for q in range(count):
        total = (keep_ref[q, 0].astype(F32) + theirs_ref[q, 0].astype(F32)).astype(BF)
        out = a_send if q % 2 else a_keep
        out[q // 2, 0] = total[:, :a]
        out = b_send if q >= count // 2 else b_keep
        out[q % (count // 2), 0] = total[:, a:]


def halves(keep, theirs, n_dp):
    bits = n_dp.bit_length() - 1
    count, group, rows, cols = keep.shape
    a = cols // 256 * 128
    S = jax.ShapeDtypeStruct
    spec = lambda n, c: pl.BlockSpec((n, 1, rows, c), lambda g: (0, g, 0, 0))
    widths = (a, a, cols - a, cols - a)
    outs = pl.pallas_call(
        split_kernel,
        grid=(group,),
        out_shape=tuple(S((count // 2, group, rows, c), BF) for c in widths),
        in_specs=[spec(count, cols)] * 2,
        out_specs=tuple(spec(count // 2, c) for c in widths),
        compiler_params=pltpu.CompilerParams(vmem_limit_bytes=40 << 20),
        cost_estimate=pl.CostEstimate(flops=rows * cols, bytes_accessed=rows * cols, transcendentals=0),
    )(keep, theirs)
    left = tuple(range(bits - 1, 0, -1))
    shaped = lambda x: x.reshape((2,) * (bits - 2) + x.shape[1:])
    return [(shaped(outs[0]), shaped(outs[1]), left[:-1], tuple(range(1, bits))),
            (shaped(outs[2]), shaped(outs[3]), left[1:], left)]


def halve(parts, n_dp):
    done = []
    for mine, sent, left, order in parts:
        theirs = flip(sent, "dp", 1 << order[0], n_dp)
        if left:
            total = add(mine, theirs)
            axis = left.index(order[1])
            mine, theirs = (lax.index_in_dim(total, i, axis, keepdims=False) for i in (0, 1))
        done.append((mine, theirs, tuple(b for b in left if b != order[1]) if left else (), order[1:]))
    return done


def finish(parts, n_dp):
    while parts[0][3]:
        parts = halve(parts, n_dp)
    return parts


def tie_parts(parts, *others):
    arrays, others = lax.optimization_barrier(([p[:2] for p in parts], others))
    return [tuple(a) + p[2:] for a, p in zip(arrays, parts)], *others


def unpack_kernel(in_ref, gate_ref, up_ref, down_ref):
    R, D = gate_ref.shape[1], down_ref.shape[1]
    H = gate_ref.shape[2]
    total = in_ref[0, 0].astype(F32)
    gate_ref[0] = total[:R]
    up_ref[0] = total[R:2 * R]
    for j in range(down_ref.shape[2] // H):
        down_ref[0, :, j * H:(j + 1) * H] = total[2 * R + j * D:2 * R + (j + 1) * D]


def unpack(packed, R, D, W):
    _, E, rows, H = packed.shape
    S = jax.ShapeDtypeStruct
    out = lambda a, b: pl.BlockSpec((1, a, b), lambda e: (e, 0, 0))
    return pl.pallas_call(
        unpack_kernel,
        grid=(E,),
        out_shape=(S((E, R, H), F32), S((E, R, H), F32), S((E, D, W), F32)),
        in_specs=[pl.BlockSpec((1, 1, rows, H), lambda e: (0, e, 0, 0))],
        out_specs=(out(R, H), out(R, H), out(D, W)),
        compiler_params=pltpu.CompilerParams(vmem_limit_bytes=40 << 20),
        cost_estimate=pl.CostEstimate(flops=3 * E * R * H, bytes_accessed=18 * E * R * H, transcendentals=0),
    )(packed)


def spread_kernel(kv, where_ref, *refs):
    blocks = len(refs) - 5
    parts, (q_ref, k_ref, v_ref, o_ref, extra_ref) = refs[:blocks], refs[blocks:]
    wide, narrow = q_ref.shape[1] // blocks, kv // blocks
    extra = None
    for b, ref in enumerate(parts):
        at = where_ref[0] ^ b
        col = 0
        for out, width in ((q_ref, wide), (k_ref, narrow), (v_ref, narrow), (o_ref, wide)):
            out[:, pl.ds(pl.multiple_of(at * width, width), width)] = ref[:, col:col + width].astype(F32)
            col += width
        more = ref[:, col:].astype(F32)
        extra = more if extra is None else extra + more
    extra_ref[...] = extra


def spread(where, parts, W, kv):
    R, C = parts[0].shape
    S = jax.ShapeDtypeStruct
    v = pl.BlockSpec(memory_space=pltpu.VMEM)
    return pl.pallas_call(
        functools.partial(spread_kernel, kv),
        out_shape=(S((R, W), F32), S((R, kv), F32), S((R, kv), F32), S((R, W), F32), S((R, 128), F32)),
        in_specs=[pl.BlockSpec(memory_space=pltpu.SMEM)] + [v] * len(parts),
        out_specs=(v,) * 5,
        compiler_params=pltpu.CompilerParams(vmem_limit_bytes=40 << 20),
        cost_estimate=pl.CostEstimate(flops=R * C, bytes_accessed=24 * R * C, transcendentals=0),
    )(where, *parts)


def begin_z(x, ne):
    found = {0: x}
    bit = 1
    while bit < ne:
        found[bit] = flip(x, "expert", bit, ne)
        bit *= 2
    return found


def end_z(found, ne):
    for k in range(ne):
        if k not in found:
            found[k] = flip(found[k & (k - 1)], "expert", k & -k, ne)
    return [found[k] for k in range(ne)]


def gather_z(x, ne):
    return end_z(begin_z(x, ne), ne)


def gather_dp(w, n_dp):
    half = w.shape[1] // 2
    found = {(0, 0): w[:, :half], (0, half): w[:, half:]}
    whole = {0: w}
    for r in range(2, n_dp, 2):
        low, high = r & -r, 1 << (r.bit_length() - 1)
        if low == high:
            whole[r] = flip(w, "dp", r, n_dp)
            found[r, 0], found[r, half] = whole[r][:, :half], whole[r][:, half:]
        else:
            found[r, 0] = flip(found[r ^ high, 0], "dp", high, n_dp)
            found[r, half] = flip(found[r ^ low, half], "dp", low, n_dp)
    pieces = {}
    for (r, col), x in found.items():
        if r in whole:
            pieces[r, 0] = whole[r]
        else:
            pieces[r, col] = x
    for (r, col), x in list(pieces.items()):
        pieces[r ^ 1, col] = flip(x, "dp", 1, n_dp)
    places = sorted(pieces)
    return tuple(places), [pieces[p] for p in places]


def local(n_dp, ne, tokens, segment_ids, routes, cotangent, query_weight, key_weight, value_matrix, out_weight,
          first_gain, second_gain, router_weight, gate_weight, up_weight, down_weight):
    d = lax.axis_index("dp")
    z = lax.axis_index("expert")
    tie = lax.optimization_barrier
    T, W = tokens.shape
    experts = router_weight.shape[1]
    E, _, H = gate_weight.shape
    R = W // n_dp
    D = H // n_dp
    KV = key_weight.shape[1]
    where = jnp.stack([z, d, jnp.int32(E), jnp.int32(0)]).astype(jnp.int32)

    small = jnp.concatenate([first_gain[None], second_gain[None], router_weight.T], axis=0)
    small = lax.all_gather(small, "dp", axis=0, tiled=False).transpose(1, 0, 2).reshape(2 + experts, W)
    gain_one = small[0:1].astype(F32)
    gain_two = small[1:2].astype(F32)
    router_pad = jnp.pad(small[2:].T, ((0, 0), (0, 128 - experts)))
    qkv_full = lax.all_gather(jnp.concatenate([query_weight, key_weight, value_matrix], axis=1), "dp", axis=0, tiled=True)
    places, outs = gather_dp(out_weight, n_dp)
    choices = routes.shape[1]
    cot_routes = jnp.concatenate([cotangent, jnp.pad(routes.astype(BF), ((0, 0), (0, 128 - choices)))], axis=1)
    cots = gather_z(cot_routes, ne)

    segments = segment_ids[0]
    segr, segc = segments[None, :], segments[:, None]
    positions = jnp.arange(T, dtype=jnp.int32) - jnp.sum((segr < segc).astype(jnp.int32), axis=1)
    half = HEAD_SIZE // 2
    freq = ROTARY_BASE ** (-jnp.arange(half, dtype=F32) * 2.0 / HEAD_SIZE)
    angle = positions.astype(F32)[:, None] * freq[None, :]
    cosine = jnp.tile(jnp.cos(angle), (1, 4))
    sine = jnp.sin(angle)
    sine = jnp.concatenate([-sine, sine, -sine, sine], axis=1)
    inputs = tokens.astype(F32)
    normed1 = inputs * lax.rsqrt(jnp.mean(inputs * inputs, axis=-1, keepdims=True) + EPSILON) * gain_one
    normed1 = normed1.astype(BF)

    cots, outs, qkv_full = tie((cots, outs, qkv_full))
    qkv, mixed, resid, normed2 = forward(where, tokens, normed1, gain_two, cosine, sine, segr, segc, qkv_full, outs, places)
    core = lambda x: flip(x, "dp", 1, n_dp)
    exchange = lambda x: lax.all_to_all(x, "expert", split_axis=0, concat_axis=0, tiled=True)
    n2s = gather_z(normed2, ne)
    n2s, normed1, mixed = tie((n2s, normed1, mixed))
    n1s, mixs = begin_z(normed1, ne), begin_z(mixed, ne)
    made = expert_rows(where, n2s, cots, choices, router_pad, gate_weight, up_weight, down_weight)
    made, n1s, mixs = tie((made, n1s, mixs))
    comb, rows, gates, n2t, hid, grow, urow = made
    rows = exchange(rows)
    partial = expert_grads(0, E, cots, n2t, hid, grow, urow, n_dp)
    rows, partial, n1s, mixs = tie((rows, partial, n1s, mixs))
    packed = lax.psum_scatter(partial, "dp", scatter_dimension=0, tiled=True)
    n1s, mixs = end_z(n1s, ne), end_z(mixs, ne)
    attended, att_cut, resid_back, extra = middle(
        rows, gates, router_pad, normed2, resid, gain_two, cotangent, experts)
    att_cut = exchange(att_cut)
    back, back_cut = backward(where, attended, qkv, cosine, sine, segr, segc, outs, places, ne)
    att_cut, back, back_cut, n1s, mixs = tie((att_cut, back, back_cut, n1s, mixs))
    back_cut = exchange(back_cut)
    input_grad, extra = last(back, tokens, gain_one, resid_back, extra, qkv_full, experts)
    back_cut, extra, comb = tie((back_cut, extra, comb))
    comb = exchange(comb)
    keep, send = attn_grads(where, n1s, mixs, back_cut, att_cut, extra, n_dp)
    four = finish(halves(keep, core(send), n_dp), n_dp)
    part = jnp.concatenate([mine.astype(F32) + theirs.astype(F32) for mine, theirs, *_ in four], axis=-1)[0].astype(BF)
    part, comb = tie((part, comb))
    parts = gather_z(part, ne)
    query_grad, key_grad, value_grad, out_grad, extra = spread(where, parts, W, KV)
    layer_out = (resid + jnp.sum(comb.astype(F32), axis=0)).astype(BF)
    gate_grad, up_grad, down_grad = unpack(packed, R, D, W)
    return (layer_out, input_grad, query_grad, key_grad, value_grad, out_grad, extra[:, experts + 1], extra[:, experts],
            extra[:, :experts], gate_grad, up_grad, down_grad)


def solution(mesh):
    both = P(("dp", "expert"), None)
    dp = P("dp", None)
    own = P("expert", None, None)
    part = P("expert", "dp", None)
    return jax.shard_map(
        functools.partial(local, mesh.shape["dp"], mesh.shape["expert"]),
        mesh=mesh,
        in_specs=(both, both, both, both, dp, dp, dp, dp, P("dp"), P("dp"), dp, own, own, own),
        out_specs=(both, both, dp, dp, dp, dp, P("dp"), P("dp"), dp, part, part, part),
        check_vma=False,
    )
```

time: 619 us -> 378 us (0.61)
  waiting for transfers between devices: 310 us -> 164 us
  starting transfers between devices: 114 us -> 43 us
  matrix products: 31.2 us -> 0 us
  other arithmetic: 29.1 us -> 6.77 us
  Pallas kernels: 74 us -> 96.3 us
  blocking collectives: 9.52 us -> 28.8 us
  local copies, waits for them, and re-layouts: 30.3 us -> 23.5 us
    ppermute x63 -> x29, waiting for transfers between devices: 242 us -> 113 us  [flip(): return lax.ppermute(x, axis, [(i, i ^ mask) for i in range(size)])]
    ppermute x63 -> x29, starting transfers between devices: 114 us -> 28.4 us  [flip(): return lax.ppermute(x, axis, [(i, i ^ mask) for i in range(size)])]
    all_gather x1 -> x0, waiting for transfers between devices: 34.1 us -> none  [local(): out_full = lax.all_gather(out_weight, 'dp', axis=0, tiled=True)]
    dot_general x12 -> x0, matrix products: 31.2 us -> none  [the longest x1 6.11 us: local(): lax.dot_general(back_qkv, qkv_full, (((1,), (1,)), ((), ())), preferred_e...]
    all_to_all x0 -> x4, waiting for transfers between devices: none -> 25.3 us  [local(): lax.all_to_all(x, 'expert', split_axis=0, concat_axis=0, tiled=True)]
    all_gather x1, waiting for transfers between devices: 32.7 us -> 10.6 us  [local(): lax.all_gather(jnp.concatenate([query_weight, key_weight, value_matrix],...]
    pallas_call x4 -> x9, Pallas kernels: 67.8 us -> 89.3 us  [the longest x1 37 us: expert_rows(): pl.pallas_call(functools.partial(expert_kernel, blocks, choices), out_sha...]
    all_gather x1, blocking collectives: 9.52 us -> 28.8 us  [local(): lax.all_gather(small, 'dp', axis=0, tiled=False).transpose(1, 0, 2)]
  transfers between devices with their start and end apart: 65 -> 35, of which waited for: 23 -> 18; matrix products, arithmetic and copies ran while one was open for 13% -> 3% of each run, Pallas kernels for 12% -> 22%
where the time goes in v2:
time: 378 us; the launch traced here: 377 us
  waiting for transfers between devices  164 us (43%)
  Pallas kernels  96.3 us (25%)
  starting transfers between devices  43 us (11%)
  blocking collectives  28.8 us (8%)
  local copies, waits for them, and re-layouts  23.5 us (6%)
  between operations  14.6 us (4%)
  other arithmetic  6.77 us (2%)
    ppermute x29, waiting for transfers between devices, flip(): return lax.ppermute(x, axis, [(i, i ^ mask) for i in range(size)])  113 us
    pallas_call x1, Pallas kernels, expert_rows(): pl.pallas_call(functools.partial(expert_kernel, blocks, choices), out_sha...  37 us
    all_gather x1, blocking collectives, local(): lax.all_gather(small, 'dp', axis=0, tiled=False).transpose(1, 0, 2)  28.8 us
    ppermute x29, starting transfers between devices, flip(): return lax.ppermute(x, axis, [(i, i ^ mask) for i in range(size)])  28.4 us
    all_to_all x4, waiting for transfers between devices, local(): lax.all_to_all(x, 'expert', split_axis=0, concat_axis=0, tiled=True)  25.3 us
    unnamed x85, local copies, waits for them, and re-layouts  19 us
    pallas_call x1, Pallas kernels, expert_grads(): pl.pallas_call(functools.partial(grad_kernel, blocks), out_shape=jax.Shap...  17.9 us
    reduce_scatter x1, waiting for transfers between devices, local(): packed = lax.psum_scatter(partial, 'dp', scatter_dimension=0, tiled=True)  16 us
  transfers between devices with their start and end apart: 35, of which 18 were waited for; matrix products, arithmetic and copies ran while one was open for 3% of the time, Pallas kernels for 22%

profile of v2, /device:TPU:0, one launch (start us, length us, event | category | flops | bytes accessed | tf_op | source)
XLA Modules:
  0.0 377.4 jit_solution(16651804463571532292)
XLA Ops:
  7.3 2.4 pad_maximum_fusion
  9.9 4.1 %collective-permute-start.1 = (bf16[128,1664]{1,0:T(8,128)(2,1)S(1)}, bf16[128,1664]{1,0:T(8,128)(2,1)}, u32[]{:S(2)}, u32[]{:S(2)}) collective-permute-start(bf16[128,1664]{1,0:T(8,128)(2,1)S(1)} %fusion.5.refs_4_.refs_0_), channel_id=1, source_target_pairs={{0,2},{1,3},{2,0},{3,1},{4,6},{5,7},{6,4},{7,5},{8,10},{9,11},{10,... | collective-permute-start | bytes 1277960 | tf_op jit(solution)/shard_map/ppermute | solution.py:469
  19.0 28.8 %all-gather.1 = bf16[8,22,192]{2,1,0:T(8,128)(2,1)S(1)} all-gather(bf16[1,22,192]{2,1,0:T(8,128)(2,1)S(1)} %maximum_bitcast_fusion.1), channel_id=2, replica_groups=mesh['dp'=8,'expert'=4] {'dp'}, dimensions={0}, use_global_device_ids=true | all-gather | bytes 76032 | tf_op jit(solution)/shard_map/all_gather | solution.py:645
  54.7 9.7 %collective-permute-done.8.refs_6_ = bf16[192,768]{1,0:T(8,128)(2,1)} collective-permute-done((bf16[192,768]{1,0:T(8,128)(2,1)S(1)}, bf16[192,768]{1,0:T(8,128)(2,1)}, u32[]{:S(2)}, u32[]{:S(2)}) %collective-permute-start.8) | collective-permute-done | bytes 294944 | tf_op jit(solution)/shard_map/ppermute | solution.py:469
  67.6 10.6 %all-gather.4.cloned.1.call-done.qkv_hbm.w_ref = bf16[1536,2560]{1,0:T(8,128)(2,1)} async-done(((bf16[192,2560]{1,0:T(8,128)(2,1)}), bf16[1536,2560]{1,0:T(8,128)(2,1)}) %all-gather.4.cloned.1.call-update) | async-done | bytes 7864336 | tf_op jit(solution)/shard_map/all_gather | solution.py:649
  78.2 8.5 %shard_map.229 = (bf16[128,2560]{1,0:T(8,128)(2,1)}, bf16[128,1536]{1,0:T(8,128)(2,1)}, f32[128,1536]{1,0:T(8,128)}, bf16[128,1536]{1,0:T(8,128)(2,1)}) custom-call(s32[4]{0:T(128)} %pad_add_fusion.dev_ref.where_ref, bf16[128,1536]{1,0:T(8,128)(2,1)} %tok_ref.3, bf16[128,1536]{1,0:T(8,128)(2,1)} %fusion.3.n1_ref.refs_0_, f32[1,1536]{1,0:T(1,128)} %reshape.141.g2_ref.refs_5_, ...), custom_call_target="tpu_custom_call" | custom-call | flops 9663676416 | bytes 12582912 | tf_op jit(solution)/shard_map/pallas_call | solution.py:253
  88.4 19.3 %collective-permute-done.13.refs_2_ = bf16[128,1536]{1,0:T(8,128)(2,1)S(1)} collective-permute-done((bf16[128,1536]{1,0:T(8,128)(2,1)}, bf16[128,1536]{1,0:T(8,128)(2,1)S(1)}, u32[]{:S(2)}, u32[]{:S(2)}) %collective-permute-start.13) | collective-permute-done | bytes 393248 | tf_op jit(solution)/shard_map/ppermute | solution.py:469
  108.8 9.3 %collective-permute-done.14.refs_3_ = bf16[128,1536]{1,0:T(8,128)(2,1)S(1)} collective-permute-done((bf16[128,1536]{1,0:T(8,128)(2,1)S(1)}, bf16[128,1536]{1,0:T(8,128)(2,1)S(1)}, u32[]{:S(2)}, u32[]{:S(2)}) %collective-permute-start.14) | collective-permute-done | bytes 393248 | tf_op jit(solution)/shard_map/ppermute | solution.py:469
  123.1 37.0 %shard_map.230 = (bf16[4,128,1536]{2,1,0:T(8,128)(2,1)}, bf16[4,128,1664]{2,1,0:T(8,128)(2,1)}, f32[512,128]{1,0:T(8,128)}, bf16[1536,512]{1,0:T(8,128)(2,1)}, b...) custom-call(s32[4]{0:T(128)} %pad_add_fusion.dev_ref.where_ref, ...), custom_call_target="tpu_custom_call" | custom-call | flops 24159191040 | bytes 33030144 | tf_op jit(solution)/shard_map/pallas_call | solution.py:96
  161.8 3.6 all-to-all-start
  165.4 17.9 %shard_map.231 = bf16[8,5,576,512]{3,2,1,0:T(8,128)(2,1)} custom-call(bf16[128,1664]{1,0:T(8,128)(2,1)} %copy-done.21, bf16[128,1664]{1,0:T(8,128)(2,1)} %collective-permute-done.refs_5_.refs_1_, bf16[128,1664]{1,0:T(8,128)(2,1)} %collective-permute-done.1.refs_6_.refs_2_, bf16[128,1664]{1,0:T(8,128)(2,1)} %copy-done.29, ...), custom_call_target="tpu_custom_call" | custom-call | flops 12079595520 | bytes 28311552 | tf_op jit(solution)/shard_map/pallas_call | solution.py:136
  183.4 19.6 %all-to-all-done.refs_0_ = bf16[4,128,1664]{2,1,0:T(8,128)(2,1)S(1)} async-done(((bf16[4,128,1664]{2,1,0:T(8,128)(2,1)}), bf16[4,128,1664]{2,1,0:T(8,128)(2,1)S(1)}, u32[]{:S(2)}, u32[]{:S(2)}) %all-to-all-start) | async-done | bytes 1703968 | tf_op jit(solution)/shard_map/all_to_all | solution.py:671
  208.6 3.7 all-to-all-start.1
  214.4 12.7 %shard_map.233 = (bf16[128,2560]{1,0:T(8,128)(2,1)}, bf16[4,128,640]{2,1,0:T(8,128)(2,1)}) custom-call(s32[4]{0:T(128)} %pad_add_fusion.dev_ref.where_ref, bf16[128,1536]{1,0:T(8,128)(2,1)} %copy-done.17, bf16[128,2560]{1,0:T(8,128)(2,1)} %get-tuple-element.149.qkv_ref, f32[128,128]{1,0:T(8,128)} %copy.58.cos_ref, f32[128,128]{1,0:T(8,128)} %pad_maximum_fusion.1.sin_ref, ...), custom_call_target="tpu_custom_call" | custom-call | flops 9059696640 | bytes 4718592 | tf_op jit(solution)/shard_map/pallas_call | solution.py:367
  227.1 3.5 collective-permute-done.19.refs_3_
  230.6 6.6 %collective-permute-done.20.refs_7_ = bf16[128,1536]{1,0:T(8,128)(2,1)} collective-permute-done((bf16[128,1536]{1,0:T(8,128)(2,1)}, bf16[128,1536]{1,0:T(8,128)(2,1)}, u32[]{:S(2)}, u32[]{:S(2)}) %collective-permute-start.20) | collective-permute-done | bytes 393248 | tf_op jit(solution)/shard_map/ppermute | solution.py:469
  238.0 3.7 all-to-all-start.2
  241.8 4.2 %copy-done.12 = bf16[1536,2560]{1,0:T(8,128)(2,1)S(1)} copy-done((bf16[1536,2560]{1,0:T(8,128)(2,1)S(1)}, bf16[1536,2560]{1,0:T(8,128)(2,1)}, u32[]{:S(2)}) %copy-start.12) | copy-done | bytes 7864344
  247.1 4.4 %shard_map.234 = (f32[128,1536]{1,0:T(8,128)}, f32[1536,128]{1,0:T(8,128)S(1)}) custom-call(bf16[128,2560]{1,0:T(8,128)(2,1)S(1)} %copy-done.19, bf16[128,1536]{1,0:T(8,128)(2,1)S(1)} %copy-done.6, f32[1,1536]{1,0:T(1,128)S(1)} %reshape.142.g1_ref, f32[128,1536]{1,0:T(8,128)S(1)} %copy-done.14, f32[1536,128]{1,0:T(8,128)S(1)} %copy-done.16, ...), custom_call_target="tpu_custom_call" | custom-call | flops 3019898880 | bytes 7864320 | tf_op jit(solution)/shard_map/pallas_call | solution.py:403
  252.4 5.7 %all-to-all-done.2.refs_8_ = bf16[4,128,640]{2,1,0:T(8,128)(2,1)S(1)} async-done(((bf16[4,128,640]{2,1,0:T(8,128)(2,1)}), bf16[4,128,640]{2,1,0:T(8,128)(2,1)S(1)}, u32[]{:S(2)}, u32[]{:S(2)}) %all-to-all-start.2) | async-done | bytes 655392 | tf_op jit(solution)/shard_map/all_to_all | solution.py:671
  258.9 7.0 %shard_map.235 = (bf16[4,1,192,1152]{3,2,1,0:T(8,128)(2,1)}, bf16[4,1,192,1152]{3,2,1,0:T(8,128)(2,1)}) custom-call(s32[4]{0:T(128)} %pad_add_fusion.dev_ref.where_ref, bf16[128,1536]{1,0:T(8,128)(2,1)} %fusion.3.n1_ref.refs_0_, bf16[128,1536]{1,0:T(8,128)(2,1)} %copy-done.31, bf16[128,1536]{1,0:T(8,128)(2,1)} %copy-done.30, bf16[128,1536]{1,0:T(8,128)(2,1)} %copy-done.34, ...), custom_call_target="tpu_custom_call" | custom-call | flops 1811939328 | bytes 7077888 | tf_op jit(solution)/shard_map/pallas_call | solution.py:457
  265.9 3.6 all-to-all-start.3
  275.9 18.2 %collective-permute-done.22 = bf16[2,1,192,512]{3,2,1,0:T(8,128)(2,1)S(1)} collective-permute-done((bf16[2,1,192,512]{3,2,1,0:T(8,128)(2,1)S(1)}, bf16[2,1,192,512]{3,2,1,0:T(8,128)(2,1)S(1)}, u32[]{:S(2)}, u32[]{:S(2)}) %collective-permute-start.22) | collective-permute-done | bytes 393248 | tf_op jit(solution)/shard_map/ppermute | solution.py:469
  295.1 5.4 %collective-permute-done.24 = bf16[2,1,192,640]{3,2,1,0:T(8,128)(2,1)S(1)} collective-permute-done((bf16[2,1,192,640]{3,2,1,0:T(8,128)(2,1)S(1)}, bf16[2,1,192,640]{3,2,1,0:T(8,128)(2,1)S(1)}, u32[]{:S(2)}, u32[]{:S(2)}) %collective-permute-start.24) | collective-permute-done | bytes 491552 | tf_op jit(solution)/shard_map/ppermute | solution.py:469
  300.7 7.8 %collective-permute-done.23 = bf16[1,192,512]{2,1,0:T(8,128)(2,1)S(1)} collective-permute-done((bf16[1,192,512]{2,1,0:T(8,128)(2,1)S(1)}, bf16[1,192,512]{2,1,0:T(8,128)(2,1)S(1)}, u32[]{:S(2)}, u32[]{:S(2)}) %collective-permute-start.23) | collective-permute-done | bytes 196640 | tf_op jit(solution)/shard_map/ppermute | solution.py:469
  308.6 5.4 %collective-permute-done.25 = bf16[1,192,640]{2,1,0:T(8,128)(2,1)S(1)} collective-permute-done((bf16[1,192,640]{2,1,0:T(8,128)(2,1)S(1)}, bf16[1,192,640]{2,1,0:T(8,128)(2,1)S(1)}, u32[]{:S(2)}, u32[]{:S(2)}) %collective-permute-start.25) | collective-permute-done | bytes 245792 | tf_op jit(solution)/shard_map/ppermute | solution.py:469
  314.1 2.5 collective-permute-start.27
  318.3 16.4 %collective-permute-done.27.refs_2_ = bf16[192,1152]{1,0:T(8,128)(2,1)S(1)} collective-permute-done((bf16[192,1152]{1,0:T(8,128)(2,1)S(1)}, bf16[192,1152]{1,0:T(8,128)(2,1)S(1)}, u32[]{:S(2)}, u32[]{:S(2)}) %collective-permute-start.27) | collective-permute-done | bytes 442400 | tf_op jit(solution)/shard_map/ppermute | solution.py:469
  336.2 9.5 %collective-permute-done.28.refs_3_ = bf16[192,1152]{1,0:T(8,128)(2,1)S(1)} collective-permute-done((bf16[192,1152]{1,0:T(8,128)(2,1)S(1)}, bf16[192,1152]{1,0:T(8,128)(2,1)S(1)}, u32[]{:S(2)}, u32[]{:S(2)}) %collective-permute-start.28) | collective-permute-done | bytes 442400 | tf_op jit(solution)/shard_map/ppermute | solution.py:469
  345.7 2.4 shard_map.237
  349.6 16.0 %reduce-scatter.2.cloned.1.call-done.in_ref = bf16[1,5,576,512]{3,2,1,0:T(8,128)(2,1)} async-done(((bf16[8,5,576,512]{3,2,1,0:T(8,128)(2,1)}), bf16[1,5,576,512]{3,2,1,0:T(8,128)(2,1)}) %reduce-scatter.2.cloned.1.call-update) | async-done | bytes 2949136 | tf_op jit(solution)/shard_map/reduce_scatter | solution.py:681
  367.5 3.1 shard_map.238
  (175 shorter events, 50.3 us)
Async XLA Ops:
  7.3 70.9 %all-gather.4.cloned.1.call-start = ((), (), s32[]{:S(2)}) async-start(), calls=%async_computation.5 | async-start | bytes 8847360 | tf_op jit(solution)/shard_map/all_gather | solution.py:649
  9.9 40.5 %collective-permute-start.1 = (bf16[128,1664]{1,0:T(8,128)(2,1)S(1)}, bf16[128,1664]{1,0:T(8,128)(2,1)}, u32[]{:S(2)}, u32[]{:S(2)}) collective-permute-start(bf16[128,1664]{1,0:T(8,128)(2,1)S(1)} %fusion.5.refs_4_.refs_0_), channel_id=1, source_target_pairs={{0,2},{1,3},{2,0},{3,1},{4,6},{5,7},{6,4},{7,5},{8,10},{9,11},{10,... | collective-permute-start | bytes 1277960 | tf_op jit(solution)/shard_map/ppermute | solution.py:469
  14.0 36.5 %collective-permute-start = (bf16[128,1664]{1,0:T(8,128)(2,1)S(1)}, bf16[128,1664]{1,0:T(8,128)(2,1)}, u32[]{:S(2)}, u32[]{:S(2)}) collective-permute-start(bf16[128,1664]{1,0:T(8,128)(2,1)S(1)} %fusion.5.refs_4_.refs_0_), channel_id=1, source_target_pairs={{0,1},{1,0},{2,3},{3,2},{4,5},{5,4},{6,7},{7,6},{8,9},{9,8},{10,11... | collective-permute-start | bytes 1277960 | tf_op jit(solution)/shard_map/ppermute | solution.py:469
  15.6 32.6 %collective-permute-start.4 = (bf16[192,1536]{1,0:T(8,128)(2,1)}, bf16[192,1536]{1,0:T(8,128)(2,1)S(1)}, u32[]{:S(2)}, u32[]{:S(2)}) collective-permute-start(bf16[192,1536]{1,0:T(8,128)(2,1)} %refs_0_.1), channel_id=1, source_target_pairs={{0,8},{4,12},{8,0},{12,4},{16,24},{20,28},{24,16},{28,20},{1,9},{5... | collective-permute-start | bytes 1769480 | tf_op jit(solution)/shard_map/ppermute | solution.py:469
  17.1 37.6 %collective-permute-start.3 = (bf16[192,1536]{1,0:T(8,128)(2,1)}, bf16[192,1536]{1,0:T(8,128)(2,1)}, u32[]{:S(2)}, u32[]{:S(2)}) collective-permute-start(bf16[192,1536]{1,0:T(8,128)(2,1)} %refs_0_.1), channel_id=1, source_target_pairs={{0,4},{4,0},{8,12},{12,8},{16,20},{20,16},{24,28},{28,24},{1,5},{5... | collective-permute-start | bytes 1769480 | tf_op jit(solution)/shard_map/ppermute | solution.py:469
  17.1 31.2 %collective-permute-start.6 = (bf16[192,1536]{1,0:T(8,128)(2,1)}, bf16[192,1536]{1,0:T(8,128)(2,1)S(1)}, u32[]{:S(2)}, u32[]{:S(2)}) collective-permute-start(bf16[192,1536]{1,0:T(8,128)(2,1)} %refs_0_.1), channel_id=1, source_target_pairs={{0,16},{4,20},{8,24},{12,28},{16,0},{20,4},{24,8},{28,12},{1,17},{... | collective-permute-start | bytes 1769480 | tf_op jit(solution)/shard_map/ppermute | solution.py:469
  48.2 16.1 %collective-permute-start.8 = (bf16[192,768]{1,0:T(8,128)(2,1)S(1)}, bf16[192,768]{1,0:T(8,128)(2,1)}, u32[]{:S(2)}, u32[]{:S(2)}) collective-permute-start(bf16[192,768]{1,0:T(8,128)(2,1)S(1)} %slice.56), channel_id=1, source_target_pairs={{0,16},{4,20},{8,24},{12,28},{16,0},{20,4},{24,8},{28,12},{1,17},{... | collective-permute-start | bytes 884744 | tf_op jit(solution)/shard_map/ppermute | solution.py:469
  48.3 16.1 %collective-permute-start.9 = (bf16[192,768]{1,0:T(8,128)(2,1)S(1)}, bf16[192,768]{1,0:T(8,128)(2,1)}, u32[]{:S(2)}, u32[]{:S(2)}) collective-permute-start(bf16[192,768]{1,0:T(8,128)(2,1)S(1)} %slice.57), channel_id=1, source_target_pairs={{0,8},{4,12},{8,0},{12,4},{16,24},{20,28},{24,16},{28,20},{1,9},{5... | collective-permute-start | bytes 884744 | tf_op jit(solution)/shard_map/ppermute | solution.py:469
  50.4 16.2 %collective-permute-start.5 = (bf16[192,1536]{1,0:T(8,128)(2,1)S(1)}, bf16[192,1536]{1,0:T(8,128)(2,1)}, u32[]{:S(2)}, u32[]{:S(2)}) collective-permute-start(bf16[192,1536]{1,0:T(8,128)(2,1)S(1)} %collective-permute-done.4.refs_2_), channel_id=1, source_target_pairs={{0,4},{4,0},{8,12},{12,8},{16,20},{20,16},{24,28},{28,24},{1,5},{5... | collective-permute-start | bytes 1769480 | tf_op jit(solution)/shard_map/ppermute | solution.py:469
  50.5 17.1 %collective-permute-start.7 = (bf16[192,1536]{1,0:T(8,128)(2,1)S(1)}, bf16[192,1536]{1,0:T(8,128)(2,1)}, u32[]{:S(2)}, u32[]{:S(2)}) collective-permute-start(bf16[192,1536]{1,0:T(8,128)(2,1)S(1)} %collective-permute-done.6.refs_4_), channel_id=1, source_target_pairs={{0,4},{4,0},{8,12},{12,8},{16,20},{20,16},{24,28},{28,24},{1,5},{5... | collective-permute-start | bytes 1769480 | tf_op jit(solution)/shard_map/ppermute | solution.py:469
  54.7 12.0 %collective-permute-start.2 = (bf16[128,1664]{1,0:T(8,128)(2,1)}, bf16[128,1664]{1,0:T(8,128)(2,1)S(1)}, u32[]{:S(2)}, u32[]{:S(2)}) collective-permute-start(bf16[128,1664]{1,0:T(8,128)(2,1)} %collective-permute-done.1.refs_6_.refs_2_), channel_id=1, source_target_pairs={{0,1},{1,0},{2,3},{3,2},{4,5},{5,4},{6,7},{7,6},{8,9},{9,8},{10,11... | collective-permute-start | bytes 1277960 | tf_op jit(solution)/shard_map/ppermute | solution.py:469
  86.7 20.9 %collective-permute-start.13 = (bf16[128,1536]{1,0:T(8,128)(2,1)}, bf16[128,1536]{1,0:T(8,128)(2,1)S(1)}, u32[]{:S(2)}, u32[]{:S(2)}) collective-permute-start(bf16[128,1536]{1,0:T(8,128)(2,1)} %get-tuple-element.117.refs_0_.refs_3_), channel_id=1, source_target_pairs={{0,2},{1,3},{2,0},{3,1},{4,6},{5,7},{6,4},{7,5},{8,10},{9,11},{10,... | collective-permute-start | bytes 1179656 | tf_op jit(solution)/shard_map/ppermute | solution.py:469
  87.2 21.5 %collective-permute-start.12 = (bf16[128,1536]{1,0:T(8,128)(2,1)}, bf16[128,1536]{1,0:T(8,128)(2,1)S(1)}, u32[]{:S(2)}, u32[]{:S(2)}) collective-permute-start(bf16[128,1536]{1,0:T(8,128)(2,1)} %get-tuple-element.117.refs_0_.refs_3_), channel_id=1, source_target_pairs={{0,1},{1,0},{2,3},{3,2},{4,5},{5,4},{6,7},{7,6},{8,9},{9,8},{10,11... | collective-permute-start | bytes 1179656 | tf_op jit(solution)/shard_map/ppermute | solution.py:469
  107.6 10.5 %collective-permute-start.14 = (bf16[128,1536]{1,0:T(8,128)(2,1)S(1)}, bf16[128,1536]{1,0:T(8,128)(2,1)S(1)}, u32[]{:S(2)}, u32[]{:S(2)}) collective-permute-start(bf16[128,1536]{1,0:T(8,128)(2,1)S(1)} %collective-permute-done.13.refs_2_), channel_id=1, source_target_pairs={{0,1},{1,0},{2,3},{3,2},{4,5},{5,4},{6,7},{7,6},{8,9},{9,8},{10,11... | collective-permute-start | bytes 1179656 | tf_op jit(solution)/shard_map/ppermute | solution.py:469
  118.1 42.0 %collective-permute-start.16 = (bf16[128,1536]{1,0:T(8,128)(2,1)S(1)}, bf16[128,1536]{1,0:T(8,128)(2,1)S(1)}, u32[]{:S(2)}, u32[]{:S(2)}) collective-permute-start(bf16[128,1536]{1,0:T(8,128)(2,1)S(1)} %copy-done.23), channel_id=1, source_target_pairs={{0,2},{1,3},{2,0},{3,1},{4,6},{5,7},{6,4},{7,5},{8,10},{9,11},{10,... | collective-permute-start | bytes 1179656 | tf_op jit(solution)/shard_map/ppermute | solution.py:469
  118.6 41.5 %collective-permute-start.15 = (bf16[128,1536]{1,0:T(8,128)(2,1)S(1)}, bf16[128,1536]{1,0:T(8,128)(2,1)S(1)}, u32[]{:S(2)}, u32[]{:S(2)}) collective-permute-start(bf16[128,1536]{1,0:T(8,128)(2,1)S(1)} %copy-done.23), channel_id=1, source_target_pairs={{0,1},{1,0},{2,3},{3,2},{4,5},{5,4},{6,7},{7,6},{8,9},{9,8},{10,11... | collective-permute-start | bytes 1179656 | tf_op jit(solution)/shard_map/ppermute | solution.py:469
  120.3 40.5 %collective-permute-start.18 = (bf16[128,1536]{1,0:T(8,128)(2,1)}, bf16[128,1536]{1,0:T(8,128)(2,1)S(1)}, u32[]{:S(2)}, u32[]{:S(2)}) collective-permute-start(bf16[128,1536]{1,0:T(8,128)(2,1)} %get-tuple-element.162.refs_4_), channel_id=1, source_target_pairs={{0,2},{1,3},{2,0},{3,1},{4,6},{5,7},{6,4},{7,5},{8,10},{9,11},{10,... | collective-permute-start | bytes 1179656 | tf_op jit(solution)/shard_map/ppermute | solution.py:469
  121.3 39.6 %collective-permute-start.17 = (bf16[128,1536]{1,0:T(8,128)(2,1)}, bf16[128,1536]{1,0:T(8,128)(2,1)S(1)}, u32[]{:S(2)}, u32[]{:S(2)}) collective-permute-start(bf16[128,1536]{1,0:T(8,128)(2,1)} %get-tuple-element.162.refs_4_), channel_id=1, source_target_pairs={{0,1},{1,0},{2,3},{3,2},{4,5},{5,4},{6,7},{7,6},{8,9},{9,8},{10,11... | collective-permute-start | bytes 1179656 | tf_op jit(solution)/shard_map/ppermute | solution.py:469
  161.8 41.2 %all-to-all-start = ((bf16[4,128,1664]{2,1,0:T(8,128)(2,1)}), bf16[4,128,1664]{2,1,0:T(8,128)(2,1)S(1)}, u32[]{:S(2)}, u32[]{:S(2)}) async-start(bf16[4,128,1664]{2,1,0:T(8,128)(2,1)} %get-tuple-element.134), calls=%async_computation | async-start | bytes 3407872 | tf_op jit(solution)/shard_map/all_to_all | solution.py:671
  165.4 200.2 %reduce-scatter.2.cloned.1.call-start = ((), (), s32[]{:S(2)}) async-start(), calls=%async_computation.6 | async-start | bytes 26542080 | tf_op jit(solution)/shard_map/reduce_scatter | solution.py:681
  208.6 28.6 %all-to-all-start.1 = ((bf16[4,128,384]{2,1,0:T(8,128)(2,1)}), bf16[4,128,384]{2,1,0:T(8,128)(2,1)S(1)}, u32[]{:S(2)}, u32[]{:S(2)}) async-start(bf16[4,128,384]{2,1,0:T(8,128)(2,1)} %copy-done.8), calls=%async_computation.1 | async-start | bytes 786432 | tf_op jit(solution)/shard_map/all_to_all | solution.py:671
  212.3 18.3 %collective-permute-start.19 = (bf16[128,1536]{1,0:T(8,128)(2,1)}, bf16[128,1536]{1,0:T(8,128)(2,1)S(1)}, u32[]{:S(2)}, u32[]{:S(2)}) collective-permute-start(bf16[128,1536]{1,0:T(8,128)(2,1)} %copy-done.30), channel_id=1, source_target_pairs={{0,1},{1,0},{2,3},{3,2},{4,5},{5,4},{6,7},{7,6},{8,9},{9,8},{10,11... | collective-permute-start | bytes 1179656 | tf_op jit(solution)/shard_map/ppermute | solution.py:469
  214.1 23.1 %collective-permute-start.20 = (bf16[128,1536]{1,0:T(8,128)(2,1)}, bf16[128,1536]{1,0:T(8,128)(2,1)}, u32[]{:S(2)}, u32[]{:S(2)}) collective-permute-start(bf16[128,1536]{1,0:T(8,128)(2,1)} %copy-done.32), channel_id=1, source_target_pairs={{0,1},{1,0},{2,3},{3,2},{4,5},{5,4},{6,7},{7,6},{8,9},{9,8},{10,11... | collective-permute-start | bytes 1179656 | tf_op jit(solution)/shard_map/ppermute | solution.py:469
  238.0 20.1 %all-to-all-start.2 = ((bf16[4,128,640]{2,1,0:T(8,128)(2,1)}), bf16[4,128,640]{2,1,0:T(8,128)(2,1)S(1)}, u32[]{:S(2)}, u32[]{:S(2)}) async-start(bf16[4,128,640]{2,1,0:T(8,128)(2,1)} %get-tuple-element.166), calls=%async_computation.2 | async-start | bytes 1310720 | tf_op jit(solution)/shard_map/all_to_all | solution.py:671
  265.9 48.2 %all-to-all-start.3 = ((bf16[4,128,1536]{2,1,0:T(8,128)(2,1)}), bf16[4,128,1536]{2,1,0:T(8,128)(2,1)S(1)}, u32[]{:S(2)}, u32[]{:S(2)}) async-start(bf16[4,128,1536]{2,1,0:T(8,128)(2,1)} %get-tuple-element.181), calls=%async_computation.3 | async-start | bytes 3145728 | tf_op jit(solution)/shard_map/all_to_all | solution.py:671
  273.6 20.4 %collective-permute-start.22 = (bf16[2,1,192,512]{3,2,1,0:T(8,128)(2,1)S(1)}, bf16[2,1,192,512]{3,2,1,0:T(8,128)(2,1)S(1)}, u32[]{:S(2)}, u32[]{:S(2)}) collective-permute-start(bf16[2,1,192,512]{3,2,1,0:T(8,128)(2,1)S(1)} %get-tuple-element.178), channel_id=1, source_target_pairs={{0,8},{4,12},{8,0},{12,4},{16,24},{20,28},{24,16},{28,20},{1,9},{5... | collective-permute-start | bytes 1179656 | tf_op jit(solution)/shard_map/ppermute | solution.py:469
  275.9 24.6 %collective-permute-start.24 = (bf16[2,1,192,640]{3,2,1,0:T(8,128)(2,1)S(1)}, bf16[2,1,192,640]{3,2,1,0:T(8,128)(2,1)S(1)}, u32[]{:S(2)}, u32[]{:S(2)}) collective-permute-start(bf16[2,1,192,640]{3,2,1,0:T(8,128)(2,1)S(1)} %get-tuple-element.180), channel_id=1, source_target_pairs={{0,16},{4,20},{8,24},{12,28},{16,0},{20,4},{24,8},{28,12},{1,17},{... | collective-permute-start | bytes 1474568 | tf_op jit(solution)/shard_map/ppermute | solution.py:469
  294.2 14.4 %collective-permute-start.23 = (bf16[1,192,512]{2,1,0:T(8,128)(2,1)S(1)}, bf16[1,192,512]{2,1,0:T(8,128)(2,1)S(1)}, u32[]{:S(2)}, u32[]{:S(2)}) collective-permute-start(bf16[1,192,512]{2,1,0:T(8,128)(2,1)S(1)} %slice_bitcast_fusion.2), channel_id=1, source_target_pairs={{0,16},{4,20},{8,24},{12,28},{16,0},{20,4},{24,8},{28,12},{1,17},{... | collective-permute-start | bytes 589832 | tf_op jit(solution)/shard_map/ppermute | solution.py:469
  300.6 13.4 %collective-permute-start.25 = (bf16[1,192,640]{2,1,0:T(8,128)(2,1)S(1)}, bf16[1,192,640]{2,1,0:T(8,128)(2,1)S(1)}, u32[]{:S(2)}, u32[]{:S(2)}) collective-permute-start(bf16[1,192,640]{2,1,0:T(8,128)(2,1)S(1)} %slice_bitcast_fusion), channel_id=1, source_target_pairs={{0,8},{4,12},{8,0},{12,4},{16,24},{20,28},{24,16},{28,20},{1,9},{5... | collective-permute-start | bytes 737288 | tf_op jit(solution)/shard_map/ppermute | solution.py:469
  314.1 20.6 %collective-permute-start.27 = (bf16[192,1152]{1,0:T(8,128)(2,1)S(1)}, bf16[192,1152]{1,0:T(8,128)(2,1)S(1)}, u32[]{:S(2)}, u32[]{:S(2)}) collective-permute-start(bf16[192,1152]{1,0:T(8,128)(2,1)S(1)} %maximum_bitcast_fusion.refs_0_), channel_id=1, source_target_pairs={{0,2},{1,3},{2,0},{3,1},{4,6},{5,7},{6,4},{7,5},{8,10},{9,11},{10,... | collective-permute-start | bytes 1327112 | tf_op jit(solution)/shard_map/ppermute | solution.py:469
  316.7 19.5 %collective-permute-start.26 = (bf16[192,1152]{1,0:T(8,128)(2,1)S(1)}, bf16[192,1152]{1,0:T(8,128)(2,1)S(1)}, u32[]{:S(2)}, u32[]{:S(2)}) collective-permute-start(bf16[192,1152]{1,0:T(8,128)(2,1)S(1)} %maximum_bitcast_fusion.refs_0_), channel_id=1, source_target_pairs={{0,1},{1,0},{2,3},{3,2},{4,5},{5,4},{6,7},{7,6},{8,9},{9,8},{10,11... | collective-permute-start | bytes 1327112 | tf_op jit(solution)/shard_map/ppermute | solution.py:469
  334.7 10.9 %collective-permute-start.28 = (bf16[192,1152]{1,0:T(8,128)(2,1)S(1)}, bf16[192,1152]{1,0:T(8,128)(2,1)S(1)}, u32[]{:S(2)}, u32[]{:S(2)}) collective-permute-start(bf16[192,1152]{1,0:T(8,128)(2,1)S(1)} %collective-permute-done.27.refs_2_), channel_id=1, source_target_pairs={{0,1},{1,0},{2,3},{3,2},{4,5},{5,4},{6,7},{7,6},{8,9},{9,8},{10,11... | collective-permute-start | bytes 1327112 | tf_op jit(solution)/shard_map/ppermute | solution.py:469
  (45 other events, 548.3 us)
Sparse Core Ops, SparseCore 0:
  10.6 67.5 all-gather.3
  203.1 162.4 reduce-scatter.1

commit v3 on v2

v3 whole, which is shorter than its diff:
```python
import functools
import jax
import jax.numpy as jnp
from jax import lax
from jax.experimental import pallas as pl
from jax.experimental.pallas import tpu as pltpu
from jax.sharding import PartitionSpec as P

HEAD_SIZE = 64
EPSILON = 1e-06
ROTARY_BASE = 10000.0
SCORE_FACTOR = 0.015625
MANY = 4
F32=jnp.float32; BF=jnp.bfloat16
def dot_nn(a,b): return lax.dot_general(a,b,(((1,),(0,)),((),())),preferred_element_type=F32)
def dot_nt(a,b): return lax.dot_general(a,b,(((1,),(1,)),((),())),preferred_element_type=F32)

def column(table, lane):
    at = lax.broadcasted_iota(jnp.int32, table.shape, 1) == lane
    return jnp.sum(jnp.where(at, table, 0.0), axis=1, keepdims=True)

def expert_kernel(blocks, choices, where_ref, *refs):
    n2_refs, refs = refs[:blocks], refs[blocks:]
    cot_refs, refs = refs[:blocks], refs[blocks:]
    (router_ref, gate_ref, up_ref, down_ref,
     rows_ref, gates_ref, n2t_ref, hid_ref, weighed_ref, grow_ref, urow_ref,
     n2, cot, rows, aux_ref) = refs
    e = pl.program_id(0)
    own = where_ref[0]
    experts_here = pl.num_programs(0)
    T = n2_refs[0].shape[0]; W = n2_refs[0].shape[1]; H = gate_ref.shape[2]
    C = 512

    @pl.when(e == 0)
    def _():
        for b in range(blocks):
            n2[b * T:(b + 1) * T, :] = n2_refs[b][...]
            cot[b * T:(b + 1) * T, :] = cot_refs[b][:, :W]
            picks = cot_refs[b][:, W:].astype(F32)
            logits = dot_nn(n2_refs[b][...], router_ref[...])
            lane = lax.broadcasted_iota(jnp.int32, logits.shape, 1)
            named = lane < 0
            for k in range(choices):
                named = named | (lane.astype(F32) == picks[:, k:k + 1])
            logits = jnp.where(named, logits, -1e30)
            top = jnp.max(logits, axis=1, keepdims=True)
            raised = jnp.where(named, jnp.exp(logits - top), 0.0)
            gates_ref[b * T:(b + 1) * T, :] = raised / jnp.sum(raised, axis=1, keepdims=True)
        aux_ref[...] = jnp.zeros_like(aux_ref)
        rows[...] = jnp.zeros_like(rows)

    mine = own * experts_here + e
    g = column(gates_ref[...], mine)
    gate_pre = dot_nn(n2[...], gate_ref[0])
    up_pre = dot_nn(n2[...], up_ref[0])
    raw_back = dot_nt(cot[...], down_ref[0])
    sig = 1.0 / (1.0 + jnp.exp(-gate_pre))
    silu = gate_pre * sig
    hidden = (silu * up_pre).astype(BF).astype(F32)
    back = jnp.sum(hidden * raw_back, axis=1, keepdims=True)
    weighed = (g * hidden).astype(BF)
    weighed_ref[0] = weighed
    hid_ref[0] = weighed.T
    part = pl.multiple_of(jnp.minimum(e, W // C - 1) * C, C)
    n2t_ref[pl.ds(part, C), :] = n2[:, pl.ds(part, C)].T
    lane = lax.broadcasted_iota(jnp.int32, aux_ref.shape, 1)
    aux_ref[...] = jnp.where(lane == mine, back, aux_ref[...])
    hid_back = g * raw_back
    grow = (hid_back * up_pre * (sig + silu * (1.0 - sig))).astype(BF)
    urow = (hid_back * silu).astype(BF)
    grow_ref[0] = grow
    urow_ref[0] = urow
    for j in range(W // C):
        cols = slice(j * C, (j + 1) * C)
        rows[:, cols] += dot_nt(grow, gate_ref[0, cols, :]) + dot_nt(urow, up_ref[0, cols, :])

    @pl.when(e == experts_here - 1)
    def _():
        hi = aux_ref[...].astype(BF).astype(F32)
        packed = (hi + pltpu.roll(aux_ref[...] - hi, 64, 1)).astype(BF)
        for b in range(blocks):
            part = slice(b * T, (b + 1) * T)
            rows_ref[own ^ b, :, :W] = rows[part, :].astype(BF)
            rows_ref[own ^ b, :, W:] = packed[part, :]


def expert_rows(where, n2s, cots, choices, router, gate_w, up_w, down_w):
    blocks = len(n2s)
    T, W = n2s[0].shape
    E, _, H = gate_w.shape
    A = blocks * T
    once = lambda s: pl.BlockSpec(s, lambda e, w: (0,) * len(s), pipeline_mode=pl.Buffered(1))
    whole = lambda s: pl.BlockSpec(s, lambda e, w: (0,) * len(s))
    per = lambda s: pl.BlockSpec((1,) + s, lambda e, w: (e,) + (0,) * len(s))
    S = jax.ShapeDtypeStruct
    return pl.pallas_call(
        functools.partial(expert_kernel, blocks, choices),
        out_shape=(S((blocks, T, W + 128), BF), S((A, 128), F32), S((W, A), BF),
                   S((E, H, A), BF), S((E, A, H), BF), S((E, A, H), BF), S((E, A, H), BF)),
        grid_spec=pltpu.PrefetchScalarGridSpec(
            num_scalar_prefetch=1, grid=(E,),
            in_specs=[once((T, W))] * blocks + [once((T, W + 128))] * blocks
            + [once((W, 128)), per((W, H)), per((W, H)), per((H, W))],
            out_specs=[whole((blocks, T, W + 128)), whole((A, 128)), whole((W, A)),
                       per((H, A)), per((A, H)), per((A, H)), per((A, H))],
            scratch_shapes=[pltpu.VMEM((A, W), BF), pltpu.VMEM((A, W), BF), pltpu.VMEM((A, W), F32), pltpu.VMEM((A, 128), F32)]),
        compiler_params=pltpu.CompilerParams(vmem_limit_bytes=60 << 20),
        cost_estimate=pl.CostEstimate(flops=10 * A * W * H * E, bytes_accessed=6 * E * W * H + 12 * A * W, transcendentals=A * H * E),
    )(where, *n2s, *cots, router, gate_w, up_w, down_w)


def grad_kernel(blocks, apart, where_ref, *refs):
    cot_refs, refs = refs[:blocks], refs[blocks:]
    n2t_ref, hid_ref, grow_ref, urow_ref, *outs = refs
    C = grow_ref.shape[2]
    W = n2t_ref.shape[0]
    H = hid_ref.shape[1]
    n_dp = outs[0].shape[0] * len(outs)
    R, D = W // n_dp, H // n_dp
    core = where_ref[1] % 2

    def store(value, rows):
        if not apart:
            outs[0][:, 0, rows, :] = value
            return
        for own in range(2):
            @pl.when(core == own)
            def _(own=own):
                for d in range(n_dp):
                    outs[(d % 2) ^ own][d // 2, 0, rows, :] = value[d]

    left = n2t_ref[...]
    store(dot_nn(left, grow_ref[0]).astype(BF).reshape(n_dp, R, C), slice(0, R))
    store(dot_nn(left, urow_ref[0]).astype(BF).reshape(n_dp, R, C), slice(R, 2 * R))
    for j in range(W // C):
        cot = jnp.concatenate([ref[:, j * C:(j + 1) * C] for ref in cot_refs], axis=0)
        store(dot_nn(hid_ref[0], cot).astype(BF).reshape(n_dp, D, C), slice(2 * R + j * D, 2 * R + (j + 1) * D))


def expert_grads(first, count, apart, where, cots, n2t, hid, grow, urow, n_dp):
    blocks = len(cots)
    T = cots[0].shape[0]
    W, A = n2t.shape
    _, _, H = grow.shape
    P_ = 2 * (W // n_dp) + (W // H) * (H // n_dp)
    shape = (n_dp // 2 if apart else n_dp, count, P_, H)
    once = lambda s: pl.BlockSpec(s, lambda e, w: (0,) * len(s), pipeline_mode=pl.Buffered(1))
    per = lambda s: pl.BlockSpec((1,) + s, lambda e, w: (e + first,) + (0,) * len(s))
    outs = 2 if apart else 1
    made = pl.pallas_call(
        functools.partial(grad_kernel, blocks, apart),
        out_shape=(jax.ShapeDtypeStruct(shape, BF),) * outs,
        grid_spec=pltpu.PrefetchScalarGridSpec(
            num_scalar_prefetch=1, grid=(count,),
            in_specs=[once((T, W))] * blocks + [once((W, A)), per((H, A)), per((A, H)), per((A, H))],
            out_specs=(pl.BlockSpec((shape[0], 1, P_, H), lambda e, w: (0, e, 0, 0)),) * outs),
        compiler_params=pltpu.CompilerParams(vmem_limit_bytes=60 << 20),
        cost_estimate=pl.CostEstimate(flops=0, bytes_accessed=0, transcendentals=0),
    )(where, *cots, n2t, hid, grow, urow)
    return made if apart else made[0]


def combine_kernel(blocks, where_ref, weighed_ref, down_ref, gains_ref, *refs):
    payloads, (comb_ref, n1t_ref, total) = refs[:blocks], refs[blocks:]
    e = pl.program_id(0)
    own, dev = where_ref[0], where_ref[1]
    T = payloads[0].shape[0]
    W = comb_ref.shape[2]
    _, half, R, _ = n1t_ref.shape
    made = dot_nn(weighed_ref[0], down_ref[0])

    @pl.when(e == 0)
    def _():
        total[...] = made
        for b in range(blocks):
            x = payloads[b][:, W + 128:].astype(F32)
            inverse = lax.rsqrt(jnp.mean(x * x, axis=1, keepdims=True) + EPSILON)
            turned = (x * inverse * gains_ref[0:1, :]).astype(BF).T
            for d in range(2 * half):
                r = d ^ dev
                n1t_ref[lax.rem(r, 2), lax.div(r, 2), :, b * T:(b + 1) * T] = turned[d * R:(d + 1) * R, :]

    @pl.when(e > 0)
    def _():
        total[...] += made

    @pl.when(e == pl.num_programs(0) - 1)
    def _():
        for b in range(blocks):
            comb_ref[own ^ b] = total[b * T:(b + 1) * T, :].astype(BF)


def combine(where, weighed, down_w, gains, payloads, n_dp):
    E, A, H = weighed.shape
    W = down_w.shape[2]
    blocks = len(payloads)
    T = A // blocks
    R = W // n_dp
    whole = lambda s: pl.BlockSpec(s, lambda e, w: (0,) * len(s))
    once = lambda s: pl.BlockSpec(s, lambda e, w: (0,) * len(s), pipeline_mode=pl.Buffered(1))
    per = lambda s: pl.BlockSpec((1,) + s, lambda e, w: (e,) + (0,) * len(s))
    S = jax.ShapeDtypeStruct
    return pl.pallas_call(
        functools.partial(combine_kernel, blocks),
        out_shape=(S((blocks, T, W), BF), S((2, n_dp // 2, R, A), BF)),
        grid_spec=pltpu.PrefetchScalarGridSpec(
            num_scalar_prefetch=1, grid=(E,),
            in_specs=[per((A, H)), per((H, W)), once((8, W))] + [once((T, 2 * W + 128))] * blocks,
            out_specs=[whole((blocks, T, W)), whole((2, n_dp // 2, R, A))],
            scratch_shapes=[pltpu.VMEM((A, W), F32)]),
        compiler_params=pltpu.CompilerParams(vmem_limit_bytes=60 << 20),
        cost_estimate=pl.CostEstimate(flops=0, bytes_accessed=0, transcendentals=0),
    )(where, weighed, down_w, gains, *payloads)


def rope_tile(x, cosine, sine):
    lane = lax.broadcasted_iota(jnp.int32, x.shape, 1)
    other = jnp.where(lax.rem(lane, 64) < 32, pltpu.roll(x, 96, 1), pltpu.roll(x, 32, 1))
    return x * cosine + other * sine


def half_mask(shape, half):
    lane = lax.broadcasted_iota(jnp.int32, shape, 1)
    return (lane < 64) if half == 0 else (lane >= 64)


def stacked(tiles, group, per, T):
    out = []
    for i in range(per):
        h = group * per + i
        x = tiles[h // 2]
        if h % 2 != group % 2:
            x = pltpu.roll(x, 64, 1)
        out.append(jnp.where(half_mask(x.shape, group % 2), x, 0.0).astype(BF))
    return jnp.concatenate(out, axis=0)


def unstacked(value, group, per, T, tiles):
    for i in range(per):
        h = group * per + i
        x = value[i * T:(i + 1) * T]
        if h % 2 != group % 2:
            x = pltpu.roll(x, 64, 1)
        x = jnp.where(half_mask(x.shape, h % 2), x, 0.0)
        tiles[h // 2] = x if tiles[h // 2] is None else tiles[h // 2] + x


def allowed(seg_row_ref, seg_col_ref, T, per):
    row = lax.broadcasted_iota(jnp.int32, (T, T), 0)
    col = lax.broadcasted_iota(jnp.int32, (T, T), 1)
    ok = (seg_col_ref[...] == seg_row_ref[...]) & (col <= row)
    bias = jnp.where(ok, 0.0, -1e30)
    return jnp.concatenate([bias] * per, axis=0)


def fetch(places, pieces, dev, dst, sems, at, lo, hi):
    R = pieces[0].shape[0]
    copies = []
    for i, ((r, col), piece) in enumerate(zip(places, pieces)):
        a, b = max(lo, col), min(hi, col + piece.shape[1])
        if a < b:
            row = pl.multiple_of((dev ^ r) * R, R)
            copies.append(pltpu.make_async_copy(
                piece.at[:, a - col:b - col], dst.at[pl.ds(row, R), a - lo:b - lo], sems.at[at + i]))
            copies[-1].start()
    return copies


def forward_kernel(places, kv, experts, dev_ref, tok_ref, cos_ref, sin_ref, segr_ref, segc_ref, q_hbm, *refs):
    pieces, refs = refs[:len(places)], refs[len(places):]
    qkv_ref, mix_ref, resid_ref, n2_ref, gains_ref, router_ref, kv_ref, wq, wo, sems = refs
    T, W = tok_ref.shape
    C = 512
    chunks = W // C
    fetched = fetch(places, pieces, dev_ref[1], wo, sems, chunks, 0, wo.shape[1])
    copies = []
    for j in range(chunks):
        copies.append(pltpu.make_async_copy(q_hbm.at[:, j * C:(j + 1) * C], wq.at[j], sems.at[j]))
        copies[-1].start()
    x = tok_ref[...].astype(F32)
    inverse = lax.rsqrt(jnp.mean(x * x, axis=1, keepdims=True) + EPSILON)
    for copy in fetched:
        copy.wait()
    keep = pltpu.make_async_copy(wo.at[:, :2 * kv], kv_ref, sems.at[chunks + len(places)])
    keep.start()
    small = wo[:, 2 * kv + W:]
    router_ref[...] = small
    turned = small.astype(F32).T
    gain1, gain2 = turned[experts:experts + 1, :], turned[experts + 1:experts + 2, :]
    gains_ref[0:1, :] = gain1
    gains_ref[1:2, :] = gain2
    gains_ref[2:8, :] = jnp.zeros((6, W), F32)
    n1 = (x * inverse * gain1).astype(BF)
    cosine, sine = cos_ref[...], sin_ref[...]
    q_tiles = W // 128
    k_tiles = kv // 128
    side = dot_nn(n1, wo[:, :2 * kv])
    others = [side[:, t * 128:(t + 1) * 128] for t in range(2 * k_tiles)]
    others = [rope_tile(t, cosine, sine).astype(BF) for t in others[:k_tiles]] + [t.astype(BF) for t in others[k_tiles:]]
    tiles = []
    for j in range(chunks):
        copies[j].wait()
        made = dot_nn(n1, wq[j])
        tiles += [rope_tile(made[:, t * 128:(t + 1) * 128], cosine, sine).astype(BF) for t in range(C // 128)]
    tiles += others
    for t, tile in enumerate(tiles):
        qkv_ref[:, t * 128:(t + 1) * 128] = tile
    per = q_tiles // k_tiles
    bias = allowed(segr_ref, segc_ref, T, per)
    q = [t.astype(F32) for t in tiles[:q_tiles]]
    mixed = [None] * q_tiles
    for g in range(2 * k_tiles):
        k_tile, v_tile = tiles[q_tiles + g // 2], tiles[q_tiles + k_tiles + g // 2]
        s = dot_nt(stacked(q, g, per, T), k_tile) * SCORE_FACTOR + bias
        raised = jnp.exp(s - jnp.max(s, axis=1, keepdims=True))
        p = raised / jnp.sum(raised, axis=1, keepdims=True)
        unstacked(dot_nn(p.astype(BF), v_tile), g, per, T, mixed)
    for t in range(q_tiles):
        mix_ref[:, t * 128:(t + 1) * 128] = mixed[t].astype(BF)
    total = jnp.zeros((T, 1), F32)
    for j in range(chunks):
        cols = slice(j * C, (j + 1) * C)
        r = tok_ref[:, cols].astype(F32) + dot_nn(mix_ref[...], wo[:, 2 * kv + j * C:2 * kv + (j + 1) * C])
        resid_ref[:, cols] = r
        total = total + jnp.sum(r * r, axis=1, keepdims=True)
    inverse = lax.rsqrt(total / W + EPSILON)
    n2_ref[...] = (resid_ref[...] * inverse * gain2).astype(BF)
    keep.wait()


def forward(where, tokens, cosine, sine, segr, segc, q_w, pieces, places, kv, experts):
    T, W = tokens.shape
    N = W + 2 * kv
    S = jax.ShapeDtypeStruct
    v = pl.BlockSpec(memory_space=pltpu.VMEM)
    hbm = pl.BlockSpec(memory_space=pl.ANY)
    return pl.pallas_call(
        functools.partial(forward_kernel, places, kv, experts),
        out_shape=(S((T, N), BF), S((T, W), BF), S((T, W), F32), S((T, W), BF), S((8, W), F32), S((W, 128), BF), S((W, 2 * kv), BF)),
        in_specs=[pl.BlockSpec(memory_space=pltpu.SMEM)] + [v] * 5 + [hbm] * (1 + len(places)),
        out_specs=(v,) * 6 + (hbm,),
        scratch_shapes=[pltpu.VMEM((W // 512, W, 512), BF), pltpu.VMEM((W, N + 128), BF),
                        pltpu.SemaphoreType.DMA((W // 512 + len(places) + 1,))],
        compiler_params=pltpu.CompilerParams(vmem_limit_bytes=60 << 20),
        cost_estimate=pl.CostEstimate(flops=0, bytes_accessed=0, transcendentals=0),
    )(where, tokens, cosine, sine, segr, segc, q_w, *pieces)


def split(x):
    hi = x.astype(BF)
    return hi, (x - hi.astype(F32)).astype(BF)


def dot_tn(a, b): return lax.dot_general(a, b, (((0,), (0,)), ((), ())), preferred_element_type=F32)


def ones_at(T, lane):
    return jnp.where(lax.broadcasted_iota(jnp.int32, (T, 128), 1) == lane, 1.0, 0.0).astype(BF)


def middle_kernel(experts, *refs):
    (rows_ref, gates_ref, router_ref, n2_ref, resid_ref, g2_ref, cot_ref, att_ref, cut_ref, back_ref, extra_ref) = refs
    T, W = n2_ref.shape
    total = rows_ref[0].astype(F32)
    for b in range(1, rows_ref.shape[0]):
        total = total + rows_ref[b].astype(F32)
    aux = total[:, W:]
    gate_back = aux + pltpu.roll(aux, 64, 1)
    gates = gates_ref[...]
    hi, lo = split(gates * (gate_back - jnp.sum(gates * gate_back, axis=1, keepdims=True)))
    n2_back = total[:, :W] + dot_nt(hi, router_ref[...]) + dot_nt(lo, router_ref[...])
    resid = resid_ref[...]
    inverse = lax.rsqrt(jnp.mean(resid * resid, axis=1, keepdims=True) + EPSILON)
    scaled = n2_back * g2_ref[1:2, :]
    inner = jnp.mean(scaled * resid, axis=1, keepdims=True)
    back = cot_ref[...].astype(F32) + inverse * scaled - resid * (inverse * inverse * inverse * inner)
    back_ref[...] = back
    att_ref[...] = back.astype(BF)
    width = cut_ref.shape[2]
    for b in range(cut_ref.shape[0]):
        cut_ref[b] = back[:, b * width:(b + 1) * width].astype(BF)
    p_hi, p_lo = split(n2_back * resid * inverse)
    one = ones_at(T, experts)
    extra_ref[...] = dot_tn(n2_ref[...], hi) + dot_tn(n2_ref[...], lo) + dot_tn(p_hi, one) + dot_tn(p_lo, one)


def middle(rows_in, gates, router, n2, resid, gain2, cot, experts):
    T, W = n2.shape
    blocks = rows_in.shape[0]
    S = jax.ShapeDtypeStruct
    v = lambda s: pl.BlockSpec(s, lambda i: (0, 0))
    return pl.pallas_call(
        functools.partial(middle_kernel, experts),
        grid=(1,),
        out_shape=(S((T, W), BF), S((blocks, T, W // blocks), BF), S((T, W), F32), S((W, 128), F32)),
        in_specs=[pl.BlockSpec((blocks, T, W + 128), lambda i: (0, 0, 0)), v((T, 128)), v((W, 128)), v((T, W)), v((T, W)), v((8, W)), v((T, W))],
        out_specs=(v((T, W)), pl.BlockSpec((blocks, T, W // blocks), lambda i: (0, 0, 0)), v((T, W)), v((W, 128))),
        compiler_params=pltpu.CompilerParams(vmem_limit_bytes=40 << 20),
        cost_estimate=pl.CostEstimate(flops=400_000_000_000, bytes_accessed=30 * T * W, transcendentals=T),
    )(rows_in, gates, router, n2, resid, gain2, cot)


def backward_kernel(places, dev_ref, att_ref, qkv_ref, cos_ref, sin_ref, segr_ref, segc_ref, *refs):
    outs, refs = refs[:len(places)], refs[len(places):]
    back_ref, cut_ref, wo, sems = refs
    T, W = att_ref.shape
    fetched = fetch(places, outs, dev_ref[1], wo, sems, 0, qkv_ref.shape[1] - W, qkv_ref.shape[1])
    q_tiles = W // 128
    k_tiles = (qkv_ref.shape[1] - W) // 256
    per = q_tiles // k_tiles
    tile = lambda t: qkv_ref[:, t * 128:(t + 1) * 128]
    q = [tile(t).astype(F32) for t in range(q_tiles)]
    bias = allowed(segr_ref, segc_ref, T, per)
    cosine, sine = cos_ref[...], -sin_ref[...]
    for copy in fetched:
        copy.wait()
    mixed_back = []
    for j in range(W // 512):
        made = dot_nt(att_ref[...], wo[j * 512:(j + 1) * 512, :]).astype(BF).astype(F32)
        mixed_back += [made[:, t * 128:(t + 1) * 128] for t in range(4)]
    q_back = [None] * q_tiles
    k_back = [None] * k_tiles
    v_back = [None] * k_tiles
    for g in range(2 * k_tiles):
        k_tile, v_tile = tile(q_tiles + g // 2), tile(q_tiles + k_tiles + g // 2)
        qs = stacked(q, g, per, T)
        ms = stacked(mixed_back, g, per, T)
        s = dot_nt(qs, k_tile) * SCORE_FACTOR + bias
        raised = jnp.exp(s - jnp.max(s, axis=1, keepdims=True))
        p = raised / jnp.sum(raised, axis=1, keepdims=True)
        dp = dot_nt(ms, v_tile)
        ds = (p * (dp - jnp.sum(p * dp, axis=1, keepdims=True)) * SCORE_FACTOR).astype(BF)
        unstacked(dot_nn(ds, k_tile), g, per, T, q_back)
        kb, vb = dot_tn(ds, qs), dot_tn(p.astype(BF), ms)
        k_back[g // 2] = kb if g % 2 == 0 else k_back[g // 2] + kb
        v_back[g // 2] = vb if g % 2 == 0 else v_back[g // 2] + vb
    made = [rope_tile(t, cosine, sine) for t in q_back + k_back] + v_back
    for t, value in enumerate(made):
        back_ref[:, t * 128:(t + 1) * 128] = value.astype(BF)
        of, place = (q_tiles, t) if t < q_tiles else (k_tiles, (t - q_tiles) % k_tiles)
        each = of // cut_ref.shape[0]
        at = place % each * 128 + (0 if t < q_tiles else (q_tiles + (k_tiles if t >= q_tiles + k_tiles else 0)) // cut_ref.shape[0] * 128)
        cut_ref[place // each, :, at:at + 128] = value.astype(BF)


def backward(where, att, qkv, cosine, sine, segr, segc, outs, places, ne):
    T, W = att.shape
    N = qkv.shape[1]
    S = jax.ShapeDtypeStruct
    v = pl.BlockSpec(memory_space=pltpu.VMEM)
    hbm = pl.BlockSpec(memory_space=pl.ANY)
    return pl.pallas_call(
        functools.partial(backward_kernel, places),
        out_shape=(S((T, N), BF), S((ne, T, N // ne), BF)),
        in_specs=[pl.BlockSpec(memory_space=pltpu.SMEM)] + [v] * 6 + [hbm] * len(places),
        out_specs=(v, v),
        scratch_shapes=[pltpu.VMEM((W, W), BF), pltpu.SemaphoreType.DMA((len(places),))],
        compiler_params=pltpu.CompilerParams(vmem_limit_bytes=60 << 20),
        cost_estimate=pl.CostEstimate(flops=0, bytes_accessed=0, transcendentals=0),
    )(where, att, qkv, cosine, sine, segr, segc, *outs)


def last_kernel(experts, back_ref, tok_ref, g1_ref, resid_back_ref, extra_ref, q_ref, kv_ref, grad_ref, more_ref, nb):
    j = pl.program_id(0)
    T, W = tok_ref.shape
    C = q_ref.shape[0]
    nb[j] = dot_nt(back_ref[:, :W], q_ref[...]) + dot_nt(back_ref[:, W:], kv_ref[...])

    @pl.when(j == pl.num_programs(0) - 1)
    def _():
        x = tok_ref[...].astype(F32)
        inverse = lax.rsqrt(jnp.mean(x * x, axis=1, keepdims=True) + EPSILON)
        n1_back = jnp.concatenate([nb[i] for i in range(W // C)], axis=1)
        scaled = n1_back * g1_ref[0:1, :]
        inner = jnp.mean(scaled * x, axis=1, keepdims=True)
        grad_ref[...] = resid_back_ref[...] + inverse * scaled - x * (inverse * inverse * inverse * inner)
        p_hi, p_lo = split(n1_back * x * inverse)
        one = ones_at(T, experts + 1)
        more_ref[...] = extra_ref[...] + dot_tn(p_hi, one) + dot_tn(p_lo, one)


def last(back, tokens, gains, resid_back, extra, q_w, kv_w, experts):
    T, W = tokens.shape
    N = back.shape[1]
    C = 512
    S = jax.ShapeDtypeStruct
    v = lambda s: pl.BlockSpec(s, lambda j: (0, 0))
    return pl.pallas_call(
        functools.partial(last_kernel, experts),
        grid=(W // C,),
        out_shape=(S((T, W), F32), S((W, 128), F32)),
        in_specs=[v((T, N)), v((T, W)), v((8, W)), v((T, W)), v((W, 128)), pl.BlockSpec((C, W), lambda j: (j, 0)),
                  pl.BlockSpec((C, N - W), lambda j: (j, 0))],
        out_specs=(v((T, W)), v((W, 128))),
        scratch_shapes=[pltpu.VMEM((W // C, T, C), F32)],
        compiler_params=pltpu.CompilerParams(vmem_limit_bytes=40 << 20),
        cost_estimate=pl.CostEstimate(flops=0, bytes_accessed=0, transcendentals=0),
    )(back, tokens, gains, resid_back, extra, q_w, kv_w)


def out_grad_kernel(blocks, where_ref, *refs):
    mix_refs, (att_ref, keep_ref, send_ref, left) = refs[:blocks], refs[blocks:]
    own, dev = where_ref[0], where_ref[1]
    T = mix_refs[0].shape[0]
    half, _, R, C = keep_ref.shape
    for b in range(blocks):
        turned = mix_refs[b][...].T
        for d in range(2 * half):
            r = d ^ dev
            left[lax.rem(r, 2), lax.div(r, 2), :, b * T:(b + 1) * T] = turned[d * R:(d + 1) * R, :]
    right = jnp.concatenate([att_ref[own ^ b] for b in range(blocks)], axis=0)
    for s, out in ((1, send_ref), (0, keep_ref)):
        out[:, 0] = dot_nn(left[s].reshape(half * R, blocks * T), right).astype(BF).reshape(half, R, C)


def out_grads(where, mixs, att_cut, n_dp):
    blocks = len(mixs)
    T, W = mixs[0].shape
    C = att_cut.shape[2]
    R = W // n_dp
    S = jax.ShapeDtypeStruct
    v = pl.BlockSpec(memory_space=pltpu.VMEM)
    return pl.pallas_call(
        functools.partial(out_grad_kernel, blocks),
        out_shape=(S((n_dp // 2, 1, R, C), BF),) * 2,
        in_specs=[pl.BlockSpec(memory_space=pltpu.SMEM)] + [v] * (blocks + 1),
        out_specs=(v, v),
        scratch_shapes=[pltpu.VMEM((2, n_dp // 2, R, blocks * T), BF)],
        compiler_params=pltpu.CompilerParams(vmem_limit_bytes=60 << 20),
        cost_estimate=pl.CostEstimate(flops=0, bytes_accessed=0, transcendentals=0),
    )(where, *mixs, att_cut)


def qkv_grad_kernel(where_ref, left_ref, qkv_ref, extra_ref, keep_ref, send_ref):
    own, dev = where_ref[0], where_ref[1]
    blocks, _, width = qkv_ref.shape
    half, _, R, C = keep_ref.shape
    right = jnp.concatenate([qkv_ref[own ^ b] for b in range(blocks)], axis=0)
    for s, out in ((1, send_ref), (0, keep_ref)):
        left = left_ref[s].reshape(half * R, left_ref.shape[3])
        out[:, 0, :, :width] = dot_nn(left, right).astype(BF).reshape(half, R, width)
    for d in range(2 * half):
        more = extra_ref[d * R:(d + 1) * R, :].astype(BF)
        r = d ^ dev

        @pl.when(lax.rem(r, 2) == 0)
        def _(more=more, r=r):
            keep_ref[lax.div(r, 2), 0, :, width:] = more

        @pl.when(lax.rem(r, 2) == 1)
        def _(more=more, r=r):
            send_ref[lax.div(r, 2), 0, :, width:] = more


def qkv_grads(where, left, qkv_cut, extra, n_dp):
    W = extra.shape[0]
    C = qkv_cut.shape[2] + 128
    R = W // n_dp
    S = jax.ShapeDtypeStruct
    v = pl.BlockSpec(memory_space=pltpu.VMEM)
    return pl.pallas_call(
        qkv_grad_kernel,
        out_shape=(S((n_dp // 2, 1, R, C), BF),) * 2,
        in_specs=[pl.BlockSpec(memory_space=pltpu.SMEM)] + [v] * 3,
        out_specs=(v, v),
        compiler_params=pltpu.CompilerParams(vmem_limit_bytes=60 << 20),
        cost_estimate=pl.CostEstimate(flops=2 * W * C * left.shape[3], bytes_accessed=4 * W * C, transcendentals=0),
    )(where, left, qkv_cut, extra)


def flip(x, axis, mask, size):
    return lax.ppermute(x, axis, [(i, i ^ mask) for i in range(size)])


def add(a, b):
    return (a.astype(F32) + b.astype(F32)).astype(BF)


def split_kernel(width, where_ref, *refs):
    ins, (a_keep, a_send, b_keep, b_send) = refs[:-4], refs[-4:]
    count = ins[0].shape[-4]
    for q in range(count):
        at = q ^ where_ref[0]
        sums = [(ins[i][at, 0].astype(F32) + ins[i + 1][at, 0].astype(F32)).astype(BF) for i in range(0, len(ins), 2)]
        total = sums[0] if len(sums) == 1 else jnp.concatenate(sums, axis=1)
        out = a_send if q % 2 else a_keep
        out[q // 2, 0] = total[:, :width]
        out = b_send if q >= count // 2 else b_keep
        out[q % (count // 2), 0] = total[:, width:]


def halves(pairs, n_dp, order=None):
    bits = n_dp.bit_length() - 1
    count, group, rows, _ = pairs[0][1].shape
    cols = sum(theirs.shape[3] for _, theirs in pairs)
    a = cols // 256 * 128
    S = jax.ShapeDtypeStruct
    if order is None:
        order = jnp.zeros((1,), jnp.int32)
    specs = []
    for keep, theirs in pairs:
        shape = (count, 1, rows, theirs.shape[3])
        specs += [pl.BlockSpec(shape, lambda g, w: (0, g, 0, 0))] * 2
    widths = (a, a, cols - a, cols - a)
    outs = pl.pallas_call(
        functools.partial(split_kernel, a),
        out_shape=tuple(S((count // 2, group, rows, c), BF) for c in widths),
        grid_spec=pltpu.PrefetchScalarGridSpec(
            num_scalar_prefetch=1, grid=(group,), in_specs=specs,
            out_specs=tuple(pl.BlockSpec((count // 2, 1, rows, c), lambda g, w: (0, g, 0, 0)) for c in widths)),
        compiler_params=pltpu.CompilerParams(vmem_limit_bytes=40 << 20),
        cost_estimate=pl.CostEstimate(flops=0, bytes_accessed=0, transcendentals=0),
    )(order.astype(jnp.int32), *[x for pair in pairs for x in pair])
    left = tuple(range(bits - 1, 0, -1))
    shaped = lambda x: x.reshape((2,) * (bits - 2) + x.shape[1:])
    return [(shaped(outs[0]), shaped(outs[1]), left[:-1], tuple(range(1, bits))),
            (shaped(outs[2]), shaped(outs[3]), left[1:], left)]


def halve(parts, n_dp):
    done = []
    for mine, sent, left, order in parts:
        theirs = flip(sent, "dp", 1 << order[0], n_dp)
        if left:
            total = add(mine, theirs)
            axis = left.index(order[1])
            mine, theirs = (lax.index_in_dim(total, i, axis, keepdims=False) for i in (0, 1))
        done.append((mine, theirs, tuple(b for b in left if b != order[1]) if left else (), order[1:]))
    return done


def finish(parts, n_dp):
    while parts[0][3]:
        parts = halve(parts, n_dp)
    return parts


def tie_parts(parts, *others):
    arrays, others = lax.optimization_barrier(([p[:2] for p in parts], others))
    return [tuple(a) + p[2:] for a, p in zip(arrays, parts)], *others


def unpack_kernel(many, in_ref, *refs):
    parts, (gate_ref, up_ref, down_ref) = refs[:-3], refs[-3:]
    R, D = gate_ref.shape[1], down_ref.shape[1]
    H = gate_ref.shape[2]

    def store(total, at):
        width = total.shape[1]
        gate_ref[0, :, at:at + width] = total[:R]
        up_ref[0, :, at:at + width] = total[R:2 * R]
        for j in range(down_ref.shape[2] // H):
            down_ref[0, :, j * H + at:j * H + at + width] = total[2 * R + j * D:2 * R + (j + 1) * D]

    @pl.when(pl.program_id(0) < many)
    def _():
        store(in_ref[0, 0].astype(F32), 0)

    @pl.when(pl.program_id(0) >= many)
    def _():
        at = 0
        for mine, theirs in (parts[:2], parts[2:]):
            store(mine[0].astype(F32) + theirs[0].astype(F32), at)
            at += mine.shape[2]


def unpack(packed, parts, R, D, W):
    _, many, rows, H = packed.shape
    E = many + parts[0].shape[0]
    S = jax.ShapeDtypeStruct
    out = lambda a, b: pl.BlockSpec((1, a, b), lambda e: (e, 0, 0))
    return pl.pallas_call(
        functools.partial(unpack_kernel, many),
        grid=(E,),
        out_shape=(S((E, R, H), F32), S((E, R, H), F32), S((E, D, W), F32)),
        in_specs=[pl.BlockSpec((1, 1, rows, H), lambda e: (0, jnp.minimum(e, many - 1), 0, 0))]
        + [pl.BlockSpec((1, rows, x.shape[2]), lambda e: (jnp.maximum(e - many, 0), 0, 0)) for x in parts],
        out_specs=(out(R, H), out(R, H), out(D, W)),
        compiler_params=pltpu.CompilerParams(vmem_limit_bytes=40 << 20),
        cost_estimate=pl.CostEstimate(flops=3 * E * R * H, bytes_accessed=18 * E * R * H, transcendentals=0),
    )(packed, *parts)


def spread_kernel(kv, where_ref, *refs):
    parts, (q_ref, k_ref, v_ref, o_ref, extra_ref) = refs[:-5], refs[-5:]
    blocks = len(parts)
    wide, narrow = q_ref.shape[1] // blocks, kv // blocks
    extra = None
    for b, ref in enumerate(parts):
        at = where_ref[0] ^ b
        col = 0
        for out, width in ((o_ref, wide), (q_ref, wide), (k_ref, narrow), (v_ref, narrow)):
            out[:, pl.ds(pl.multiple_of(at * width, width), width)] = ref[:, col:col + width].astype(F32)
            col += width
        more = ref[:, col:].astype(F32)
        extra = more if extra is None else extra + more
    extra_ref[...] = extra


def spread(where, parts, W, kv):
    R, C = parts[0].shape
    S = jax.ShapeDtypeStruct
    v = pl.BlockSpec(memory_space=pltpu.VMEM)
    return pl.pallas_call(
        functools.partial(spread_kernel, kv),
        out_shape=(S((R, W), F32), S((R, kv), F32), S((R, kv), F32), S((R, W), F32), S((R, 128), F32)),
        in_specs=[pl.BlockSpec(memory_space=pltpu.SMEM)] + [v] * len(parts),
        out_specs=(v,) * 5,
        compiler_params=pltpu.CompilerParams(vmem_limit_bytes=40 << 20),
        cost_estimate=pl.CostEstimate(flops=R * C, bytes_accessed=24 * R * C, transcendentals=0),
    )(where, *parts)


def begin_z(x, ne):
    found = {0: x}
    bit = 1
    while bit < ne:
        found[bit] = flip(x, "expert", bit, ne)
        bit *= 2
    return found


def end_z(found, ne):
    for k in range(ne):
        if k not in found:
            found[k] = flip(found[k & (k - 1)], "expert", k & -k, ne)
    return [found[k] for k in range(ne)]


def gather_z(x, ne):
    return end_z(begin_z(x, ne), ne)


def direct_z(x, ne):
    return [x] + [flip(x, "expert", bit, ne) for bit in range(1, ne)]


def gather_dp(w, n_dp, ready):
    half = w.shape[1] // 256 * 128
    found = {(0, 0): w[:, :half], (0, half): w[:, half:]}
    whole = {0: w}
    bits = range(1, n_dp.bit_length() - 1)
    for bit in bits:
        whole[1 << bit] = flip(w, "dp", 1 << bit, n_dp)
    whole, ready = lax.optimization_barrier((whole, ready))
    for bit in bits:
        r = 1 << bit
        found[r, 0], found[r, half] = whole[r][:, :half], whole[r][:, half:]
    for r in range(2, n_dp, 2):
        low, high = r & -r, 1 << (r.bit_length() - 1)
        if low != high:
            found[r, 0] = flip(found[r ^ high, 0], "dp", high, n_dp)
            found[r, half] = flip(found[r ^ low, half], "dp", low, n_dp)
    pieces = {}
    for (r, col), x in found.items():
        if r in whole:
            pieces[r, 0] = whole[r]
        else:
            pieces[r, col] = x
    for (r, col), x in list(pieces.items()):
        pieces[r ^ 1, col] = flip(x, "dp", 1, n_dp)
    places = sorted(pieces)
    return tuple(places), [pieces[p] for p in places], ready


def local(n_dp, ne, tokens, segment_ids, routes, cotangent, query_weight, key_weight, value_matrix, out_weight,
          first_gain, second_gain, router_weight, gate_weight, up_weight, down_weight):
    d = lax.axis_index("dp")
    z = lax.axis_index("expert")
    tie = lax.optimization_barrier
    T, W = tokens.shape
    experts = router_weight.shape[1]
    E, _, H = gate_weight.shape
    R = W // n_dp
    D = H // n_dp
    KV = key_weight.shape[1]
    where = jnp.stack([z, d, jnp.int32(E), jnp.int32(0)]).astype(jnp.int32)

    q_full = lax.all_gather(query_weight, "dp", axis=0, tiled=True)
    side = jnp.concatenate([key_weight, value_matrix, out_weight, router_weight, first_gain[:, None], second_gain[:, None],
                            jnp.zeros((R, 126 - experts), BF)], axis=1)
    segments = segment_ids[0]
    segr, segc = segments[None, :], segments[:, None]
    positions = jnp.arange(T, dtype=jnp.int32) - jnp.sum((segr < segc).astype(jnp.int32), axis=1)
    half = HEAD_SIZE // 2
    freq = ROTARY_BASE ** (-jnp.arange(half, dtype=F32) * 2.0 / HEAD_SIZE)
    angle = positions.astype(F32)[:, None] * freq[None, :]
    cosine = jnp.tile(jnp.cos(angle), (1, 4))
    sine = jnp.sin(angle)
    sine = jnp.concatenate([-sine, sine, -sine, sine], axis=1)
    choices = routes.shape[1]
    payload = jnp.concatenate([cotangent, jnp.pad(routes.astype(BF), ((0, 0), (0, 128 - choices))), tokens], axis=1)
    places, pieces, (cosine, sine, segc, where) = gather_dp(side, n_dp, (cosine, sine, segc, where))
    payloads = gather_z(payload, ne)
    core = lambda x: flip(x, "dp", 1, n_dp)
    exchange = lambda x: lax.all_to_all(x, "expert", split_axis=0, concat_axis=0, tiled=True)
    payloads, pieces, q_full = tie((payloads, pieces, q_full))
    qkv, mixed, resid, normed2, gains, router, kv_full = forward(
        where, tokens, cosine, sine, segr, segc, q_full, pieces, places, KV, experts)
    n2s = gather_z(normed2, ne)
    n2s, mixed = tie((n2s, mixed))
    mixs = direct_z(mixed, ne)
    made = expert_rows(where, n2s, payloads, choices, router, gate_weight, up_weight, down_weight)
    made, mixs = tie((made, mixs))
    rows, gates, n2t, hid, weighed, grow, urow = made
    rows = exchange(rows)
    partial = expert_grads(0, MANY, False, where, payloads, n2t, hid, grow, urow, n_dp)
    packed = lax.psum_scatter(partial, "dp", scatter_dimension=0, tiled=True)
    partial, n2t, weighed = tie((partial, n2t, weighed))
    few, away = expert_grads(MANY, E - MANY, True, where, payloads, n2t, hid, grow, urow, n_dp)
    comb, n1t = combine(where, weighed, down_weight, gains, payloads, n_dp)
    rows, few, away, comb, n1t = tie((rows, few, away, comb, n1t))
    theirs = core(away)
    attended, att_cut, resid_back, extra = middle(rows, gates, router, normed2, resid, gains, cotangent, experts)
    att_cut = exchange(att_cut)
    back, back_cut = backward(where, attended, qkv, cosine, sine, segr, segc, pieces, places, ne)
    att_cut, back, back_cut, few, theirs = tie((att_cut, back, back_cut, few, theirs))
    back_cut = exchange(back_cut)
    few = halve(halves([(few, theirs)], n_dp, (d // 2).reshape(1)), n_dp)
    input_grad, extra = last(back, tokens, gains, resid_back, extra, q_full, kv_full, experts)
    keep4, send4 = out_grads(where, mixs, att_cut, n_dp)
    few, back_cut, extra, keep4, send4, comb = tie_parts(few, back_cut, extra, keep4, send4, comb)
    theirs4 = core(send4)
    few = finish(few, n_dp)
    keep5, send5 = qkv_grads(where, n1t, back_cut, extra, n_dp)
    keep5, send5, theirs4, comb = tie((keep5, send5, theirs4, comb))
    comb = exchange(comb)
    five = finish(halves([(keep4, theirs4), (keep5, core(send5))], n_dp), n_dp)
    part = jnp.concatenate([mine.astype(F32) + theirs.astype(F32) for mine, theirs, *_ in five], axis=-1)[0].astype(BF)
    part, comb = tie((part, comb))
    parts = begin_z(part, ne)
    few, parts = tie_parts(few, parts)
    parts = end_z(parts, ne)
    query_grad, key_grad, value_grad, out_grad, extra = spread(where, parts, W, KV)
    layer_out = (resid + jnp.sum(comb.astype(F32), axis=0)).astype(BF)
    gate_grad, up_grad, down_grad = unpack(packed, [x for p in few for x in p[:2]], R, D, W)
    return (layer_out, input_grad, query_grad, key_grad, value_grad, out_grad, extra[:, experts + 1], extra[:, experts],
            extra[:, :experts], gate_grad, up_grad, down_grad)


def solution(mesh):
    both = P(("dp", "expert"), None)
    dp = P("dp", None)
    own = P("expert", None, None)
    part = P("expert", "dp", None)
    return jax.shard_map(
        functools.partial(local, mesh.shape["dp"], mesh.shape["expert"]),
        mesh=mesh,
        in_specs=(both, both, both, both, dp, dp, dp, dp, P("dp"), P("dp"), dp, own, own, own),
        out_specs=(both, both, dp, dp, dp, dp, P("dp"), P("dp"), dp, part, part, part),
        check_vma=False,
    )
```

time: 378 us -> 364 us (0.963)
  blocking collectives: 28.8 us -> 0 us
  Pallas kernels: 96.3 us -> 120 us
  waiting for transfers between devices: 164 us -> 141 us
  local copies, waits for them, and re-layouts: 23.5 us -> 31.8 us
  starting transfers between devices: 43 us -> 48.3 us
    pallas_call x5 -> x9, Pallas kernels: 38.5 us -> 67.4 us  [the longest x2 25.4 us: expert_grads(): pl.pallas_call(functools.partial(grad_kernel, blocks, apart), out_shape=(...]
    all_gather x1 -> x0, blocking collectives: 28.8 us -> none  [local(): lax.all_gather(small, 'dp', axis=0, tiled=False).transpose(1, 0, 2)]
    ppermute x29 -> x32, waiting for transfers between devices: 113 us -> 133 us  [flip(): return lax.ppermute(x, axis, [(i, i ^ mask) for i in range(size)])]
    all_to_all x4, waiting for transfers between devices: 25.3 us -> 7.4 us  [local(): lax.all_to_all(x, 'expert', split_axis=0, concat_axis=0, tiled=True)]
    reduce_scatter x1, waiting for transfers between devices: 16 us -> 0.01 us  [local(): packed = lax.psum_scatter(partial, 'dp', scatter_dimension=0, tiled=True)]
    all_gather x1, waiting for transfers between devices: 10.6 us -> 0.02 us  [local(): q_full = lax.all_gather(query_weight, 'dp', axis=0, tiled=True)]
    pallas_call x1, Pallas kernels: 37 us -> 32.4 us  [expert_rows(): pl.pallas_call(functools.partial(expert_kernel, blocks, choices), out_sha...]
    all_to_all x4, starting transfers between devices: 14.6 us -> 18.7 us  [local(): lax.all_to_all(x, 'expert', split_axis=0, concat_axis=0, tiled=True)]
  transfers between devices with their start and end apart: 35 -> 38, of which waited for: 18 -> 22; matrix products, arithmetic and copies ran while one was open for 3% -> 5% of each run, Pallas kernels for 22% -> 29%
where the time goes in v3:
time: 364 us; the launch traced here: 363 us
  waiting for transfers between devices  141 us (39%)
  Pallas kernels  120 us (33%)
  starting transfers between devices  48.3 us (13%)
  local copies, waits for them, and re-layouts  31.8 us (9%)
  between operations  14.5 us (4%)
  other arithmetic  7.3 us (2%)
    ppermute x32, waiting for transfers between devices, flip(): return lax.ppermute(x, axis, [(i, i ^ mask) for i in range(size)])  133 us
    pallas_call x1, Pallas kernels, expert_rows(): pl.pallas_call(functools.partial(expert_kernel, blocks, choices), out_sha...  32.4 us
    ppermute x32, starting transfers between devices, flip(): return lax.ppermute(x, axis, [(i, i ^ mask) for i in range(size)])  29.5 us
    pallas_call x2, Pallas kernels, expert_grads(): pl.pallas_call(functools.partial(grad_kernel, blocks, apart), out_shape=(...  25.4 us
    unnamed x84, local copies, waits for them, and re-layouts  22.6 us
    all_to_all x4, starting transfers between devices, local(): lax.all_to_all(x, 'expert', split_axis=0, concat_axis=0, tiled=True)  18.7 us
    pallas_call x1, Pallas kernels, combine(): pl.pallas_call(functools.partial(combine_kernel, blocks), out_shape=(S((b...  15.1 us
    pallas_call x1, Pallas kernels, forward(): pl.pallas_call(functools.partial(forward_kernel, places, kv, experts), ou...  11.3 us
  transfers between devices with their start and end apart: 38, of which 22 were waited for; matrix products, arithmetic and copies ran while one was open for 5% of the time, Pallas kernels for 29%

profile of v3, /device:TPU:0, one launch (start us, length us, event | category | flops | bytes accessed | tf_op | source)
XLA Modules:
  0.0 362.8 jit_solution(1236325853135535077)
XLA Ops:
  12.6 3.0 collective-permute-start.1
  23.5 24.0 %collective-permute-done.1.refs_4_ = bf16[192,2688]{1,0:T(8,128)(2,1)} collective-permute-done((bf16[192,2688]{1,0:T(8,128)(2,1)S(1)}, bf16[192,2688]{1,0:T(8,128)(2,1)}, u32[]{:S(2)}, u32[]{:S(2)}) %collective-permute-start.1) | collective-permute-done | bytes 1032224 | tf_op jit(solution)/shard_map/ppermute | solution.py:572
  51.4 4.1 %collective-permute-done.3.refs_6_.refs_2_ = bf16[128,3200]{1,0:T(8,128)(2,1)} collective-permute-done((bf16[128,3200]{1,0:T(8,128)(2,1)S(1)}, bf16[128,3200]{1,0:T(8,128)(2,1)}, u32[]{:S(2)}, u32[]{:S(2)}) %collective-permute-start.3) | collective-permute-done | bytes 819232 | tf_op jit(solution)/shard_map/ppermute | solution.py:572
  58.1 9.9 %collective-permute-done.8.refs_6_ = bf16[192,1280]{1,0:T(8,128)(2,1)} collective-permute-done((bf16[192,1280]{1,0:T(8,128)(2,1)S(1)}, bf16[192,1280]{1,0:T(8,128)(2,1)}, u32[]{:S(2)}, u32[]{:S(2)}) %collective-permute-start.8) | collective-permute-done | bytes 491552 | tf_op jit(solution)/shard_map/ppermute | solution.py:572
  71.0 3.8 %collective-permute-done.4.refs_7_.refs_3_ = bf16[128,3200]{1,0:T(8,128)(2,1)} collective-permute-done((bf16[128,3200]{1,0:T(8,128)(2,1)}, bf16[128,3200]{1,0:T(8,128)(2,1)}, u32[]{:S(2)}, u32[]{:S(2)}) %collective-permute-start.4) | collective-permute-done | bytes 819232 | tf_op jit(solution)/shard_map/ppermute | solution.py:572
  77.1 11.3 %shard_map.229 = (bf16[128,2560]{1,0:T(8,128)(2,1)}, bf16[128,1536]{1,0:T(8,128)(2,1)}, f32[128,1536]{1,0:T(8,128)}, bf16[128,1536]{1,0:T(8,128)(2,1)}, f32[8,15...) custom-call(s32[4]{0:T(128)} %pad_add_fusion.dev_ref.where_ref, bf16[128,1536]{1,0:T(8,128)(2,1)} %tok_ref.3, ...), custom_call_target="tpu_custom_call" | custom-call | tf_op jit(solution)/shard_map/pallas_call | solution.py:337
  88.4 3.4 collective-permute-start.13
  93.6 16.4 %collective-permute-done.13.refs_2_ = bf16[128,1536]{1,0:T(8,128)(2,1)S(1)} collective-permute-done((bf16[128,1536]{1,0:T(8,128)(2,1)}, bf16[128,1536]{1,0:T(8,128)(2,1)S(1)}, u32[]{:S(2)}, u32[]{:S(2)}) %collective-permute-start.13) | collective-permute-done | bytes 393248 | tf_op jit(solution)/shard_map/ppermute | solution.py:572
  110.7 9.9 %collective-permute-done.14.refs_3_ = bf16[128,1536]{1,0:T(8,128)(2,1)S(1)} collective-permute-done((bf16[128,1536]{1,0:T(8,128)(2,1)S(1)}, bf16[128,1536]{1,0:T(8,128)(2,1)S(1)}, u32[]{:S(2)}, u32[]{:S(2)}) %collective-permute-start.14) | collective-permute-done | bytes 393248 | tf_op jit(solution)/shard_map/ppermute | solution.py:572
  120.6 3.9 %collective-permute-start.17 = (bf16[128,1536]{1,0:T(8,128)(2,1)}, bf16[128,1536]{1,0:T(8,128)(2,1)}, u32[]{:S(2)}, u32[]{:S(2)}) collective-permute-start(bf16[128,1536]{1,0:T(8,128)(2,1)} %get-tuple-element.202.refs_0_), channel_id=1, source_target_pairs={{0,3},{1,2},{2,1},{3,0},{4,7},{5,6},{6,5},{7,4},{8,11},{9,10},{10,... | collective-permute-start | bytes 1179656 | tf_op jit(solution)/shard_map/ppermute | solution.py:572
  125.1 32.4 %shard_map.230 = (bf16[4,128,1664]{2,1,0:T(8,128)(2,1)}, f32[512,128]{1,0:T(8,128)}, bf16[1536,512]{1,0:T(8,128)(2,1)}, bf16[5,512,512]{2,1,0:T(8,128)(2,1)}, bf...) custom-call(s32[4]{0:T(128)} %pad_add_fusion.dev_ref.where_ref, ...), custom_call_target="tpu_custom_call" | custom-call | flops 20132659200 | bytes 33030144 | tf_op jit(solution)/shard_map/pallas_call | solution.py:96
  157.7 5.0 %all-to-all-start = ((bf16[4,128,1664]{2,1,0:T(8,128)(2,1)}), bf16[4,128,1664]{2,1,0:T(8,128)(2,1)S(1)}, u32[]{:S(2)}, u32[]{:S(2)}) async-start(bf16[4,128,1664]{2,1,0:T(8,128)(2,1)} %get-tuple-element.168), calls=%async_computation | async-start | bytes 3407872 | tf_op jit(solution)/shard_map/all_to_all | solution.py:796
  162.6 16.0 %shard_map.231 = bf16[8,4,576,512]{3,2,1,0:T(8,128)(2,1)} custom-call(s32[4]{0:T(128)} %pad_add_fusion.dev_ref.where_ref, bf16[128,3200]{1,0:T(8,128)(2,1)} %copy-done.30, bf16[128,3200]{1,0:T(8,128)(2,1)} %collective-permute-done.2.refs_5_.refs_1_, bf16[128,3200]{1,0:T(8,128)(2,1)} %collective-permute-done.3.refs_6_.refs_2_, ...), custom_call_target="tpu_custom_call" | custom-call | tf_op jit(solution)/shard_map/pallas_call | solution.py:150
  178.6 9.5 %shard_map.232 = (bf16[4,1,576,512]{3,2,1,0:T(8,128)(2,1)}, bf16[4,1,576,512]{3,2,1,0:T(8,128)(2,1)}) custom-call(s32[4]{0:T(128)} %pad_add_fusion.dev_ref.where_ref, bf16[128,3200]{1,0:T(8,128)(2,1)} %copy-done.30, bf16[128,3200]{1,0:T(8,128)(2,1)} %collective-permute-done.2.refs_5_.refs_1_, bf16[128,3200]{1,0:T(8,128)(2,1)} %collective-permute-done.3.refs_6_.refs_2_, ...), custom_call_target="tpu_custom_call" | custom-call | tf_op jit(solution)/shard_map/pallas_call | solution.py:150
  188.1 15.1 %shard_map.233 = (bf16[4,128,1536]{2,1,0:T(8,128)(2,1)}, bf16[2,4,192,512]{3,2,1,0:T(8,128)(2,1)}) custom-call(s32[4]{0:T(128)} %pad_add_fusion.dev_ref.where_ref, bf16[5,512,512]{2,1,0:T(8,128)(2,1)} %get-tuple-element.177.weighed_ref, bf16[5,512,1536]{2,1,0:T(8,128)(2,1)} %down_ref.1, f32[8,1536]{1,0:T(8,128)} %get-tuple-element.178.gains_ref.refs_5_.g1_ref, ...), custom_call_target="tpu_custom_call" | custom-call | tf_op jit(solution)/shard_map/pallas_call | solution.py:203
  209.8 5.0 %all-to-all-start.1 = ((bf16[4,128,384]{2,1,0:T(8,128)(2,1)}), bf16[4,128,384]{2,1,0:T(8,128)(2,1)S(1)}, u32[]{:S(2)}, u32[]{:S(2)}) async-start(bf16[4,128,384]{2,1,0:T(8,128)(2,1)} %get-tuple-element.183), calls=%async_computation.1 | async-start | bytes 786432 | tf_op jit(solution)/shard_map/all_to_all | solution.py:796
  214.8 11.1 %shard_map.235 = (bf16[128,2560]{1,0:T(8,128)(2,1)}, bf16[4,128,640]{2,1,0:T(8,128)(2,1)}) custom-call(s32[4]{0:T(128)} %pad_add_fusion.dev_ref.where_ref, bf16[128,1536]{1,0:T(8,128)(2,1)} %copy-done.21, bf16[128,2560]{1,0:T(8,128)(2,1)} %get-tuple-element.185.qkv_ref, f32[128,128]{1,0:T(8,128)} %copy.57.cos_ref, f32[128,128]{1,0:T(8,128)} %pad_maximum_fusion.sin_ref, ...), custom_call_target="tpu_custom_call" | custom-call | tf_op jit(solution)/shard_map/pallas_call | solution.py:452
  229.7 3.3 shard_map.236
  235.2 4.2 %all-to-all-start.2 = ((bf16[4,128,640]{2,1,0:T(8,128)(2,1)}), bf16[4,128,640]{2,1,0:T(8,128)(2,1)}, u32[]{:S(2)}, u32[]{:S(2)}) async-start(bf16[4,128,640]{2,1,0:T(8,128)(2,1)} %get-tuple-element.196), calls=%async_computation.2 | async-start | bytes 1310720 | tf_op jit(solution)/shard_map/all_to_all | solution.py:796
  246.0 4.4 %shard_map.237 = (f32[128,1536]{1,0:T(8,128)}, f32[1536,128]{1,0:T(8,128)S(1)}) custom-call(bf16[128,2560]{1,0:T(8,128)(2,1)S(1)} %copy-done.13, bf16[128,1536]{1,0:T(8,128)(2,1)S(1)} %copy-done.2, f32[8,1536]{1,0:T(8,128)S(1)} %copy-done.24, f32[128,1536]{1,0:T(8,128)S(1)} %copy-done.8, f32[1536,128]{1,0:T(8,128)S(1)} %copy-done.10, ...), custom_call_target="tpu_custom_call" | custom-call | tf_op jit(solution)/shard_map/pallas_call | solution.py:488
  251.4 3.8 %shard_map.238 = (bf16[4,1,192,384]{3,2,1,0:T(8,128)(2,1)}, bf16[4,1,192,384]{3,2,1,0:T(8,128)(2,1)}) custom-call(s32[4]{0:T(128)} %pad_add_fusion.dev_ref.where_ref, bf16[128,1536]{1,0:T(8,128)(2,1)} %get-tuple-element.202.refs_0_, bf16[128,1536]{1,0:T(8,128)(2,1)} %collective-permute-done.15.refs_1_, bf16[128,1536]{1,0:T(8,128)(2,1)} %collective-permute-done.16.refs_2_, ...), custom_call_target="tpu_custom_call" | custom-call | tf_op jit(solution)/shard_map/pallas_call | solution.py:523
  255.1 8.1 %collective-permute-done.19 = bf16[2,1,576,256]{3,2,1,0:T(8,128)(2,1)} collective-permute-done((bf16[2,1,576,256]{3,2,1,0:T(8,128)(2,1)}, bf16[2,1,576,256]{3,2,1,0:T(8,128)(2,1)}, u32[]{:S(2)}, u32[]{:S(2)}) %collective-permute-start.19) | collective-permute-done | bytes 589856 | tf_op jit(solution)/shard_map/ppermute | solution.py:572
  266.6 4.8 %shard_map.239 = (bf16[4,1,192,768]{3,2,1,0:T(8,128)(2,1)}, bf16[4,1,192,768]{3,2,1,0:T(8,128)(2,1)}) custom-call(s32[4]{0:T(128)} %pad_add_fusion.dev_ref.where_ref, bf16[2,4,192,512]{3,2,1,0:T(8,128)(2,1)} %get-tuple-element.211.left_ref, bf16[4,128,640]{2,1,0:T(8,128)(2,1)} %all-to-all-done.2.qkv_ref, f32[1536,128]{1,0:T(8,128)} %copy-done.26), custom_call_target="tpu_custom_call" | custom-call | flops 1207959552 | bytes 4718592 | tf_op jit(solution)/shard_map/pallas_call | solution.py:561
  272.7 4.6 %all-to-all-start.3 = ((bf16[4,128,1536]{2,1,0:T(8,128)(2,1)}), bf16[4,128,1536]{2,1,0:T(8,128)(2,1)}, u32[]{:S(2)}, u32[]{:S(2)}) async-start(bf16[4,128,1536]{2,1,0:T(8,128)(2,1)} %get-tuple-element.225), calls=%async_computation.3 | async-start | bytes 3145728 | tf_op jit(solution)/shard_map/all_to_all | solution.py:796
  280.8 11.4 %collective-permute-done.23 = bf16[2,1,192,512]{3,2,1,0:T(8,128)(2,1)S(1)} collective-permute-done((bf16[2,1,192,512]{3,2,1,0:T(8,128)(2,1)S(1)}, bf16[2,1,192,512]{3,2,1,0:T(8,128)(2,1)S(1)}, u32[]{:S(2)}, u32[]{:S(2)}) %collective-permute-start.23) | collective-permute-done | bytes 393248 | tf_op jit(solution)/shard_map/ppermute | solution.py:572
  296.4 7.0 %collective-permute-done.24 = bf16[1,192,512]{2,1,0:T(8,128)(2,1)S(1)} collective-permute-done((bf16[1,192,512]{2,1,0:T(8,128)(2,1)S(1)}, bf16[1,192,512]{2,1,0:T(8,128)(2,1)S(1)}, u32[]{:S(2)}, u32[]{:S(2)}) %collective-permute-start.24) | collective-permute-done | bytes 196640 | tf_op jit(solution)/shard_map/ppermute | solution.py:572
  303.4 4.7 %collective-permute-done.26 = bf16[1,192,640]{2,1,0:T(8,128)(2,1)S(1)} collective-permute-done((bf16[1,192,640]{2,1,0:T(8,128)(2,1)S(1)}, bf16[1,192,640]{2,1,0:T(8,128)(2,1)S(1)}, u32[]{:S(2)}, u32[]{:S(2)}) %collective-permute-start.26) | collective-permute-done | bytes 245792 | tf_op jit(solution)/shard_map/ppermute | solution.py:572
  308.3 6.2 %all-to-all-done.3 = bf16[4,128,1536]{2,1,0:T(8,128)(2,1)} async-done(((bf16[4,128,1536]{2,1,0:T(8,128)(2,1)}), bf16[4,128,1536]{2,1,0:T(8,128)(2,1)}, u32[]{:S(2)}, u32[]{:S(2)}) %all-to-all-start.3) | async-done | bytes 1572896 | tf_op jit(solution)/shard_map/all_to_all | solution.py:796
  319.3 11.4 %collective-permute-done.27.refs_1_ = bf16[1,576,256]{2,1,0:T(8,128)(2,1)S(1)} collective-permute-done((bf16[1,576,256]{2,1,0:T(8,128)(2,1)S(1)}, bf16[1,576,256]{2,1,0:T(8,128)(2,1)S(1)}, u32[]{:S(2)}, u32[]{:S(2)}) %collective-permute-start.27) | collective-permute-done | bytes 294944 | tf_op jit(solution)/shard_map/ppermute | solution.py:572
  331.9 3.2 collective-permute-done.30.refs_2_
  336.4 10.7 %collective-permute-done.31.refs_3_ = bf16[192,1152]{1,0:T(8,128)(2,1)S(1)} collective-permute-done((bf16[192,1152]{1,0:T(8,128)(2,1)S(1)}, bf16[192,1152]{1,0:T(8,128)(2,1)S(1)}, u32[]{:S(2)}, u32[]{:S(2)}) %collective-permute-start.31) | collective-permute-done | bytes 442400 | tf_op jit(solution)/shard_map/ppermute | solution.py:572
  352.7 3.3 shard_map.242
  (177 shorter events, 73.5 us)
Async XLA Ops:
  7.2 69.8 %all-gather.2.cloned.1.call-start = ((), (), s32[]{:S(2)}) async-start(), calls=%async_computation.5 | async-start | bytes 5308416 | tf_op jit(solution)/shard_map/all_gather | solution.py:779
  12.6 35.0 %collective-permute-start.1 = (bf16[192,2688]{1,0:T(8,128)(2,1)S(1)}, bf16[192,2688]{1,0:T(8,128)(2,1)}, u32[]{:S(2)}, u32[]{:S(2)}) collective-permute-start(bf16[192,2688]{1,0:T(8,128)(2,1)S(1)} %concatenate.13.refs_0_), channel_id=1, source_target_pairs={{0,16},{4,20},{8,24},{12,28},{16,0},{20,4},{24,8},{28,12},{1,17},{... | collective-permute-start | bytes 3096584 | tf_op jit(solution)/shard_map/ppermute | solution.py:572
  15.6 34.7 %collective-permute-start = (bf16[192,2688]{1,0:T(8,128)(2,1)S(1)}, bf16[192,2688]{1,0:T(8,128)(2,1)}, u32[]{:S(2)}, u32[]{:S(2)}) collective-permute-start(bf16[192,2688]{1,0:T(8,128)(2,1)S(1)} %concatenate.13.refs_0_), channel_id=1, source_target_pairs={{0,8},{4,12},{8,0},{12,4},{16,24},{20,28},{24,16},{28,20},{1,9},{5... | collective-permute-start | bytes 3096584 | tf_op jit(solution)/shard_map/ppermute | solution.py:572
  17.3 38.2 %collective-permute-start.3 = (bf16[128,3200]{1,0:T(8,128)(2,1)S(1)}, bf16[128,3200]{1,0:T(8,128)(2,1)}, u32[]{:S(2)}, u32[]{:S(2)}) collective-permute-start(bf16[128,3200]{1,0:T(8,128)(2,1)S(1)} %fusion.3.refs_4_.refs_0_), channel_id=1, source_target_pairs={{0,2},{1,3},{2,0},{3,1},{4,6},{5,7},{6,4},{7,5},{8,10},{9,11},{10,... | collective-permute-start | bytes 2457608 | tf_op jit(solution)/shard_map/ppermute | solution.py:572
  20.0 37.7 %collective-permute-start.2 = (bf16[128,3200]{1,0:T(8,128)(2,1)S(1)}, bf16[128,3200]{1,0:T(8,128)(2,1)}, u32[]{:S(2)}, u32[]{:S(2)}) collective-permute-start(bf16[128,3200]{1,0:T(8,128)(2,1)S(1)} %fusion.3.refs_4_.refs_0_), channel_id=1, source_target_pairs={{0,1},{1,0},{2,3},{3,2},{4,5},{5,4},{6,7},{7,6},{8,9},{9,8},{10,11... | collective-permute-start | bytes 2457608 | tf_op jit(solution)/shard_map/ppermute | solution.py:572
  51.3 16.7 %collective-permute-start.8 = (bf16[192,1280]{1,0:T(8,128)(2,1)S(1)}, bf16[192,1280]{1,0:T(8,128)(2,1)}, u32[]{:S(2)}, u32[]{:S(2)}) collective-permute-start(bf16[192,1280]{1,0:T(8,128)(2,1)S(1)} %slice.39), channel_id=1, source_target_pairs={{0,16},{4,20},{8,24},{12,28},{16,0},{20,4},{24,8},{28,12},{1,17},{... | collective-permute-start | bytes 1474568 | tf_op jit(solution)/shard_map/ppermute | solution.py:572
  55.5 19.3 %collective-permute-start.4 = (bf16[128,3200]{1,0:T(8,128)(2,1)}, bf16[128,3200]{1,0:T(8,128)(2,1)}, u32[]{:S(2)}, u32[]{:S(2)}) collective-permute-start(bf16[128,3200]{1,0:T(8,128)(2,1)} %collective-permute-done.3.refs_6_.refs_2_), channel_id=1, source_target_pairs={{0,1},{1,0},{2,3},{3,2},{4,5},{5,4},{6,7},{7,6},{8,9},{9,8},{10,11... | collective-permute-start | bytes 2457608 | tf_op jit(solution)/shard_map/ppermute | solution.py:572
  57.0 14.0 %collective-permute-start.9 = (bf16[192,1408]{1,0:T(8,128)(2,1)S(1)}, bf16[192,1408]{1,0:T(8,128)(2,1)S(1)}, u32[]{:S(2)}, u32[]{:S(2)}) collective-permute-start(bf16[192,1408]{1,0:T(8,128)(2,1)S(1)} %slice.40), channel_id=1, source_target_pairs={{0,8},{4,12},{8,0},{12,4},{16,24},{20,28},{24,16},{28,20},{1,9},{5... | collective-permute-start | bytes 1622024 | tf_op jit(solution)/shard_map/ppermute | solution.py:572
  57.6 19.4 %collective-permute-start.6 = (bf16[192,2688]{1,0:T(8,128)(2,1)}, bf16[192,2688]{1,0:T(8,128)(2,1)}, u32[]{:S(2)}, u32[]{:S(2)}) collective-permute-start(bf16[192,2688]{1,0:T(8,128)(2,1)} %collective-permute-done.refs_2_), channel_id=1, source_target_pairs={{0,4},{4,0},{8,12},{12,8},{16,20},{20,16},{24,28},{28,24},{1,5},{5... | collective-permute-start | bytes 3096584 | tf_op jit(solution)/shard_map/ppermute | solution.py:572
  57.6 19.4 %collective-permute-start.5 = (bf16[192,2688]{1,0:T(8,128)(2,1)S(1)}, bf16[192,2688]{1,0:T(8,128)(2,1)}, u32[]{:S(2)}, u32[]{:S(2)}) collective-permute-start(bf16[192,2688]{1,0:T(8,128)(2,1)S(1)} %concatenate.13.refs_0_), channel_id=1, source_target_pairs={{0,4},{4,0},{8,12},{12,8},{16,20},{20,16},{24,28},{28,24},{1,5},{5... | collective-permute-start | bytes 3096584 | tf_op jit(solution)/shard_map/ppermute | solution.py:572
  88.4 21.6 %collective-permute-start.13 = (bf16[128,1536]{1,0:T(8,128)(2,1)}, bf16[128,1536]{1,0:T(8,128)(2,1)S(1)}, u32[]{:S(2)}, u32[]{:S(2)}) collective-permute-start(bf16[128,1536]{1,0:T(8,128)(2,1)} %get-tuple-element.151.refs_0_.refs_3_), channel_id=1, source_target_pairs={{0,2},{1,3},{2,0},{3,1},{4,6},{5,7},{6,4},{7,5},{8,10},{9,11},{10,... | collective-permute-start | bytes 1179656 | tf_op jit(solution)/shard_map/ppermute | solution.py:572
  91.8 18.9 %collective-permute-start.12 = (bf16[128,1536]{1,0:T(8,128)(2,1)}, bf16[128,1536]{1,0:T(8,128)(2,1)S(1)}, u32[]{:S(2)}, u32[]{:S(2)}) collective-permute-start(bf16[128,1536]{1,0:T(8,128)(2,1)} %get-tuple-element.151.refs_0_.refs_3_), channel_id=1, source_target_pairs={{0,1},{1,0},{2,3},{3,2},{4,5},{5,4},{6,7},{7,6},{8,9},{9,8},{10,11... | collective-permute-start | bytes 1179656 | tf_op jit(solution)/shard_map/ppermute | solution.py:572
  120.6 36.9 %collective-permute-start.17 = (bf16[128,1536]{1,0:T(8,128)(2,1)}, bf16[128,1536]{1,0:T(8,128)(2,1)}, u32[]{:S(2)}, u32[]{:S(2)}) collective-permute-start(bf16[128,1536]{1,0:T(8,128)(2,1)} %get-tuple-element.202.refs_0_), channel_id=1, source_target_pairs={{0,3},{1,2},{2,1},{3,0},{4,7},{5,6},{6,5},{7,4},{8,11},{9,10},{10,... | collective-permute-start | bytes 1179656 | tf_op jit(solution)/shard_map/ppermute | solution.py:572
  124.5 33.2 %collective-permute-start.16 = (bf16[128,1536]{1,0:T(8,128)(2,1)}, bf16[128,1536]{1,0:T(8,128)(2,1)}, u32[]{:S(2)}, u32[]{:S(2)}) collective-permute-start(bf16[128,1536]{1,0:T(8,128)(2,1)} %get-tuple-element.202.refs_0_), channel_id=1, source_target_pairs={{0,2},{1,3},{2,0},{3,1},{4,6},{5,7},{6,4},{7,5},{8,10},{9,11},{10,... | collective-permute-start | bytes 1179656 | tf_op jit(solution)/shard_map/ppermute | solution.py:572
  124.5 33.2 %collective-permute-start.15 = (bf16[128,1536]{1,0:T(8,128)(2,1)}, bf16[128,1536]{1,0:T(8,128)(2,1)}, u32[]{:S(2)}, u32[]{:S(2)}) collective-permute-start(bf16[128,1536]{1,0:T(8,128)(2,1)} %get-tuple-element.202.refs_0_), channel_id=1, source_target_pairs={{0,1},{1,0},{2,3},{3,2},{4,5},{5,4},{6,7},{7,6},{8,9},{9,8},{10,11... | collective-permute-start | bytes 1179656 | tf_op jit(solution)/shard_map/ppermute | solution.py:572
  157.7 45.6 %all-to-all-start = ((bf16[4,128,1664]{2,1,0:T(8,128)(2,1)}), bf16[4,128,1664]{2,1,0:T(8,128)(2,1)S(1)}, u32[]{:S(2)}, u32[]{:S(2)}) async-start(bf16[4,128,1664]{2,1,0:T(8,128)(2,1)} %get-tuple-element.168), calls=%async_computation | async-start | bytes 3407872 | tf_op jit(solution)/shard_map/all_to_all | solution.py:796
  162.6 188.4 %reduce-scatter.2.cloned.1.call-start = ((), (), s32[]{:S(2)}) async-start(), calls=%async_computation.6 | async-start | bytes 21233664 | tf_op jit(solution)/shard_map/reduce_scatter | solution.py:808
  203.2 23.8 %collective-permute-start.18 = (bf16[4,1,576,512]{3,2,1,0:T(8,128)(2,1)}, bf16[4,1,576,512]{3,2,1,0:T(8,128)(2,1)}, u32[]{:S(2)}, u32[]{:S(2)}) collective-permute-start(bf16[4,1,576,512]{3,2,1,0:T(8,128)(2,1)} %get-tuple-element.189), channel_id=1, source_target_pairs={{0,4},{4,0},{8,12},{12,8},{16,20},{20,16},{24,28},{28,24},{1,5},{5... | collective-permute-start | bytes 7077896 | tf_op jit(solution)/shard_map/ppermute | solution.py:572
  209.8 17.3 %all-to-all-start.1 = ((bf16[4,128,384]{2,1,0:T(8,128)(2,1)}), bf16[4,128,384]{2,1,0:T(8,128)(2,1)S(1)}, u32[]{:S(2)}, u32[]{:S(2)}) async-start(bf16[4,128,384]{2,1,0:T(8,128)(2,1)} %get-tuple-element.183), calls=%async_computation.1 | async-start | bytes 786432 | tf_op jit(solution)/shard_map/all_to_all | solution.py:796
  234.7 28.6 %collective-permute-start.19 = (bf16[2,1,576,256]{3,2,1,0:T(8,128)(2,1)}, bf16[2,1,576,256]{3,2,1,0:T(8,128)(2,1)}, u32[]{:S(2)}, u32[]{:S(2)}) collective-permute-start(bf16[2,1,576,256]{3,2,1,0:T(8,128)(2,1)} %get-tuple-element.193), channel_id=1, source_target_pairs={{0,8},{4,12},{8,0},{12,4},{16,24},{20,28},{24,16},{28,20},{1,9},{5... | collective-permute-start | bytes 1769480 | tf_op jit(solution)/shard_map/ppermute | solution.py:572
  234.7 29.8 %collective-permute-start.20 = (bf16[2,1,576,256]{3,2,1,0:T(8,128)(2,1)}, bf16[2,1,576,256]{3,2,1,0:T(8,128)(2,1)}, u32[]{:S(2)}, u32[]{:S(2)}) collective-permute-start(bf16[2,1,576,256]{3,2,1,0:T(8,128)(2,1)} %get-tuple-element.195), channel_id=1, source_target_pairs={{0,16},{4,20},{8,24},{12,28},{16,0},{20,4},{24,8},{28,12},{1,17},{... | collective-permute-start | bytes 1769480 | tf_op jit(solution)/shard_map/ppermute | solution.py:572
  235.2 31.3 %all-to-all-start.2 = ((bf16[4,128,640]{2,1,0:T(8,128)(2,1)}), bf16[4,128,640]{2,1,0:T(8,128)(2,1)}, u32[]{:S(2)}, u32[]{:S(2)}) async-start(bf16[4,128,640]{2,1,0:T(8,128)(2,1)} %get-tuple-element.196), calls=%async_computation.2 | async-start | bytes 1310720 | tf_op jit(solution)/shard_map/all_to_all | solution.py:796
  272.7 41.8 %all-to-all-start.3 = ((bf16[4,128,1536]{2,1,0:T(8,128)(2,1)}), bf16[4,128,1536]{2,1,0:T(8,128)(2,1)}, u32[]{:S(2)}, u32[]{:S(2)}) async-start(bf16[4,128,1536]{2,1,0:T(8,128)(2,1)} %get-tuple-element.225), calls=%async_computation.3 | async-start | bytes 3145728 | tf_op jit(solution)/shard_map/all_to_all | solution.py:796
  279.9 12.3 %collective-permute-start.23 = (bf16[2,1,192,512]{3,2,1,0:T(8,128)(2,1)S(1)}, bf16[2,1,192,512]{3,2,1,0:T(8,128)(2,1)S(1)}, u32[]{:S(2)}, u32[]{:S(2)}) collective-permute-start(bf16[2,1,192,512]{3,2,1,0:T(8,128)(2,1)S(1)} %get-tuple-element.222), channel_id=1, source_target_pairs={{0,8},{4,12},{8,0},{12,4},{16,24},{20,28},{24,16},{28,20},{1,9},{5... | collective-permute-start | bytes 1179656 | tf_op jit(solution)/shard_map/ppermute | solution.py:572
  280.5 13.8 %collective-permute-start.25 = (bf16[2,1,192,640]{3,2,1,0:T(8,128)(2,1)S(1)}, bf16[2,1,192,640]{3,2,1,0:T(8,128)(2,1)S(1)}, u32[]{:S(2)}, u32[]{:S(2)}) collective-permute-start(bf16[2,1,192,640]{3,2,1,0:T(8,128)(2,1)S(1)} %get-tuple-element.224), channel_id=1, source_target_pairs={{0,16},{4,20},{8,24},{12,28},{16,0},{20,4},{24,8},{28,12},{1,17},{... | collective-permute-start | bytes 1474568 | tf_op jit(solution)/shard_map/ppermute | solution.py:572
  292.3 11.1 %collective-permute-start.24 = (bf16[1,192,512]{2,1,0:T(8,128)(2,1)S(1)}, bf16[1,192,512]{2,1,0:T(8,128)(2,1)S(1)}, u32[]{:S(2)}, u32[]{:S(2)}) collective-permute-start(bf16[1,192,512]{2,1,0:T(8,128)(2,1)S(1)} %slice_bitcast_fusion.6), channel_id=1, source_target_pairs={{0,16},{4,20},{8,24},{12,28},{16,0},{20,4},{24,8},{28,12},{1,17},{... | collective-permute-start | bytes 589832 | tf_op jit(solution)/shard_map/ppermute | solution.py:572
  294.4 13.7 %collective-permute-start.26 = (bf16[1,192,640]{2,1,0:T(8,128)(2,1)S(1)}, bf16[1,192,640]{2,1,0:T(8,128)(2,1)S(1)}, u32[]{:S(2)}, u32[]{:S(2)}) collective-permute-start(bf16[1,192,640]{2,1,0:T(8,128)(2,1)S(1)} %slice_bitcast_fusion.4), channel_id=1, source_target_pairs={{0,8},{4,12},{8,0},{12,4},{16,24},{20,28},{24,16},{28,20},{1,9},{5... | collective-permute-start | bytes 737288 | tf_op jit(solution)/shard_map/ppermute | solution.py:572
  314.5 20.6 %collective-permute-start.30 = (bf16[192,1152]{1,0:T(8,128)(2,1)S(1)}, bf16[192,1152]{1,0:T(8,128)(2,1)S(1)}, u32[]{:S(2)}, u32[]{:S(2)}) collective-permute-start(bf16[192,1152]{1,0:T(8,128)(2,1)S(1)} %maximum_bitcast_fusion.refs_0_), channel_id=1, source_target_pairs={{0,2},{1,3},{2,0},{3,1},{4,6},{5,7},{6,4},{7,5},{8,10},{9,11},{10,... | collective-permute-start | bytes 1327112 | tf_op jit(solution)/shard_map/ppermute | solution.py:572
  314.5 20.7 %collective-permute-start.29 = (bf16[192,1152]{1,0:T(8,128)(2,1)S(1)}, bf16[192,1152]{1,0:T(8,128)(2,1)S(1)}, u32[]{:S(2)}, u32[]{:S(2)}) collective-permute-start(bf16[192,1152]{1,0:T(8,128)(2,1)S(1)} %maximum_bitcast_fusion.refs_0_), channel_id=1, source_target_pairs={{0,1},{1,0},{2,3},{3,2},{4,5},{5,4},{6,7},{7,6},{8,9},{9,8},{10,11... | collective-permute-start | bytes 1327112 | tf_op jit(solution)/shard_map/ppermute | solution.py:572
  316.5 14.1 %collective-permute-start.27 = (bf16[1,576,256]{2,1,0:T(8,128)(2,1)S(1)}, bf16[1,576,256]{2,1,0:T(8,128)(2,1)S(1)}, u32[]{:S(2)}, u32[]{:S(2)}) collective-permute-start(bf16[1,576,256]{2,1,0:T(8,128)(2,1)S(1)} %get-tuple-element.229), channel_id=1, source_target_pairs={{0,16},{4,20},{8,24},{12,28},{16,0},{20,4},{24,8},{28,12},{1,17},{... | collective-permute-start | bytes 884744 | tf_op jit(solution)/shard_map/ppermute | solution.py:572
  316.7 15.2 %collective-permute-start.28 = (bf16[1,576,256]{2,1,0:T(8,128)(2,1)S(1)}, bf16[1,576,256]{2,1,0:T(8,128)(2,1)S(1)}, u32[]{:S(2)}, u32[]{:S(2)}) collective-permute-start(bf16[1,576,256]{2,1,0:T(8,128)(2,1)S(1)} %copy-done.34), channel_id=1, source_target_pairs={{0,8},{4,12},{8,0},{12,4},{16,24},{20,28},{24,16},{28,20},{1,9},{5... | collective-permute-start | bytes 884744 | tf_op jit(solution)/shard_map/ppermute | solution.py:572
  335.3 11.8 %collective-permute-start.31 = (bf16[192,1152]{1,0:T(8,128)(2,1)S(1)}, bf16[192,1152]{1,0:T(8,128)(2,1)S(1)}, u32[]{:S(2)}, u32[]{:S(2)}) collective-permute-start(bf16[192,1152]{1,0:T(8,128)(2,1)S(1)} %collective-permute-done.30.refs_2_), channel_id=1, source_target_pairs={{0,1},{1,0},{2,3},{3,2},{4,5},{5,4},{6,7},{7,6},{8,9},{9,8},{10,11... | collective-permute-start | bytes 1327112 | tf_op jit(solution)/shard_map/ppermute | solution.py:572
  (47 other events, 438.6 us)
Sparse Core Ops, SparseCore 0:
  9.9 55.1 all-gather.1
  178.8 154.7 reduce-scatter.1

commit v4 on v3

--- a/solution.py
+++ b/solution.py
@@ -21,10 +21,10 @@
 
 def expert_kernel(blocks, choices, where_ref, *refs):
     n2_refs, refs = refs[:blocks], refs[blocks:]
-    cot_refs, refs = refs[:blocks], refs[blocks:]
-    (router_ref, gate_ref, up_ref, down_ref,
+    pick_refs, refs = refs[:blocks], refs[blocks:]
+    (router_ref, gate_ref, up_ref, raw_ref,
      rows_ref, gates_ref, n2t_ref, hid_ref, weighed_ref, grow_ref, urow_ref,
-     n2, cot, rows, aux_ref) = refs
+     n2, rows, aux_ref) = refs
     e = pl.program_id(0)
     own = where_ref[0]
     experts_here = pl.num_programs(0)
@@ -35,8 +35,7 @@
     def _():
         for b in range(blocks):
             n2[b * T:(b + 1) * T, :] = n2_refs[b][...]
-            cot[b * T:(b + 1) * T, :] = cot_refs[b][:, :W]
-            picks = cot_refs[b][:, W:].astype(F32)
+            picks = pick_refs[b][...].astype(F32)
             logits = dot_nn(n2_refs[b][...], router_ref[...])
             lane = lax.broadcasted_iota(jnp.int32, logits.shape, 1)
             named = lane < 0
@@ -53,7 +52,7 @@
     g = column(gates_ref[...], mine)
     gate_pre = dot_nn(n2[...], gate_ref[0])
     up_pre = dot_nn(n2[...], up_ref[0])
-    raw_back = dot_nt(cot[...], down_ref[0])
+    raw_back = raw_ref[0]
     sig = 1.0 / (1.0 + jnp.exp(-gate_pre))
     silu = gate_pre * sig
     hidden = (silu * up_pre).astype(BF).astype(F32)
@@ -84,7 +83,7 @@
             rows_ref[own ^ b, :, W:] = packed[part, :]
 
 
-def expert_rows(where, n2s, cots, choices, router, gate_w, up_w, down_w):
+def expert_rows(where, n2s, payloads, choices, router, gate_w, up_w, raw):
     blocks = len(n2s)
     T, W = n2s[0].shape
     E, _, H = gate_w.shape
@@ -99,14 +98,14 @@
                    S((E, H, A), BF), S((E, A, H), BF), S((E, A, H), BF), S((E, A, H), BF)),
         grid_spec=pltpu.PrefetchScalarGridSpec(
             num_scalar_prefetch=1, grid=(E,),
-            in_specs=[once((T, W))] * blocks + [once((T, W + 128))] * blocks
-            + [once((W, 128)), per((W, H)), per((W, H)), per((H, W))],
+            in_specs=[once((T, W))] * blocks + [pl.BlockSpec((T, 128), lambda e, w: (0, W // 128), pipeline_mode=pl.Buffered(1))] * blocks
+            + [once((W, 128)), per((W, H)), per((W, H)), per((A, H))],
             out_specs=[whole((blocks, T, W + 128)), whole((A, 128)), whole((W, A)),
                        per((H, A)), per((A, H)), per((A, H)), per((A, H))],
-            scratch_shapes=[pltpu.VMEM((A, W), BF), pltpu.VMEM((A, W), BF), pltpu.VMEM((A, W), F32), pltpu.VMEM((A, 128), F32)]),
+            scratch_shapes=[pltpu.VMEM((A, W), BF), pltpu.VMEM((A, W), F32), pltpu.VMEM((A, 128), F32)]),
         compiler_params=pltpu.CompilerParams(vmem_limit_bytes=60 << 20),
-        cost_estimate=pl.CostEstimate(flops=10 * A * W * H * E, bytes_accessed=6 * E * W * H + 12 * A * W, transcendentals=A * H * E),
-    )(where, *n2s, *cots, router, gate_w, up_w, down_w)
+        cost_estimate=pl.CostEstimate(flops=8 * A * W * H * E, bytes_accessed=6 * E * W * H + 12 * A * W, transcendentals=A * H * E),
+    )(where, *n2s, *payloads, router, gate_w, up_w, raw)
 
 
 def grad_kernel(blocks, apart, where_ref, *refs):
@@ -160,25 +159,14 @@
     return made if apart else made[0]
 
 
-def combine_kernel(blocks, where_ref, weighed_ref, down_ref, gains_ref, *refs):
-    payloads, (comb_ref, n1t_ref, total) = refs[:blocks], refs[blocks:]
+def combine_kernel(weighed_ref, down_ref, keep_ref, send_ref, total):
     e = pl.program_id(0)
-    own, dev = where_ref[0], where_ref[1]
-    T = payloads[0].shape[0]
-    W = comb_ref.shape[2]
-    _, half, R, _ = n1t_ref.shape
+    half, T, _ = keep_ref.shape
     made = dot_nn(weighed_ref[0], down_ref[0])
 
     @pl.when(e == 0)
     def _():
         total[...] = made
-        for b in range(blocks):
-            x = payloads[b][:, W + 128:].astype(F32)
-            inverse = lax.rsqrt(jnp.mean(x * x, axis=1, keepdims=True) + EPSILON)
-            turned = (x * inverse * gains_ref[0:1, :]).astype(BF).T
-            for d in range(2 * half):
-                r = d ^ dev
-                n1t_ref[lax.rem(r, 2), lax.div(r, 2), :, b * T:(b + 1) * T] = turned[d * R:(d + 1) * R, :]
 
     @pl.when(e > 0)
     def _():
@@ -186,31 +174,85 @@
 
     @pl.when(e == pl.num_programs(0) - 1)
     def _():
-        for b in range(blocks):
-            comb_ref[own ^ b] = total[b * T:(b + 1) * T, :].astype(BF)
-
-
-def combine(where, weighed, down_w, gains, payloads, n_dp):
+        for b in range(2 * half):
+            out = send_ref if b % 2 else keep_ref
+            out[b // 2] = total[b * T:(b + 1) * T, :].astype(BF)
+
+
+def combine(weighed, down_w, blocks):
     E, A, H = weighed.shape
     W = down_w.shape[2]
-    blocks = len(payloads)
     T = A // blocks
-    R = W // n_dp
-    whole = lambda s: pl.BlockSpec(s, lambda e, w: (0,) * len(s))
-    once = lambda s: pl.BlockSpec(s, lambda e, w: (0,) * len(s), pipeline_mode=pl.Buffered(1))
-    per = lambda s: pl.BlockSpec((1,) + s, lambda e, w: (e,) + (0,) * len(s))
-    S = jax.ShapeDtypeStruct
-    return pl.pallas_call(
-        functools.partial(combine_kernel, blocks),
-        out_shape=(S((blocks, T, W), BF), S((2, n_dp // 2, R, A), BF)),
-        grid_spec=pltpu.PrefetchScalarGridSpec(
-            num_scalar_prefetch=1, grid=(E,),
-            in_specs=[per((A, H)), per((H, W)), once((8, W))] + [once((T, 2 * W + 128))] * blocks,
-            out_specs=[whole((blocks, T, W)), whole((2, n_dp // 2, R, A))],
-            scratch_shapes=[pltpu.VMEM((A, W), F32)]),
+    per = lambda s: pl.BlockSpec((1,) + s, lambda e: (e,) + (0,) * len(s))
+    out = pl.BlockSpec((blocks // 2, T, W), lambda e: (0, 0, 0))
+    return pl.pallas_call(
+        combine_kernel,
+        out_shape=(jax.ShapeDtypeStruct((blocks // 2, T, W), BF),) * 2,
+        grid=(E,),
+        in_specs=[per((A, H)), per((H, W))],
+        out_specs=(out, out),
+        scratch_shapes=[pltpu.VMEM((A, W), F32)],
         compiler_params=pltpu.CompilerParams(vmem_limit_bytes=60 << 20),
         cost_estimate=pl.CostEstimate(flops=0, bytes_accessed=0, transcendentals=0),
-    )(where, weighed, down_w, gains, *payloads)
+    )(weighed, down_w)
+
+
+def raw_kernel(blocks, *refs):
+    payloads, (down_ref, out_ref, cot) = refs[:blocks], refs[blocks:]
+    T = payloads[0].shape[0]
+
+    @pl.when(pl.program_id(0) == 0)
+    def _():
+        for b in range(blocks):
+            cot[b * T:(b + 1) * T, :] = payloads[b][...]
+
+    out_ref[0] = dot_nt(cot[...], down_ref[0])
+
+
+def raw_back(payloads, down_w):
+    blocks = len(payloads)
+    T = payloads[0].shape[0]
+    E, H, W = down_w.shape
+    A = blocks * T
+    return pl.pallas_call(
+        functools.partial(raw_kernel, blocks),
+        grid=(E,),
+        out_shape=jax.ShapeDtypeStruct((E, A, H), F32),
+        in_specs=[pl.BlockSpec((T, W), lambda e: (0, 0), pipeline_mode=pl.Buffered(1))] * blocks
+        + [pl.BlockSpec((1, H, W), lambda e: (e, 0, 0))],
+        out_specs=pl.BlockSpec((1, A, H), lambda e: (e, 0, 0)),
+        scratch_shapes=[pltpu.VMEM((A, W), BF)],
+        compiler_params=pltpu.CompilerParams(vmem_limit_bytes=60 << 20),
+        cost_estimate=pl.CostEstimate(flops=0, bytes_accessed=0, transcendentals=0),
+    )(*payloads, down_w)
+
+
+def normed_kernel(where_ref, gains_ref, *refs):
+    payloads, out_ref = refs[:-1], refs[-1]
+    T = payloads[0].shape[0]
+    W = gains_ref.shape[1]
+    _, half, R, _ = out_ref.shape
+    for b, ref in enumerate(payloads):
+        x = ref[:, W + 128:].astype(F32)
+        inverse = lax.rsqrt(jnp.mean(x * x, axis=1, keepdims=True) + EPSILON)
+        turned = (x * inverse * gains_ref[0:1, :]).astype(BF).T
+        for d in range(2 * half):
+            r = d ^ where_ref[1]
+            out_ref[lax.rem(r, 2), lax.div(r, 2), :, b * T:(b + 1) * T] = turned[d * R:(d + 1) * R, :]
+
+
+def normed_turned(where, gains, payloads, n_dp):
+    T = payloads[0].shape[0]
+    W = gains.shape[1]
+    v = pl.BlockSpec(memory_space=pltpu.VMEM)
+    return pl.pallas_call(
+        normed_kernel,
+        out_shape=jax.ShapeDtypeStruct((2, n_dp // 2, W // n_dp, len(payloads) * T), BF),
+        in_specs=[pl.BlockSpec(memory_space=pltpu.SMEM)] + [v] * (1 + len(payloads)),
+        out_specs=v,
+        compiler_params=pltpu.CompilerParams(vmem_limit_bytes=40 << 20),
+        cost_estimate=pl.CostEstimate(flops=0, bytes_accessed=0, transcendentals=0),
+    )(where, gains, *payloads)
 
 
 def rope_tile(x, cosine, sine):
@@ -731,10 +773,6 @@
     return end_z(begin_z(x, ne), ne)
 
 
-def direct_z(x, ne):
-    return [x] + [flip(x, "expert", bit, ne) for bit in range(1, ne)]
-
-
 def gather_dp(w, n_dp, ready):
     half = w.shape[1] // 256 * 128
     found = {(0, 0): w[:, :half], (0, half): w[:, half:]}
@@ -797,10 +835,12 @@
     payloads, pieces, q_full = tie((payloads, pieces, q_full))
     qkv, mixed, resid, normed2, gains, router, kv_full = forward(
         where, tokens, cosine, sine, segr, segc, q_full, pieces, places, KV, experts)
-    n2s = gather_z(normed2, ne)
-    n2s, mixed = tie((n2s, mixed))
-    mixs = direct_z(mixed, ne)
-    made = expert_rows(where, n2s, payloads, choices, router, gate_weight, up_weight, down_weight)
+    raw = raw_back(payloads, down_weight)
+    n1t = normed_turned(where, gains, payloads, n_dp)
+    n2s, raw, n1t = tie((begin_z(normed2, ne), raw, n1t))
+    n2s, mixed = tie((end_z(n2s, ne), mixed))
+    mixs = begin_z(mixed, ne)
+    made = expert_rows(where, n2s, payloads, choices, router, gate_weight, up_weight, raw)
     made, mixs = tie((made, mixs))
     rows, gates, n2t, hid, weighed, grow, urow = made
     rows = exchange(rows)
@@ -808,32 +848,39 @@
     packed = lax.psum_scatter(partial, "dp", scatter_dimension=0, tiled=True)
     partial, n2t, weighed = tie((partial, n2t, weighed))
     few, away = expert_grads(MANY, E - MANY, True, where, payloads, n2t, hid, grow, urow, n_dp)
-    comb, n1t = combine(where, weighed, down_weight, gains, payloads, n_dp)
-    rows, few, away, comb, n1t = tie((rows, few, away, comb, n1t))
+    comb, comb_away = combine(weighed, down_weight, ne)
+    rows, few, away, comb, comb_away, mixs = tie((rows, few, away, comb, comb_away, mixs))
+    mixs = end_z(mixs, ne)
+    comb_in = flip(comb_away, "expert", 1, ne)
     theirs = core(away)
     attended, att_cut, resid_back, extra = middle(rows, gates, router, normed2, resid, gains, cotangent, experts)
     att_cut = exchange(att_cut)
     back, back_cut = backward(where, attended, qkv, cosine, sine, segr, segc, pieces, places, ne)
-    att_cut, back, back_cut, few, theirs = tie((att_cut, back, back_cut, few, theirs))
+    att_cut, back, back_cut, few, theirs, comb_in = tie((att_cut, back, back_cut, few, theirs, comb_in))
     back_cut = exchange(back_cut)
-    few = halve(halves([(few, theirs)], n_dp, (d // 2).reshape(1)), n_dp)
+    few = halves([(few, theirs)], n_dp, (d // 2).reshape(1))
     input_grad, extra = last(back, tokens, gains, resid_back, extra, q_full, kv_full, experts)
     keep4, send4 = out_grads(where, mixs, att_cut, n_dp)
-    few, back_cut, extra, keep4, send4, comb = tie_parts(few, back_cut, extra, keep4, send4, comb)
+    comb = comb.astype(F32) + comb_in.astype(F32)
+    comb, comb_far = comb[0], comb[1:].astype(BF)
+    few, back_cut, extra, keep4, send4, comb_far = tie_parts(few, back_cut, extra, keep4, send4, comb_far)
+    comb_far = [flip(comb_far[i], "expert", 2 * (i + 1), ne) for i in range(ne // 2 - 1)]
     theirs4 = core(send4)
+    keep5, send5 = qkv_grads(where, n1t, back_cut, extra, n_dp)
+    keep5, send5, theirs4 = tie((keep5, send5, theirs4))
+    five = halve(halves([(keep4, theirs4), (keep5, core(send5))], n_dp), n_dp)
+    five, comb_far = tie_parts(five, comb_far)
+    five = finish(five, n_dp)
+    part = jnp.concatenate([mine.astype(F32) + theirs.astype(F32) for mine, theirs, *_ in five], axis=-1)[0].astype(BF)
+    few, part = tie_parts(few, part)
+    parts = begin_z(part, ne)
+    few, parts = tie_parts(halve(few, n_dp), parts)
+    parts = end_z(parts, ne)
     few = finish(few, n_dp)
-    keep5, send5 = qkv_grads(where, n1t, back_cut, extra, n_dp)
-    keep5, send5, theirs4, comb = tie((keep5, send5, theirs4, comb))
-    comb = exchange(comb)
-    five = finish(halves([(keep4, theirs4), (keep5, core(send5))], n_dp), n_dp)
-    part = jnp.concatenate([mine.astype(F32) + theirs.astype(F32) for mine, theirs, *_ in five], axis=-1)[0].astype(BF)
-    part, comb = tie((part, comb))
-    parts = begin_z(part, ne)
-    few, parts = tie_parts(few, parts)
-    parts = end_z(parts, ne)
+    made = unpack(packed, [x for p in few for x in p[:2]], R, D, W)
+    parts, (gate_grad, up_grad, down_grad) = tie((parts, made))
     query_grad, key_grad, value_grad, out_grad, extra = spread(where, parts, W, KV)
-    layer_out = (resid + jnp.sum(comb.astype(F32), axis=0)).astype(BF)
-    gate_grad, up_grad, down_grad = unpack(packed, [x for p in few for x in p[:2]], R, D, W)
+    layer_out = (resid + comb + sum(x.astype(F32) for x in comb_far)).astype(BF)
     return (layer_out, input_grad, query_grad, key_grad, value_grad, out_grad, extra[:, experts + 1], extra[:, experts],
             extra[:, :experts], gate_grad, up_grad, down_grad)
 

time: 364 us -> 349 us (0.959)
  waiting for transfers between devices: 141 us -> 124 us
    ppermute x32 -> x34, waiting for transfers between devices: 133 us -> 119 us  [flip(): return lax.ppermute(x, axis, [(i, i ^ mask) for i in range(size)])]
    ppermute x32 -> x34, starting transfers between devices: 29.5 us -> 38.8 us  [flip(): return lax.ppermute(x, axis, [(i, i ^ mask) for i in range(size)])]
    all_to_all x4 -> x3, starting transfers between devices: 18.7 us -> 11.5 us  [local(): lax.all_to_all(x, 'expert', split_axis=0, concat_axis=0, tiled=True)]
    pallas_call x1 -> x3, Pallas kernels: 15.1 us -> 21.9 us  [the longest x1 11 us: combine(): pl.pallas_call(combine_kernel, out_shape=(jax.ShapeDtypeStruct((blocks //...]
    pallas_call x1, Pallas kernels: 32.4 us -> 27.7 us  [expert_rows(): pl.pallas_call(functools.partial(expert_kernel, blocks, choices), out_sha...]
    all_to_all x4 -> x3, waiting for transfers between devices: 7.4 us -> 4.19 us  [local(): lax.all_to_all(x, 'expert', split_axis=0, concat_axis=0, tiled=True)]
    unnamed x84 -> x96, local copies, waits for them, and re-layouts: 22.6 us -> 19.6 us
  transfers between devices with their start and end apart: 38 -> 39, of which waited for: 22 -> 21; matrix products, arithmetic and copies ran while one was open for 5% -> 5% of each run, Pallas kernels for 29% -> 31%
where the time goes in v4:
time: 349 us; the launch traced here: 348 us
  waiting for transfers between devices  124 us (36%)
  Pallas kernels  121 us (35%)
  starting transfers between devices  50.4 us (14%)
  local copies, waits for them, and re-layouts  31.8 us (9%)
  between operations  14.7 us (4%)
  other arithmetic  6.34 us (2%)
    ppermute x34, waiting for transfers between devices, flip(): return lax.ppermute(x, axis, [(i, i ^ mask) for i in range(size)])  119 us
    ppermute x34, starting transfers between devices, flip(): return lax.ppermute(x, axis, [(i, i ^ mask) for i in range(size)])  38.8 us
    pallas_call x1, Pallas kernels, expert_rows(): pl.pallas_call(functools.partial(expert_kernel, blocks, choices), out_sha...  27.7 us
    pallas_call x2, Pallas kernels, expert_grads(): pl.pallas_call(functools.partial(grad_kernel, blocks, apart), out_shape=(...  25.5 us
    unnamed x96, local copies, waits for them, and re-layouts  19.6 us
    all_to_all x3, starting transfers between devices, local(): lax.all_to_all(x, 'expert', split_axis=0, concat_axis=0, tiled=True)  11.5 us
    pallas_call x1, Pallas kernels, forward(): pl.pallas_call(functools.partial(forward_kernel, places, kv, experts), ou...  11.3 us
    pallas_call x1, Pallas kernels, backward(): pl.pallas_call(functools.partial(backward_kernel, places), out_shape=(S((...  11.1 us
  transfers between devices with their start and end apart: 39, of which 21 were waited for; matrix products, arithmetic and copies ran while one was open for 5% of the time, Pallas kernels for 31%

profile of v4, /device:TPU:0, one launch (start us, length us, event | category | flops | bytes accessed | tf_op | source)
XLA Modules:
  0.0 347.8 jit_solution(3575175428789060725)
XLA Ops:
  12.6 3.0 collective-permute-start.1
  26.5 21.1 %collective-permute-done.1.refs_4_ = bf16[192,2688]{1,0:T(8,128)(2,1)} collective-permute-done((bf16[192,2688]{1,0:T(8,128)(2,1)S(1)}, bf16[192,2688]{1,0:T(8,128)(2,1)}, u32[]{:S(2)}, u32[]{:S(2)}) %collective-permute-start.1) | collective-permute-done | bytes 1032224 | tf_op jit(solution)/shard_map/ppermute | solution.py:614
  47.5 2.7 collective-permute-done.refs_2_
  52.1 3.2 collective-permute-done.3.refs_2_.refs_6_
  58.1 9.9 %collective-permute-done.8.refs_6_ = bf16[192,1280]{1,0:T(8,128)(2,1)} collective-permute-done((bf16[192,1280]{1,0:T(8,128)(2,1)S(1)}, bf16[192,1280]{1,0:T(8,128)(2,1)}, u32[]{:S(2)}, u32[]{:S(2)}) %collective-permute-start.8) | collective-permute-done | bytes 491552 | tf_op jit(solution)/shard_map/ppermute | solution.py:614
  68.0 3.1 collective-permute-done.9.refs_7_
  71.1 3.3 collective-permute-done.4.refs_3_.refs_7_
  76.7 11.3 %shard_map.229 = (bf16[128,2560]{1,0:T(8,128)(2,1)}, bf16[128,1536]{1,0:T(8,128)(2,1)}, f32[128,1536]{1,0:T(8,128)}, bf16[128,1536]{1,0:T(8,128)(2,1)}, f32[8,15...) custom-call(s32[4]{0:T(128)} %pad_add_fusion.dev_ref.where_ref, bf16[128,1536]{1,0:T(8,128)(2,1)} %tok_ref.3, ...), custom_call_target="tpu_custom_call" | custom-call | tf_op jit(solution)/shard_map/pallas_call | solution.py:379
  88.1 3.4 collective-permute-start.13
  93.3 9.6 %shard_map.230.refs_11_ = f32[5,512,512]{2,1,0:T(8,128)} custom-call(bf16[128,3200]{1,0:T(8,128)(2,1)} %copy-done, bf16[128,3200]{1,0:T(8,128)(2,1)} %copy-done.5, bf16[128,3200]{1,0:T(8,128)(2,1)} %copy-done.3, bf16[128,3200]{1,0:T(8,128)(2,1)} %copy-done.7, bf16[5,512,1536]{2,1,0:T(8,128)(2,1)} %down_ref.1), custom_call_target="tpu_custom_call" | custom-call | tf_op jit(solution)/shard_map/pallas_call | solution.py:217
  105.4 4.6 %collective-permute-done.13.refs_2_ = bf16[128,1536]{1,0:T(8,128)(2,1)} collective-permute-done((bf16[128,1536]{1,0:T(8,128)(2,1)}, bf16[128,1536]{1,0:T(8,128)(2,1)}, u32[]{:S(2)}, u32[]{:S(2)}) %collective-permute-start.13) | collective-permute-done | bytes 393248 | tf_op jit(solution)/shard_map/ppermute | solution.py:614
  111.7 9.3 %collective-permute-done.14.refs_3_ = bf16[128,1536]{1,0:T(8,128)(2,1)S(1)} collective-permute-done((bf16[128,1536]{1,0:T(8,128)(2,1)}, bf16[128,1536]{1,0:T(8,128)(2,1)S(1)}, u32[]{:S(2)}, u32[]{:S(2)}) %collective-permute-start.14) | collective-permute-done | bytes 393248 | tf_op jit(solution)/shard_map/ppermute | solution.py:614
  125.3 27.7 %shard_map.232 = (bf16[4,128,1664]{2,1,0:T(8,128)(2,1)}, f32[512,128]{1,0:T(8,128)}, bf16[1536,512]{1,0:T(8,128)(2,1)}, bf16[5,512,512]{2,1,0:T(8,128)(2,1)}, bf...) custom-call(s32[4]{0:T(128)} %pad_add_fusion.dev_ref.where_ref, ...), custom_call_target="tpu_custom_call" | custom-call | flops 16106127360 | bytes 33030144 | tf_op jit(solution)/shard_map/pallas_call | solution.py:95
  153.8 3.6 %all-to-all-start = ((bf16[4,128,1664]{2,1,0:T(8,128)(2,1)}), bf16[4,128,1664]{2,1,0:T(8,128)(2,1)S(1)}, u32[]{:S(2)}, u32[]{:S(2)}) async-start(bf16[4,128,1664]{2,1,0:T(8,128)(2,1)} %get-tuple-element.195), calls=%async_computation | async-start | bytes 3407872 | tf_op jit(solution)/shard_map/all_to_all | solution.py:834
  157.4 16.0 %shard_map.233 = bf16[8,4,576,512]{3,2,1,0:T(8,128)(2,1)} custom-call(s32[4]{0:T(128)} %pad_add_fusion.dev_ref.where_ref, bf16[128,3200]{1,0:T(8,128)(2,1)} %copy-done, bf16[128,3200]{1,0:T(8,128)(2,1)} %copy-done.5, bf16[128,3200]{1,0:T(8,128)(2,1)} %copy-done.3, bf16[128,3200]{1,0:T(8,128)(2,1)} %copy-done.7, ...), custom_call_target="tpu_custom_call" | custom-call | tf_op jit(solution)/shard_map/pallas_call | solution.py:149
  173.5 9.5 %shard_map.234 = (bf16[4,1,576,512]{3,2,1,0:T(8,128)(2,1)}, bf16[4,1,576,512]{3,2,1,0:T(8,128)(2,1)}) custom-call(s32[4]{0:T(128)} %pad_add_fusion.dev_ref.where_ref, bf16[128,3200]{1,0:T(8,128)(2,1)} %copy-done, bf16[128,3200]{1,0:T(8,128)(2,1)} %copy-done.5, bf16[128,3200]{1,0:T(8,128)(2,1)} %copy-done.3, bf16[128,3200]{1,0:T(8,128)(2,1)} %copy-done.7, ...), custom_call_target="tpu_custom_call" | custom-call | tf_op jit(solution)/shard_map/pallas_call | solution.py:149
  182.9 11.0 %shard_map.235 = (bf16[2,128,1536]{2,1,0:T(8,128)(2,1)}, bf16[2,128,1536]{2,1,0:T(8,128)(2,1)}) custom-call(bf16[5,512,512]{2,1,0:T(8,128)(2,1)} %get-tuple-element.204.weighed_ref, bf16[5,512,1536]{2,1,0:T(8,128)(2,1)} %down_ref.1), custom_call_target="tpu_custom_call" | custom-call | tf_op jit(solution)/shard_map/pallas_call | solution.py:188
  204.4 3.7 %all-to-all-start.1 = ((bf16[4,128,384]{2,1,0:T(8,128)(2,1)}), bf16[4,128,384]{2,1,0:T(8,128)(2,1)S(1)}, u32[]{:S(2)}, u32[]{:S(2)}) async-start(bf16[4,128,384]{2,1,0:T(8,128)(2,1)} %copy-done.21), calls=%async_computation.1 | async-start | bytes 786432 | tf_op jit(solution)/shard_map/all_to_all | solution.py:834
  208.1 11.1 %shard_map.237 = (bf16[128,2560]{1,0:T(8,128)(2,1)}, bf16[4,128,640]{2,1,0:T(8,128)(2,1)}) custom-call(s32[4]{0:T(128)} %pad_add_fusion.dev_ref.where_ref, bf16[128,1536]{1,0:T(8,128)(2,1)} %copy-done.20, bf16[128,2560]{1,0:T(8,128)(2,1)} %get-tuple-element.215.qkv_ref, f32[128,128]{1,0:T(8,128)} %copy.57.cos_ref, f32[128,128]{1,0:T(8,128)} %pad_maximum_fusion.sin_ref, ...), custom_call_target="tpu_custom_call" | custom-call | tf_op jit(solution)/shard_map/pallas_call | solution.py:494
  221.2 4.2 %all-to-all-start.2 = ((bf16[4,128,640]{2,1,0:T(8,128)(2,1)}), bf16[4,128,640]{2,1,0:T(8,128)(2,1)}, u32[]{:S(2)}, u32[]{:S(2)}) async-start(bf16[4,128,640]{2,1,0:T(8,128)(2,1)} %get-tuple-element.228), calls=%async_computation.2 | async-start | bytes 1310720 | tf_op jit(solution)/shard_map/all_to_all | solution.py:834
  236.6 4.4 %shard_map.239 = (f32[128,1536]{1,0:T(8,128)}, f32[1536,128]{1,0:T(8,128)S(1)}) custom-call(bf16[128,2560]{1,0:T(8,128)(2,1)S(1)} %copy-done.18, bf16[128,1536]{1,0:T(8,128)(2,1)S(1)} %copy-done.10, f32[8,1536]{1,0:T(8,128)S(1)} %copy-done.24, f32[128,1536]{1,0:T(8,128)S(1)} %get-tuple-element.230.resid_back_ref, ...), custom_call_target="tpu_custom_call" | custom-call | tf_op jit(solution)/shard_map/pallas_call | solution.py:530
  241.9 4.3 %collective-permute-done.19.refs_3_ = bf16[128,1536]{1,0:T(8,128)(2,1)S(1)} collective-permute-done((bf16[128,1536]{1,0:T(8,128)(2,1)}, bf16[128,1536]{1,0:T(8,128)(2,1)S(1)}, u32[]{:S(2)}, u32[]{:S(2)}) %collective-permute-start.19) | collective-permute-done | bytes 393248 | tf_op jit(solution)/shard_map/ppermute | solution.py:614
  246.9 3.7 %shard_map.240 = (bf16[4,1,192,384]{3,2,1,0:T(8,128)(2,1)}, bf16[4,1,192,384]{3,2,1,0:T(8,128)(2,1)}) custom-call(s32[4]{0:T(128)} %pad_add_fusion.dev_ref.where_ref, bf16[128,1536]{1,0:T(8,128)(2,1)} %get-tuple-element.234.refs_0_, bf16[128,1536]{1,0:T(8,128)(2,1)} %copy-done.42, bf16[128,1536]{1,0:T(8,128)(2,1)} %collective-permute-done.16.refs_2_, ...), custom_call_target="tpu_custom_call" | custom-call | tf_op jit(solution)/shard_map/pallas_call | solution.py:565
  250.7 5.4 %shard_map.241 = (bf16[4,1,192,768]{3,2,1,0:T(8,128)(2,1)}, bf16[4,1,192,768]{3,2,1,0:T(8,128)(2,1)}) custom-call(s32[4]{0:T(128)} %pad_add_fusion.dev_ref.where_ref, bf16[2,4,192,512]{3,2,1,0:T(8,128)(2,1)} %copy-done.14, bf16[4,128,640]{2,1,0:T(8,128)(2,1)} %all-to-all-done.2.qkv_ref, f32[1536,128]{1,0:T(8,128)} %copy-done.27), custom_call_target="tpu_custom_call" | custom-call | flops 1207959552 | bytes 4718592 | tf_op jit(solution)/shard_map/pallas_call | solution.py:603
  256.3 2.8 collective-permute-done.21.refs_3_
  264.8 9.5 %collective-permute-done.22 = bf16[2,1,192,512]{3,2,1,0:T(8,128)(2,1)S(1)} collective-permute-done((bf16[2,1,192,512]{3,2,1,0:T(8,128)(2,1)S(1)}, bf16[2,1,192,512]{3,2,1,0:T(8,128)(2,1)S(1)}, u32[]{:S(2)}, u32[]{:S(2)}) %collective-permute-start.22) | collective-permute-done | bytes 393248 | tf_op jit(solution)/shard_map/ppermute | solution.py:614
  277.1 4.8 %collective-permute-done.24 = bf16[128,1536]{1,0:T(8,128)(2,1)S(1)} collective-permute-done((bf16[128,1536]{1,0:T(8,128)(2,1)S(1)}, bf16[128,1536]{1,0:T(8,128)(2,1)S(1)}, u32[]{:S(2)}, u32[]{:S(2)}) %collective-permute-start.24) | collective-permute-done | bytes 393248 | tf_op jit(solution)/shard_map/ppermute | solution.py:614
  283.6 9.9 %collective-permute-done.25 = bf16[1,192,512]{2,1,0:T(8,128)(2,1)S(1)} collective-permute-done((bf16[1,192,512]{2,1,0:T(8,128)(2,1)S(1)}, bf16[1,192,512]{2,1,0:T(8,128)(2,1)S(1)}, u32[]{:S(2)}, u32[]{:S(2)}) %collective-permute-start.25) | collective-permute-done | bytes 196640 | tf_op jit(solution)/shard_map/ppermute | solution.py:614
  299.0 3.0 collective-permute-start.29
  301.9 20.1 %collective-permute-done.27 = bf16[2,1,576,256]{3,2,1,0:T(8,128)(2,1)S(1)} collective-permute-done((bf16[2,1,576,256]{3,2,1,0:T(8,128)(2,1)S(1)}, bf16[2,1,576,256]{3,2,1,0:T(8,128)(2,1)S(1)}, u32[]{:S(2)}, u32[]{:S(2)}) %collective-permute-start.27) | collective-permute-done | bytes 589856 | tf_op jit(solution)/shard_map/ppermute | solution.py:614
  326.9 4.0 %collective-permute-done.32.refs_1_ = bf16[1,576,256]{2,1,0:T(8,128)(2,1)S(1)} collective-permute-done((bf16[1,576,256]{2,1,0:T(8,128)(2,1)S(1)}, bf16[1,576,256]{2,1,0:T(8,128)(2,1)S(1)}, u32[]{:S(2)}, u32[]{:S(2)}) %collective-permute-start.32) | collective-permute-done | bytes 294944 | tf_op jit(solution)/shard_map/ppermute | solution.py:614
  333.7 3.3 shard_map.243
  (194 shorter events, 86.8 us)
Async XLA Ops:
  7.2 69.5 %all-gather.2.cloned.1.call-start = ((), (), s32[]{:S(2)}) async-start(), calls=%async_computation.4 | async-start | bytes 5308416 | tf_op jit(solution)/shard_map/all_gather | solution.py:817
  12.6 35.0 %collective-permute-start.1 = (bf16[192,2688]{1,0:T(8,128)(2,1)S(1)}, bf16[192,2688]{1,0:T(8,128)(2,1)}, u32[]{:S(2)}, u32[]{:S(2)}) collective-permute-start(bf16[192,2688]{1,0:T(8,128)(2,1)S(1)} %concatenate.13.refs_0_), channel_id=1, source_target_pairs={{0,16},{4,20},{8,24},{12,28},{16,0},{20,4},{24,8},{28,12},{1,17},{... | collective-permute-start | bytes 3096584 | tf_op jit(solution)/shard_map/ppermute | solution.py:614
  15.6 34.7 %collective-permute-start = (bf16[192,2688]{1,0:T(8,128)(2,1)S(1)}, bf16[192,2688]{1,0:T(8,128)(2,1)}, u32[]{:S(2)}, u32[]{:S(2)}) collective-permute-start(bf16[192,2688]{1,0:T(8,128)(2,1)S(1)} %concatenate.13.refs_0_), channel_id=1, source_target_pairs={{0,8},{4,12},{8,0},{12,4},{16,24},{20,28},{24,16},{28,20},{1,9},{5... | collective-permute-start | bytes 3096584 | tf_op jit(solution)/shard_map/ppermute | solution.py:614
  17.3 38.0 %collective-permute-start.3 = (bf16[128,3200]{1,0:T(8,128)(2,1)S(1)}, bf16[128,3200]{1,0:T(8,128)(2,1)S(1)}, u32[]{:S(2)}, u32[]{:S(2)}) collective-permute-start(bf16[128,3200]{1,0:T(8,128)(2,1)S(1)} %fusion.3.refs_0_.refs_4_), channel_id=1, source_target_pairs={{0,2},{1,3},{2,0},{3,1},{4,6},{5,7},{6,4},{7,5},{8,10},{9,11},{10,... | collective-permute-start | bytes 2457608 | tf_op jit(solution)/shard_map/ppermute | solution.py:614
  20.0 37.7 %collective-permute-start.2 = (bf16[128,3200]{1,0:T(8,128)(2,1)S(1)}, bf16[128,3200]{1,0:T(8,128)(2,1)S(1)}, u32[]{:S(2)}, u32[]{:S(2)}) collective-permute-start(bf16[128,3200]{1,0:T(8,128)(2,1)S(1)} %fusion.3.refs_0_.refs_4_), channel_id=1, source_target_pairs={{0,1},{1,0},{2,3},{3,2},{4,5},{5,4},{6,7},{7,6},{8,9},{9,8},{10,11... | collective-permute-start | bytes 2457608 | tf_op jit(solution)/shard_map/ppermute | solution.py:614
  52.0 16.0 %collective-permute-start.8 = (bf16[192,1280]{1,0:T(8,128)(2,1)S(1)}, bf16[192,1280]{1,0:T(8,128)(2,1)}, u32[]{:S(2)}, u32[]{:S(2)}) collective-permute-start(bf16[192,1280]{1,0:T(8,128)(2,1)S(1)} %slice.46), channel_id=1, source_target_pairs={{0,16},{4,20},{8,24},{12,28},{16,0},{20,4},{24,8},{28,12},{1,17},{... | collective-permute-start | bytes 1474568 | tf_op jit(solution)/shard_map/ppermute | solution.py:614
  55.4 19.0 %collective-permute-start.4 = (bf16[128,3200]{1,0:T(8,128)(2,1)S(1)}, bf16[128,3200]{1,0:T(8,128)(2,1)S(1)}, u32[]{:S(2)}, u32[]{:S(2)}) collective-permute-start(bf16[128,3200]{1,0:T(8,128)(2,1)S(1)} %collective-permute-done.3.refs_2_.refs_6_), channel_id=1, source_target_pairs={{0,1},{1,0},{2,3},{3,2},{4,5},{5,4},{6,7},{7,6},{8,9},{9,8},{10,11... | collective-permute-start | bytes 2457608 | tf_op jit(solution)/shard_map/ppermute | solution.py:614
  57.0 14.1 %collective-permute-start.9 = (bf16[192,1408]{1,0:T(8,128)(2,1)S(1)}, bf16[192,1408]{1,0:T(8,128)(2,1)}, u32[]{:S(2)}, u32[]{:S(2)}) collective-permute-start(bf16[192,1408]{1,0:T(8,128)(2,1)S(1)} %slice.47), channel_id=1, source_target_pairs={{0,8},{4,12},{8,0},{12,4},{16,24},{20,28},{24,16},{28,20},{1,9},{5... | collective-permute-start | bytes 1622024 | tf_op jit(solution)/shard_map/ppermute | solution.py:614
  57.6 19.0 %collective-permute-start.6 = (bf16[192,2688]{1,0:T(8,128)(2,1)}, bf16[192,2688]{1,0:T(8,128)(2,1)}, u32[]{:S(2)}, u32[]{:S(2)}) collective-permute-start(bf16[192,2688]{1,0:T(8,128)(2,1)} %collective-permute-done.refs_2_), channel_id=1, source_target_pairs={{0,4},{4,0},{8,12},{12,8},{16,20},{20,16},{24,28},{28,24},{1,5},{5... | collective-permute-start | bytes 3096584 | tf_op jit(solution)/shard_map/ppermute | solution.py:614
  57.6 19.0 %collective-permute-start.5 = (bf16[192,2688]{1,0:T(8,128)(2,1)}, bf16[192,2688]{1,0:T(8,128)(2,1)}, u32[]{:S(2)}, u32[]{:S(2)}) collective-permute-start(bf16[192,2688]{1,0:T(8,128)(2,1)} %copy-done.35), channel_id=1, source_target_pairs={{0,4},{4,0},{8,12},{12,8},{16,20},{20,16},{24,28},{28,24},{1,5},{5... | collective-permute-start | bytes 3096584 | tf_op jit(solution)/shard_map/ppermute | solution.py:614
  88.1 21.9 %collective-permute-start.13 = (bf16[128,1536]{1,0:T(8,128)(2,1)}, bf16[128,1536]{1,0:T(8,128)(2,1)}, u32[]{:S(2)}, u32[]{:S(2)}) collective-permute-start(bf16[128,1536]{1,0:T(8,128)(2,1)} %get-tuple-element.181.refs_0_.refs_3_), channel_id=1, source_target_pairs={{0,2},{1,3},{2,0},{3,1},{4,6},{5,7},{6,4},{7,5},{8,10},{9,11},{10,... | collective-permute-start | bytes 1179656 | tf_op jit(solution)/shard_map/ppermute | solution.py:614
  91.6 18.6 %collective-permute-start.12 = (bf16[128,1536]{1,0:T(8,128)(2,1)}, bf16[128,1536]{1,0:T(8,128)(2,1)}, u32[]{:S(2)}, u32[]{:S(2)}) collective-permute-start(bf16[128,1536]{1,0:T(8,128)(2,1)} %get-tuple-element.181.refs_0_.refs_3_), channel_id=1, source_target_pairs={{0,1},{1,0},{2,3},{3,2},{4,5},{5,4},{6,7},{7,6},{8,9},{9,8},{10,11... | collective-permute-start | bytes 1179656 | tf_op jit(solution)/shard_map/ppermute | solution.py:614
  110.2 10.9 %collective-permute-start.14 = (bf16[128,1536]{1,0:T(8,128)(2,1)}, bf16[128,1536]{1,0:T(8,128)(2,1)S(1)}, u32[]{:S(2)}, u32[]{:S(2)}) collective-permute-start(bf16[128,1536]{1,0:T(8,128)(2,1)} %collective-permute-done.13.refs_2_), channel_id=1, source_target_pairs={{0,1},{1,0},{2,3},{3,2},{4,5},{5,4},{6,7},{7,6},{8,9},{9,8},{10,11... | collective-permute-start | bytes 1179656 | tf_op jit(solution)/shard_map/ppermute | solution.py:614
  121.0 32.0 %collective-permute-start.16 = (bf16[128,1536]{1,0:T(8,128)(2,1)S(1)}, bf16[128,1536]{1,0:T(8,128)(2,1)}, u32[]{:S(2)}, u32[]{:S(2)}) collective-permute-start(bf16[128,1536]{1,0:T(8,128)(2,1)S(1)} %copy-done.41), channel_id=1, source_target_pairs={{0,2},{1,3},{2,0},{3,1},{4,6},{5,7},{6,4},{7,5},{8,10},{9,11},{10,... | collective-permute-start | bytes 1179656 | tf_op jit(solution)/shard_map/ppermute | solution.py:614
  123.6 29.4 %collective-permute-start.15 = (bf16[128,1536]{1,0:T(8,128)(2,1)S(1)}, bf16[128,1536]{1,0:T(8,128)(2,1)S(1)}, u32[]{:S(2)}, u32[]{:S(2)}) collective-permute-start(bf16[128,1536]{1,0:T(8,128)(2,1)S(1)} %copy-done.41), channel_id=1, source_target_pairs={{0,1},{1,0},{2,3},{3,2},{4,5},{5,4},{6,7},{7,6},{8,9},{9,8},{10,11... | collective-permute-start | bytes 1179656 | tf_op jit(solution)/shard_map/ppermute | solution.py:614
  153.8 42.4 %all-to-all-start = ((bf16[4,128,1664]{2,1,0:T(8,128)(2,1)}), bf16[4,128,1664]{2,1,0:T(8,128)(2,1)S(1)}, u32[]{:S(2)}, u32[]{:S(2)}) async-start(bf16[4,128,1664]{2,1,0:T(8,128)(2,1)} %get-tuple-element.195), calls=%async_computation | async-start | bytes 3407872 | tf_op jit(solution)/shard_map/all_to_all | solution.py:834
  157.4 174.7 %reduce-scatter.2.cloned.1.call-start = ((), (), s32[]{:S(2)}) async-start(), calls=%async_computation.5 | async-start | bytes 21233664 | tf_op jit(solution)/shard_map/reduce_scatter | solution.py:848
  196.2 25.0 %collective-permute-start.18 = (bf16[2,128,1536]{2,1,0:T(8,128)(2,1)}, bf16[2,128,1536]{2,1,0:T(8,128)(2,1)}, u32[]{:S(2)}, u32[]{:S(2)}) collective-permute-start(bf16[2,128,1536]{2,1,0:T(8,128)(2,1)} %get-tuple-element.220), channel_id=1, source_target_pairs={{0,1},{1,0},{2,3},{3,2},{4,5},{5,4},{6,7},{7,6},{8,9},{9,8},{10,11... | collective-permute-start | bytes 2359304 | tf_op jit(solution)/shard_map/ppermute | solution.py:614
  196.2 25.0 %collective-permute-start.17 = (bf16[4,1,576,512]{3,2,1,0:T(8,128)(2,1)}, bf16[4,1,576,512]{3,2,1,0:T(8,128)(2,1)}, u32[]{:S(2)}, u32[]{:S(2)}) collective-permute-start(bf16[4,1,576,512]{3,2,1,0:T(8,128)(2,1)} %get-tuple-element.219), channel_id=1, source_target_pairs={{0,4},{4,0},{8,12},{12,8},{16,20},{20,16},{24,28},{28,24},{1,5},{5... | collective-permute-start | bytes 7077896 | tf_op jit(solution)/shard_map/ppermute | solution.py:614
  204.4 16.8 %all-to-all-start.1 = ((bf16[4,128,384]{2,1,0:T(8,128)(2,1)}), bf16[4,128,384]{2,1,0:T(8,128)(2,1)S(1)}, u32[]{:S(2)}, u32[]{:S(2)}) async-start(bf16[4,128,384]{2,1,0:T(8,128)(2,1)} %copy-done.21), calls=%async_computation.1 | async-start | bytes 786432 | tf_op jit(solution)/shard_map/all_to_all | solution.py:834
  221.2 29.4 %all-to-all-start.2 = ((bf16[4,128,640]{2,1,0:T(8,128)(2,1)}), bf16[4,128,640]{2,1,0:T(8,128)(2,1)}, u32[]{:S(2)}, u32[]{:S(2)}) async-start(bf16[4,128,640]{2,1,0:T(8,128)(2,1)} %get-tuple-element.228), calls=%async_computation.2 | async-start | bytes 1310720 | tf_op jit(solution)/shard_map/all_to_all | solution.py:834
  225.5 20.7 %collective-permute-start.19 = (bf16[128,1536]{1,0:T(8,128)(2,1)}, bf16[128,1536]{1,0:T(8,128)(2,1)S(1)}, u32[]{:S(2)}, u32[]{:S(2)}) collective-permute-start(bf16[128,1536]{1,0:T(8,128)(2,1)} %collective-permute-done.16.refs_2_), channel_id=1, source_target_pairs={{0,1},{1,0},{2,3},{3,2},{4,5},{5,4},{6,7},{7,6},{8,9},{9,8},{10,11... | collective-permute-start | bytes 1179656 | tf_op jit(solution)/shard_map/ppermute | solution.py:614
  260.8 13.5 %collective-permute-start.22 = (bf16[2,1,192,512]{3,2,1,0:T(8,128)(2,1)S(1)}, bf16[2,1,192,512]{3,2,1,0:T(8,128)(2,1)S(1)}, u32[]{:S(2)}, u32[]{:S(2)}) collective-permute-start(bf16[2,1,192,512]{3,2,1,0:T(8,128)(2,1)S(1)} %get-tuple-element.251), channel_id=1, source_target_pairs={{0,8},{4,12},{8,0},{12,4},{16,24},{20,28},{24,16},{28,20},{1,9},{5... | collective-permute-start | bytes 1179656 | tf_op jit(solution)/shard_map/ppermute | solution.py:614
  261.6 20.3 %collective-permute-start.24 = (bf16[128,1536]{1,0:T(8,128)(2,1)S(1)}, bf16[128,1536]{1,0:T(8,128)(2,1)S(1)}, u32[]{:S(2)}, u32[]{:S(2)}) collective-permute-start(bf16[128,1536]{1,0:T(8,128)(2,1)S(1)} %bitcast.35), channel_id=1, source_target_pairs={{0,2},{1,3},{2,0},{3,1},{4,6},{5,7},{6,4},{7,5},{8,10},{9,11},{10,... | collective-permute-start | bytes 1179656 | tf_op jit(solution)/shard_map/ppermute | solution.py:614
  263.9 13.0 %collective-permute-start.23 = (bf16[2,1,192,640]{3,2,1,0:T(8,128)(2,1)S(1)}, bf16[2,1,192,640]{3,2,1,0:T(8,128)(2,1)S(1)}, u32[]{:S(2)}, u32[]{:S(2)}) collective-permute-start(bf16[2,1,192,640]{3,2,1,0:T(8,128)(2,1)S(1)} %get-tuple-element.253), channel_id=1, source_target_pairs={{0,16},{4,20},{8,24},{12,28},{16,0},{20,4},{24,8},{28,12},{1,17},{... | collective-permute-start | bytes 1474568 | tf_op jit(solution)/shard_map/ppermute | solution.py:614
  281.9 11.6 %collective-permute-start.25 = (bf16[1,192,512]{2,1,0:T(8,128)(2,1)S(1)}, bf16[1,192,512]{2,1,0:T(8,128)(2,1)S(1)}, u32[]{:S(2)}, u32[]{:S(2)}) collective-permute-start(bf16[1,192,512]{2,1,0:T(8,128)(2,1)S(1)} %get-tuple-element.262), channel_id=1, source_target_pairs={{0,16},{4,20},{8,24},{12,28},{16,0},{20,4},{24,8},{28,12},{1,17},{... | collective-permute-start | bytes 589832 | tf_op jit(solution)/shard_map/ppermute | solution.py:614
  282.5 13.6 %collective-permute-start.26 = (bf16[1,192,640]{2,1,0:T(8,128)(2,1)S(1)}, bf16[1,192,640]{2,1,0:T(8,128)(2,1)S(1)}, u32[]{:S(2)}, u32[]{:S(2)}) collective-permute-start(bf16[1,192,640]{2,1,0:T(8,128)(2,1)S(1)} %get-tuple-element.264), channel_id=1, source_target_pairs={{0,8},{4,12},{8,0},{12,4},{16,24},{20,28},{24,16},{28,20},{1,9},{5... | collective-permute-start | bytes 737288 | tf_op jit(solution)/shard_map/ppermute | solution.py:614
  296.3 25.7 %collective-permute-start.27 = (bf16[2,1,576,256]{3,2,1,0:T(8,128)(2,1)S(1)}, bf16[2,1,576,256]{3,2,1,0:T(8,128)(2,1)S(1)}, u32[]{:S(2)}, u32[]{:S(2)}) collective-permute-start(bf16[2,1,576,256]{3,2,1,0:T(8,128)(2,1)S(1)} %copy-done.31), channel_id=1, source_target_pairs={{0,8},{4,12},{8,0},{12,4},{16,24},{20,28},{24,16},{28,20},{1,9},{5... | collective-permute-start | bytes 1769480 | tf_op jit(solution)/shard_map/ppermute | solution.py:614
  297.4 24.7 %collective-permute-start.28 = (bf16[2,1,576,256]{3,2,1,0:T(8,128)(2,1)S(1)}, bf16[2,1,576,256]{3,2,1,0:T(8,128)(2,1)S(1)}, u32[]{:S(2)}, u32[]{:S(2)}) collective-permute-start(bf16[2,1,576,256]{3,2,1,0:T(8,128)(2,1)S(1)} %copy-done.29), channel_id=1, source_target_pairs={{0,16},{4,20},{8,24},{12,28},{16,0},{20,4},{24,8},{28,12},{1,17},{... | collective-permute-start | bytes 1769480 | tf_op jit(solution)/shard_map/ppermute | solution.py:614
  299.0 23.5 %collective-permute-start.30 = (bf16[192,1152]{1,0:T(8,128)(2,1)S(1)}, bf16[192,1152]{1,0:T(8,128)(2,1)S(1)}, u32[]{:S(2)}, u32[]{:S(2)}) collective-permute-start(bf16[192,1152]{1,0:T(8,128)(2,1)S(1)} %maximum_bitcast_fusion.refs_0_), channel_id=1, source_target_pairs={{0,2},{1,3},{2,0},{3,1},{4,6},{5,7},{6,4},{7,5},{8,10},{9,11},{10,... | collective-permute-start | bytes 1327112 | tf_op jit(solution)/shard_map/ppermute | solution.py:614
  299.0 23.5 %collective-permute-start.29 = (bf16[192,1152]{1,0:T(8,128)(2,1)S(1)}, bf16[192,1152]{1,0:T(8,128)(2,1)S(1)}, u32[]{:S(2)}, u32[]{:S(2)}) collective-permute-start(bf16[192,1152]{1,0:T(8,128)(2,1)S(1)} %maximum_bitcast_fusion.refs_0_), channel_id=1, source_target_pairs={{0,1},{1,0},{2,3},{3,2},{4,5},{5,4},{6,7},{7,6},{8,9},{9,8},{10,11... | collective-permute-start | bytes 1327112 | tf_op jit(solution)/shard_map/ppermute | solution.py:614
  324.5 12.5 %collective-permute-start.31 = (bf16[192,1152]{1,0:T(8,128)(2,1)S(1)}, bf16[192,1152]{1,0:T(8,128)(2,1)S(1)}, u32[]{:S(2)}, u32[]{:S(2)}) collective-permute-start(bf16[192,1152]{1,0:T(8,128)(2,1)S(1)} %collective-permute-done.30.refs_2_), channel_id=1, source_target_pairs={{0,1},{1,0},{2,3},{3,2},{4,5},{5,4},{6,7},{7,6},{8,9},{9,8},{10,11... | collective-permute-start | bytes 1327112 | tf_op jit(solution)/shard_map/ppermute | solution.py:614
  (54 other events, 500.3 us)
Sparse Core Ops, SparseCore 0:
  9.9 54.3 all-gather.1
  173.6 148.3 reduce-scatter.1

commit v5 on v4

--- a/solution.py
+++ b/solution.py
@@ -50,28 +50,30 @@
 
     mine = own * experts_here + e
     g = column(gates_ref[...], mine)
-    gate_pre = dot_nn(n2[...], gate_ref[0])
-    up_pre = dot_nn(n2[...], up_ref[0])
-    raw_back = raw_ref[0]
-    sig = 1.0 / (1.0 + jnp.exp(-gate_pre))
-    silu = gate_pre * sig
-    hidden = (silu * up_pre).astype(BF).astype(F32)
-    back = jnp.sum(hidden * raw_back, axis=1, keepdims=True)
-    weighed = (g * hidden).astype(BF)
-    weighed_ref[0] = weighed
-    hid_ref[0] = weighed.T
+    sides = [slice(h * (H // 2), (h + 1) * (H // 2)) for h in range(2)]
+    pres = [(dot_nn(n2[...], gate_ref[0, :, s]), dot_nn(n2[...], up_ref[0, :, s])) for s in sides]
+    back = jnp.zeros((blocks * T, 1), F32)
+    for s, (gate_pre, up_pre) in zip(sides, pres):
+        raw = raw_ref[0, :, s]
+        sig = 0.5 * jnp.tanh(0.5 * gate_pre) + 0.5
+        silu = gate_pre * sig
+        hidden = (silu * up_pre).astype(BF).astype(F32)
+        back = back + jnp.sum(hidden * raw, axis=1, keepdims=True)
+        weighed = (g * hidden).astype(BF)
+        weighed_ref[0, :, s] = weighed
+        hid_ref[0, s, :] = weighed.T
+        hid_back = g * raw
+        grow = (hid_back * up_pre * (sig + silu * (1.0 - sig))).astype(BF)
+        urow = (hid_back * silu).astype(BF)
+        grow_ref[0, :, s] = grow
+        urow_ref[0, :, s] = urow
+    lane = lax.broadcasted_iota(jnp.int32, aux_ref.shape, 1)
+    aux_ref[...] = jnp.where(lane == mine, back, aux_ref[...])
     part = pl.multiple_of(jnp.minimum(e, W // C - 1) * C, C)
     n2t_ref[pl.ds(part, C), :] = n2[:, pl.ds(part, C)].T
-    lane = lax.broadcasted_iota(jnp.int32, aux_ref.shape, 1)
-    aux_ref[...] = jnp.where(lane == mine, back, aux_ref[...])
-    hid_back = g * raw_back
-    grow = (hid_back * up_pre * (sig + silu * (1.0 - sig))).astype(BF)
-    urow = (hid_back * silu).astype(BF)
-    grow_ref[0] = grow
-    urow_ref[0] = urow
     for j in range(W // C):
         cols = slice(j * C, (j + 1) * C)
-        rows[:, cols] += dot_nt(grow, gate_ref[0, cols, :]) + dot_nt(urow, up_ref[0, cols, :])
+        rows[:, cols] += dot_nt(grow_ref[0], gate_ref[0, cols, :]) + dot_nt(urow_ref[0], up_ref[0, cols, :])
 
     @pl.when(e == experts_here - 1)
     def _():
@@ -682,45 +684,39 @@
     return [tuple(a) + p[2:] for a, p in zip(arrays, parts)], *others
 
 
-def unpack_kernel(many, in_ref, *refs):
-    parts, (gate_ref, up_ref, down_ref) = refs[:-3], refs[-3:]
+def unpack_kernel(parts, *refs):
+    gate_ref, up_ref, down_ref = refs[-3:]
     R, D = gate_ref.shape[1], down_ref.shape[1]
     H = gate_ref.shape[2]
-
-    def store(total, at):
+    at = 0
+    for i in range(0, len(parts), 2):
+        total = refs[parts[i]][0].astype(F32)
+        if parts[i + 1] is not None:
+            total = total + refs[parts[i + 1]][0].astype(F32)
         width = total.shape[1]
         gate_ref[0, :, at:at + width] = total[:R]
         up_ref[0, :, at:at + width] = total[R:2 * R]
         for j in range(down_ref.shape[2] // H):
             down_ref[0, :, j * H + at:j * H + at + width] = total[2 * R + j * D:2 * R + (j + 1) * D]
-
-    @pl.when(pl.program_id(0) < many)
-    def _():
-        store(in_ref[0, 0].astype(F32), 0)
-
-    @pl.when(pl.program_id(0) >= many)
-    def _():
-        at = 0
-        for mine, theirs in (parts[:2], parts[2:]):
-            store(mine[0].astype(F32) + theirs[0].astype(F32), at)
-            at += mine.shape[2]
-
-
-def unpack(packed, parts, R, D, W):
-    _, many, rows, H = packed.shape
-    E = many + parts[0].shape[0]
-    S = jax.ShapeDtypeStruct
-    out = lambda a, b: pl.BlockSpec((1, a, b), lambda e: (e, 0, 0))
-    return pl.pallas_call(
-        functools.partial(unpack_kernel, many),
-        grid=(E,),
+        at += width
+
+
+def unpack(first, ins, parts, before, E, R, D, W):
+    count, rows, _ = ins[0].shape
+    H = before[0].shape[2] if before else ins[0].shape[2]
+    S = jax.ShapeDtypeStruct
+    out = lambda a, b: pl.BlockSpec((1, a, b), lambda e: (e + first, 0, 0))
+    return pl.pallas_call(
+        functools.partial(unpack_kernel, parts),
+        grid=(count,),
         out_shape=(S((E, R, H), F32), S((E, R, H), F32), S((E, D, W), F32)),
-        in_specs=[pl.BlockSpec((1, 1, rows, H), lambda e: (0, jnp.minimum(e, many - 1), 0, 0))]
-        + [pl.BlockSpec((1, rows, x.shape[2]), lambda e: (jnp.maximum(e - many, 0), 0, 0)) for x in parts],
+        in_specs=[pl.BlockSpec((1, rows, x.shape[2]), lambda e: (e, 0, 0)) for x in ins]
+        + [pl.BlockSpec(memory_space=pl.ANY)] * len(before),
         out_specs=(out(R, H), out(R, H), out(D, W)),
+        input_output_aliases={len(ins) + i: i for i in range(len(before))},
         compiler_params=pltpu.CompilerParams(vmem_limit_bytes=40 << 20),
-        cost_estimate=pl.CostEstimate(flops=3 * E * R * H, bytes_accessed=18 * E * R * H, transcendentals=0),
-    )(packed, *parts)
+        cost_estimate=pl.CostEstimate(flops=3 * count * R * H, bytes_accessed=18 * count * R * H, transcendentals=0),
+    )(*ins, *before)
 
 
 def spread_kernel(kv, where_ref, *refs):
@@ -873,13 +869,12 @@
     five = finish(five, n_dp)
     part = jnp.concatenate([mine.astype(F32) + theirs.astype(F32) for mine, theirs, *_ in five], axis=-1)[0].astype(BF)
     few, part = tie_parts(few, part)
-    parts = begin_z(part, ne)
-    few, parts = tie_parts(halve(few, n_dp), parts)
-    parts = end_z(parts, ne)
+    parts = gather_z(part, ne)
     few = finish(few, n_dp)
-    made = unpack(packed, [x for p in few for x in p[:2]], R, D, W)
-    parts, (gate_grad, up_grad, down_grad) = tie((parts, made))
+    made = unpack(0, [packed[0]], (0, None), (), E, R, D, W)
+    parts, made = tie((parts, made))
     query_grad, key_grad, value_grad, out_grad, extra = spread(where, parts, W, KV)
+    gate_grad, up_grad, down_grad = unpack(MANY, [x for p in few for x in p[:2]], (0, 1, 2, 3), made, E, R, D, W)
     layer_out = (resid + comb + sum(x.astype(F32) for x in comb_far)).astype(BF)
     return (layer_out, input_grad, query_grad, key_grad, value_grad, out_grad, extra[:, experts + 1], extra[:, experts],
             extra[:, :experts], gate_grad, up_grad, down_grad)

time: 349 us -> 343 us (0.983)
  waiting for transfers between devices: 124 us -> 119 us
    ppermute x34, waiting for transfers between devices: 119 us -> 114 us  [flip(): return lax.ppermute(x, axis, [(i, i ^ mask) for i in range(size)])]
    unnamed x96 -> x100, local copies, waits for them, and re-layouts: 19.6 us -> 19.9 us
  transfers between devices with their start and end apart: 39 -> 39, of which waited for: 21 -> 20; matrix products, arithmetic and copies ran while one was open for 5% -> 6% of each run, Pallas kernels for 31% -> 31%
where the time goes in v5:
time: 343 us; the launch traced here: 341 us
  Pallas kernels  120 us (35%)
  waiting for transfers between devices  119 us (35%)
  starting transfers between devices  48.6 us (14%)
  local copies, waits for them, and re-layouts  32.9 us (10%)
  between operations  14.7 us (4%)
  other arithmetic  6.45 us (2%)
    ppermute x34, waiting for transfers between devices, flip(): return lax.ppermute(x, axis, [(i, i ^ mask) for i in range(size)])  114 us
    ppermute x34, starting transfers between devices, flip(): return lax.ppermute(x, axis, [(i, i ^ mask) for i in range(size)])  37.1 us
    pallas_call x1, Pallas kernels, expert_rows(): pl.pallas_call(functools.partial(expert_kernel, blocks, choices), out_sha...  26.6 us
    pallas_call x2, Pallas kernels, expert_grads(): pl.pallas_call(functools.partial(grad_kernel, blocks, apart), out_shape=(...  25.5 us
    unnamed x100, local copies, waits for them, and re-layouts  19.9 us
    all_to_all x3, starting transfers between devices, local(): lax.all_to_all(x, 'expert', split_axis=0, concat_axis=0, tiled=True)  11.5 us
    pallas_call x1, Pallas kernels, forward(): pl.pallas_call(functools.partial(forward_kernel, places, kv, experts), ou...  11.3 us
    pallas_call x1, Pallas kernels, backward(): pl.pallas_call(functools.partial(backward_kernel, places), out_shape=(S((...  11.1 us
  transfers between devices with their start and end apart: 39, of which 20 were waited for; matrix products, arithmetic and copies ran while one was open for 6% of the time, Pallas kernels for 31%

profile of v5, /device:TPU:0, one launch (start us, length us, event | category | flops | bytes accessed | tf_op | source)
XLA Modules:
  0.0 341.4 jit_solution(6951336367589232659)
XLA Ops:
  12.6 3.0 collective-permute-start.1
  26.6 21.0 %collective-permute-done.1.refs_4_ = bf16[192,2688]{1,0:T(8,128)(2,1)} collective-permute-done((bf16[192,2688]{1,0:T(8,128)(2,1)S(1)}, bf16[192,2688]{1,0:T(8,128)(2,1)}, u32[]{:S(2)}, u32[]{:S(2)}) %collective-permute-start.1) | collective-permute-done | bytes 1032224 | tf_op jit(solution)/shard_map/ppermute | solution.py:616
  47.5 2.7 collective-permute-done.refs_2_
  52.1 3.2 collective-permute-done.3.refs_2_.refs_6_
  58.1 9.9 %collective-permute-done.8.refs_6_ = bf16[192,1280]{1,0:T(8,128)(2,1)} collective-permute-done((bf16[192,1280]{1,0:T(8,128)(2,1)S(1)}, bf16[192,1280]{1,0:T(8,128)(2,1)}, u32[]{:S(2)}, u32[]{:S(2)}) %collective-permute-start.8) | collective-permute-done | bytes 491552 | tf_op jit(solution)/shard_map/ppermute | solution.py:616
  68.0 3.1 collective-permute-done.9.refs_7_
  71.1 3.3 collective-permute-done.4.refs_3_.refs_7_
  76.7 11.3 %shard_map.229 = (bf16[128,2560]{1,0:T(8,128)(2,1)}, bf16[128,1536]{1,0:T(8,128)(2,1)}, f32[128,1536]{1,0:T(8,128)}, bf16[128,1536]{1,0:T(8,128)(2,1)}, f32[8,15...) custom-call(s32[4]{0:T(128)} %pad_add_fusion.dev_ref.where_ref, bf16[128,1536]{1,0:T(8,128)(2,1)} %tok_ref.3, ...), custom_call_target="tpu_custom_call" | custom-call | tf_op jit(solution)/shard_map/pallas_call | solution.py:381
  88.1 3.4 %collective-permute-start.13 = (bf16[128,1536]{1,0:T(8,128)(2,1)}, bf16[128,1536]{1,0:T(8,128)(2,1)}, u32[]{:S(2)}, u32[]{:S(2)}) collective-permute-start(bf16[128,1536]{1,0:T(8,128)(2,1)} %get-tuple-element.177.refs_0_.refs_3_), channel_id=1, source_target_pairs={{0,2},{1,3},{2,0},{3,1},{4,6},{5,7},{6,4},{7,5},{8,10},{9,11},{10,... | collective-permute-start | bytes 1179656 | tf_op jit(solution)/shard_map/ppermute | solution.py:616
  93.3 9.6 %shard_map.230.refs_11_ = f32[5,512,512]{2,1,0:T(8,128)} custom-call(bf16[128,3200]{1,0:T(8,128)(2,1)} %copy-done, bf16[128,3200]{1,0:T(8,128)(2,1)} %copy-done.5, bf16[128,3200]{1,0:T(8,128)(2,1)} %copy-done.3, bf16[128,3200]{1,0:T(8,128)(2,1)} %copy-done.7, bf16[5,512,1536]{2,1,0:T(8,128)(2,1)} %down_ref.1), custom_call_target="tpu_custom_call" | custom-call | tf_op jit(solution)/shard_map/pallas_call | solution.py:219
  105.4 4.6 %collective-permute-done.13.refs_2_ = bf16[128,1536]{1,0:T(8,128)(2,1)} collective-permute-done((bf16[128,1536]{1,0:T(8,128)(2,1)}, bf16[128,1536]{1,0:T(8,128)(2,1)}, u32[]{:S(2)}, u32[]{:S(2)}) %collective-permute-start.13) | collective-permute-done | bytes 393248 | tf_op jit(solution)/shard_map/ppermute | solution.py:616
  111.7 9.3 %collective-permute-done.14.refs_3_ = bf16[128,1536]{1,0:T(8,128)(2,1)S(1)} collective-permute-done((bf16[128,1536]{1,0:T(8,128)(2,1)}, bf16[128,1536]{1,0:T(8,128)(2,1)S(1)}, u32[]{:S(2)}, u32[]{:S(2)}) %collective-permute-start.14) | collective-permute-done | bytes 393248 | tf_op jit(solution)/shard_map/ppermute | solution.py:616
  125.3 26.6 %shard_map.232 = (bf16[4,128,1664]{2,1,0:T(8,128)(2,1)}, f32[512,128]{1,0:T(8,128)}, bf16[1536,512]{1,0:T(8,128)(2,1)}, bf16[5,512,512]{2,1,0:T(8,128)(2,1)}, bf...) custom-call(s32[4]{0:T(128)} %pad_add_fusion.dev_ref.where_ref, ...), custom_call_target="tpu_custom_call" | custom-call | flops 16106127360 | bytes 33030144 | tf_op jit(solution)/shard_map/pallas_call | solution.py:97
  152.7 3.6 %all-to-all-start = ((bf16[4,128,1664]{2,1,0:T(8,128)(2,1)}), bf16[4,128,1664]{2,1,0:T(8,128)(2,1)S(1)}, u32[]{:S(2)}, u32[]{:S(2)}) async-start(bf16[4,128,1664]{2,1,0:T(8,128)(2,1)} %get-tuple-element.191), calls=%async_computation | async-start | bytes 3407872 | tf_op jit(solution)/shard_map/all_to_all | solution.py:830
  156.3 16.0 %shard_map.233 = bf16[8,4,576,512]{3,2,1,0:T(8,128)(2,1)} custom-call(s32[4]{0:T(128)} %pad_add_fusion.dev_ref.where_ref, bf16[128,3200]{1,0:T(8,128)(2,1)} %copy-done, bf16[128,3200]{1,0:T(8,128)(2,1)} %copy-done.5, bf16[128,3200]{1,0:T(8,128)(2,1)} %copy-done.3, bf16[128,3200]{1,0:T(8,128)(2,1)} %copy-done.7, ...), custom_call_target="tpu_custom_call" | custom-call | tf_op jit(solution)/shard_map/pallas_call | solution.py:151
  172.4 9.5 %shard_map.234 = (bf16[4,1,576,512]{3,2,1,0:T(8,128)(2,1)}, bf16[4,1,576,512]{3,2,1,0:T(8,128)(2,1)}) custom-call(s32[4]{0:T(128)} %pad_add_fusion.dev_ref.where_ref, bf16[128,3200]{1,0:T(8,128)(2,1)} %copy-done, bf16[128,3200]{1,0:T(8,128)(2,1)} %copy-done.5, bf16[128,3200]{1,0:T(8,128)(2,1)} %copy-done.3, bf16[128,3200]{1,0:T(8,128)(2,1)} %copy-done.7, ...), custom_call_target="tpu_custom_call" | custom-call | tf_op jit(solution)/shard_map/pallas_call | solution.py:151
  181.8 11.0 %shard_map.235 = (bf16[2,128,1536]{2,1,0:T(8,128)(2,1)}, bf16[2,128,1536]{2,1,0:T(8,128)(2,1)}) custom-call(bf16[5,512,512]{2,1,0:T(8,128)(2,1)} %get-tuple-element.200.weighed_ref, bf16[5,512,1536]{2,1,0:T(8,128)(2,1)} %down_ref.1), custom_call_target="tpu_custom_call" | custom-call | tf_op jit(solution)/shard_map/pallas_call | solution.py:190
  203.4 3.7 %all-to-all-start.1 = ((bf16[4,128,384]{2,1,0:T(8,128)(2,1)}), bf16[4,128,384]{2,1,0:T(8,128)(2,1)S(1)}, u32[]{:S(2)}, u32[]{:S(2)}) async-start(bf16[4,128,384]{2,1,0:T(8,128)(2,1)} %copy-done.23), calls=%async_computation.1 | async-start | bytes 786432 | tf_op jit(solution)/shard_map/all_to_all | solution.py:830
  207.1 11.1 %shard_map.237 = (bf16[128,2560]{1,0:T(8,128)(2,1)}, bf16[4,128,640]{2,1,0:T(8,128)(2,1)}) custom-call(s32[4]{0:T(128)} %pad_add_fusion.dev_ref.where_ref, bf16[128,1536]{1,0:T(8,128)(2,1)} %copy-done.22, bf16[128,2560]{1,0:T(8,128)(2,1)} %get-tuple-element.211.qkv_ref, f32[128,128]{1,0:T(8,128)} %copy.60.cos_ref, f32[128,128]{1,0:T(8,128)} %pad_maximum_fusion.sin_ref, ...), custom_call_target="tpu_custom_call" | custom-call | tf_op jit(solution)/shard_map/pallas_call | solution.py:496
  220.2 4.2 %all-to-all-start.2 = ((bf16[4,128,640]{2,1,0:T(8,128)(2,1)}), bf16[4,128,640]{2,1,0:T(8,128)(2,1)}, u32[]{:S(2)}, u32[]{:S(2)}) async-start(bf16[4,128,640]{2,1,0:T(8,128)(2,1)} %get-tuple-element.224), calls=%async_computation.2 | async-start | bytes 1310720 | tf_op jit(solution)/shard_map/all_to_all | solution.py:830
  233.0 2.8 copy-done.2
  235.9 4.5 %shard_map.239 = (f32[128,1536]{1,0:T(8,128)}, f32[1536,128]{1,0:T(8,128)S(1)}) custom-call(bf16[128,2560]{1,0:T(8,128)(2,1)S(1)} %copy-done.18, bf16[128,1536]{1,0:T(8,128)(2,1)S(1)} %copy-done.10, f32[8,1536]{1,0:T(8,128)S(1)} %copy-done.26, f32[128,1536]{1,0:T(8,128)S(1)} %get-tuple-element.226.resid_back_ref, ...), custom_call_target="tpu_custom_call" | custom-call | tf_op jit(solution)/shard_map/pallas_call | solution.py:532
  241.2 3.8 %collective-permute-done.19.refs_3_ = bf16[128,1536]{1,0:T(8,128)(2,1)S(1)} collective-permute-done((bf16[128,1536]{1,0:T(8,128)(2,1)}, bf16[128,1536]{1,0:T(8,128)(2,1)S(1)}, u32[]{:S(2)}, u32[]{:S(2)}) %collective-permute-start.19) | collective-permute-done | bytes 393248 | tf_op jit(solution)/shard_map/ppermute | solution.py:616
  245.7 3.7 %shard_map.240 = (bf16[4,1,192,384]{3,2,1,0:T(8,128)(2,1)}, bf16[4,1,192,384]{3,2,1,0:T(8,128)(2,1)}) custom-call(s32[4]{0:T(128)} %pad_add_fusion.dev_ref.where_ref, bf16[128,1536]{1,0:T(8,128)(2,1)} %get-tuple-element.230.refs_0_, bf16[128,1536]{1,0:T(8,128)(2,1)} %copy-done.44, bf16[128,1536]{1,0:T(8,128)(2,1)} %collective-permute-done.16.refs_2_, ...), custom_call_target="tpu_custom_call" | custom-call | tf_op jit(solution)/shard_map/pallas_call | solution.py:567
  249.5 5.1 %shard_map.241 = (bf16[4,1,192,768]{3,2,1,0:T(8,128)(2,1)}, bf16[4,1,192,768]{3,2,1,0:T(8,128)(2,1)}) custom-call(s32[4]{0:T(128)} %pad_add_fusion.dev_ref.where_ref, bf16[2,4,192,512]{3,2,1,0:T(8,128)(2,1)} %copy-done.14, bf16[4,128,640]{2,1,0:T(8,128)(2,1)} %all-to-all-done.2.qkv_ref, f32[1536,128]{1,0:T(8,128)} %copy-done.29), custom_call_target="tpu_custom_call" | custom-call | flops 1207959552 | bytes 4718592 | tf_op jit(solution)/shard_map/pallas_call | solution.py:605
  254.9 2.8 collective-permute-done.21.refs_3_
  263.0 10.2 %collective-permute-done.22 = bf16[2,1,192,512]{3,2,1,0:T(8,128)(2,1)S(1)} collective-permute-done((bf16[2,1,192,512]{3,2,1,0:T(8,128)(2,1)S(1)}, bf16[2,1,192,512]{3,2,1,0:T(8,128)(2,1)S(1)}, u32[]{:S(2)}, u32[]{:S(2)}) %collective-permute-start.22) | collective-permute-done | bytes 393248 | tf_op jit(solution)/shard_map/ppermute | solution.py:616
  275.6 4.6 %collective-permute-done.24 = bf16[128,1536]{1,0:T(8,128)(2,1)S(1)} collective-permute-done((bf16[128,1536]{1,0:T(8,128)(2,1)S(1)}, bf16[128,1536]{1,0:T(8,128)(2,1)S(1)}, u32[]{:S(2)}, u32[]{:S(2)}) %collective-permute-start.24) | collective-permute-done | bytes 393248 | tf_op jit(solution)/shard_map/ppermute | solution.py:616
  282.0 9.8 %collective-permute-done.25 = bf16[1,192,512]{2,1,0:T(8,128)(2,1)S(1)} collective-permute-done((bf16[1,192,512]{2,1,0:T(8,128)(2,1)S(1)}, bf16[1,192,512]{2,1,0:T(8,128)(2,1)S(1)}, u32[]{:S(2)}, u32[]{:S(2)}) %collective-permute-start.25) | collective-permute-done | bytes 196640 | tf_op jit(solution)/shard_map/ppermute | solution.py:616
  297.4 2.9 collective-permute-start.27
  300.3 15.9 %collective-permute-done.28.refs_2_ = bf16[192,1152]{1,0:T(8,128)(2,1)S(1)} collective-permute-done((bf16[192,1152]{1,0:T(8,128)(2,1)S(1)}, bf16[192,1152]{1,0:T(8,128)(2,1)S(1)}, u32[]{:S(2)}, u32[]{:S(2)}) %collective-permute-start.28) | collective-permute-done | bytes 442400 | tf_op jit(solution)/shard_map/ppermute | solution.py:616
  316.2 5.1 %collective-permute-done.30 = bf16[2,1,576,256]{3,2,1,0:T(8,128)(2,1)S(1)} collective-permute-done((bf16[2,1,576,256]{3,2,1,0:T(8,128)(2,1)S(1)}, bf16[2,1,576,256]{3,2,1,0:T(8,128)(2,1)S(1)}, u32[]{:S(2)}, u32[]{:S(2)}) %collective-permute-start.30) | collective-permute-done | bytes 589856 | tf_op jit(solution)/shard_map/ppermute | solution.py:616
  (199 shorter events, 85.4 us)
Async XLA Ops:
  7.2 69.5 %all-gather.2.cloned.1.call-start = ((), (), s32[]{:S(2)}) async-start(), calls=%async_computation.4 | async-start | bytes 5308416 | tf_op jit(solution)/shard_map/all_gather | solution.py:813
  12.6 35.0 %collective-permute-start.1 = (bf16[192,2688]{1,0:T(8,128)(2,1)S(1)}, bf16[192,2688]{1,0:T(8,128)(2,1)}, u32[]{:S(2)}, u32[]{:S(2)}) collective-permute-start(bf16[192,2688]{1,0:T(8,128)(2,1)S(1)} %concatenate.13.refs_0_), channel_id=1, source_target_pairs={{0,16},{4,20},{8,24},{12,28},{16,0},{20,4},{24,8},{28,12},{1,17},{... | collective-permute-start | bytes 3096584 | tf_op jit(solution)/shard_map/ppermute | solution.py:616
  15.6 34.7 %collective-permute-start = (bf16[192,2688]{1,0:T(8,128)(2,1)S(1)}, bf16[192,2688]{1,0:T(8,128)(2,1)}, u32[]{:S(2)}, u32[]{:S(2)}) collective-permute-start(bf16[192,2688]{1,0:T(8,128)(2,1)S(1)} %concatenate.13.refs_0_), channel_id=1, source_target_pairs={{0,8},{4,12},{8,0},{12,4},{16,24},{20,28},{24,16},{28,20},{1,9},{5... | collective-permute-start | bytes 3096584 | tf_op jit(solution)/shard_map/ppermute | solution.py:616
  17.3 38.0 %collective-permute-start.3 = (bf16[128,3200]{1,0:T(8,128)(2,1)S(1)}, bf16[128,3200]{1,0:T(8,128)(2,1)S(1)}, u32[]{:S(2)}, u32[]{:S(2)}) collective-permute-start(bf16[128,3200]{1,0:T(8,128)(2,1)S(1)} %fusion.3.refs_0_.refs_4_), channel_id=1, source_target_pairs={{0,2},{1,3},{2,0},{3,1},{4,6},{5,7},{6,4},{7,5},{8,10},{9,11},{10,... | collective-permute-start | bytes 2457608 | tf_op jit(solution)/shard_map/ppermute | solution.py:616
  20.0 37.7 %collective-permute-start.2 = (bf16[128,3200]{1,0:T(8,128)(2,1)S(1)}, bf16[128,3200]{1,0:T(8,128)(2,1)S(1)}, u32[]{:S(2)}, u32[]{:S(2)}) collective-permute-start(bf16[128,3200]{1,0:T(8,128)(2,1)S(1)} %fusion.3.refs_0_.refs_4_), channel_id=1, source_target_pairs={{0,1},{1,0},{2,3},{3,2},{4,5},{5,4},{6,7},{7,6},{8,9},{9,8},{10,11... | collective-permute-start | bytes 2457608 | tf_op jit(solution)/shard_map/ppermute | solution.py:616
  52.0 16.0 %collective-permute-start.8 = (bf16[192,1280]{1,0:T(8,128)(2,1)S(1)}, bf16[192,1280]{1,0:T(8,128)(2,1)}, u32[]{:S(2)}, u32[]{:S(2)}) collective-permute-start(bf16[192,1280]{1,0:T(8,128)(2,1)S(1)} %slice.46), channel_id=1, source_target_pairs={{0,16},{4,20},{8,24},{12,28},{16,0},{20,4},{24,8},{28,12},{1,17},{... | collective-permute-start | bytes 1474568 | tf_op jit(solution)/shard_map/ppermute | solution.py:616
  55.4 19.0 %collective-permute-start.4 = (bf16[128,3200]{1,0:T(8,128)(2,1)S(1)}, bf16[128,3200]{1,0:T(8,128)(2,1)S(1)}, u32[]{:S(2)}, u32[]{:S(2)}) collective-permute-start(bf16[128,3200]{1,0:T(8,128)(2,1)S(1)} %collective-permute-done.3.refs_2_.refs_6_), channel_id=1, source_target_pairs={{0,1},{1,0},{2,3},{3,2},{4,5},{5,4},{6,7},{7,6},{8,9},{9,8},{10,11... | collective-permute-start | bytes 2457608 | tf_op jit(solution)/shard_map/ppermute | solution.py:616
  57.0 14.1 %collective-permute-start.9 = (bf16[192,1408]{1,0:T(8,128)(2,1)S(1)}, bf16[192,1408]{1,0:T(8,128)(2,1)}, u32[]{:S(2)}, u32[]{:S(2)}) collective-permute-start(bf16[192,1408]{1,0:T(8,128)(2,1)S(1)} %slice.47), channel_id=1, source_target_pairs={{0,8},{4,12},{8,0},{12,4},{16,24},{20,28},{24,16},{28,20},{1,9},{5... | collective-permute-start | bytes 1622024 | tf_op jit(solution)/shard_map/ppermute | solution.py:616
  57.6 19.0 %collective-permute-start.6 = (bf16[192,2688]{1,0:T(8,128)(2,1)}, bf16[192,2688]{1,0:T(8,128)(2,1)}, u32[]{:S(2)}, u32[]{:S(2)}) collective-permute-start(bf16[192,2688]{1,0:T(8,128)(2,1)} %collective-permute-done.refs_2_), channel_id=1, source_target_pairs={{0,4},{4,0},{8,12},{12,8},{16,20},{20,16},{24,28},{28,24},{1,5},{5... | collective-permute-start | bytes 3096584 | tf_op jit(solution)/shard_map/ppermute | solution.py:616
  57.6 19.0 %collective-permute-start.5 = (bf16[192,2688]{1,0:T(8,128)(2,1)}, bf16[192,2688]{1,0:T(8,128)(2,1)}, u32[]{:S(2)}, u32[]{:S(2)}) collective-permute-start(bf16[192,2688]{1,0:T(8,128)(2,1)} %copy-done.37), channel_id=1, source_target_pairs={{0,4},{4,0},{8,12},{12,8},{16,20},{20,16},{24,28},{28,24},{1,5},{5... | collective-permute-start | bytes 3096584 | tf_op jit(solution)/shard_map/ppermute | solution.py:616
  88.1 21.9 %collective-permute-start.13 = (bf16[128,1536]{1,0:T(8,128)(2,1)}, bf16[128,1536]{1,0:T(8,128)(2,1)}, u32[]{:S(2)}, u32[]{:S(2)}) collective-permute-start(bf16[128,1536]{1,0:T(8,128)(2,1)} %get-tuple-element.177.refs_0_.refs_3_), channel_id=1, source_target_pairs={{0,2},{1,3},{2,0},{3,1},{4,6},{5,7},{6,4},{7,5},{8,10},{9,11},{10,... | collective-permute-start | bytes 1179656 | tf_op jit(solution)/shard_map/ppermute | solution.py:616
  91.6 18.6 %collective-permute-start.12 = (bf16[128,1536]{1,0:T(8,128)(2,1)}, bf16[128,1536]{1,0:T(8,128)(2,1)}, u32[]{:S(2)}, u32[]{:S(2)}) collective-permute-start(bf16[128,1536]{1,0:T(8,128)(2,1)} %get-tuple-element.177.refs_0_.refs_3_), channel_id=1, source_target_pairs={{0,1},{1,0},{2,3},{3,2},{4,5},{5,4},{6,7},{7,6},{8,9},{9,8},{10,11... | collective-permute-start | bytes 1179656 | tf_op jit(solution)/shard_map/ppermute | solution.py:616
  121.0 30.9 %collective-permute-start.16 = (bf16[128,1536]{1,0:T(8,128)(2,1)S(1)}, bf16[128,1536]{1,0:T(8,128)(2,1)}, u32[]{:S(2)}, u32[]{:S(2)}) collective-permute-start(bf16[128,1536]{1,0:T(8,128)(2,1)S(1)} %copy-done.43), channel_id=1, source_target_pairs={{0,2},{1,3},{2,0},{3,1},{4,6},{5,7},{6,4},{7,5},{8,10},{9,11},{10,... | collective-permute-start | bytes 1179656 | tf_op jit(solution)/shard_map/ppermute | solution.py:616
  123.6 28.4 %collective-permute-start.15 = (bf16[128,1536]{1,0:T(8,128)(2,1)S(1)}, bf16[128,1536]{1,0:T(8,128)(2,1)S(1)}, u32[]{:S(2)}, u32[]{:S(2)}) collective-permute-start(bf16[128,1536]{1,0:T(8,128)(2,1)S(1)} %copy-done.43), channel_id=1, source_target_pairs={{0,1},{1,0},{2,3},{3,2},{4,5},{5,4},{6,7},{7,6},{8,9},{9,8},{10,11... | collective-permute-start | bytes 1179656 | tf_op jit(solution)/shard_map/ppermute | solution.py:616
  152.7 42.4 %all-to-all-start = ((bf16[4,128,1664]{2,1,0:T(8,128)(2,1)}), bf16[4,128,1664]{2,1,0:T(8,128)(2,1)S(1)}, u32[]{:S(2)}, u32[]{:S(2)}) async-start(bf16[4,128,1664]{2,1,0:T(8,128)(2,1)} %get-tuple-element.191), calls=%async_computation | async-start | bytes 3407872 | tf_op jit(solution)/shard_map/all_to_all | solution.py:830
  156.3 169.1 %reduce-scatter.2.cloned.1.call-start = ((), (), s32[]{:S(2)}) async-start(), calls=%async_computation.5 | async-start | bytes 21233664 | tf_op jit(solution)/shard_map/reduce_scatter | solution.py:844
  195.1 25.0 %collective-permute-start.18 = (bf16[2,128,1536]{2,1,0:T(8,128)(2,1)}, bf16[2,128,1536]{2,1,0:T(8,128)(2,1)}, u32[]{:S(2)}, u32[]{:S(2)}) collective-permute-start(bf16[2,128,1536]{2,1,0:T(8,128)(2,1)} %get-tuple-element.216), channel_id=1, source_target_pairs={{0,1},{1,0},{2,3},{3,2},{4,5},{5,4},{6,7},{7,6},{8,9},{9,8},{10,11... | collective-permute-start | bytes 2359304 | tf_op jit(solution)/shard_map/ppermute | solution.py:616
  195.1 25.0 %collective-permute-start.17 = (bf16[4,1,576,512]{3,2,1,0:T(8,128)(2,1)}, bf16[4,1,576,512]{3,2,1,0:T(8,128)(2,1)}, u32[]{:S(2)}, u32[]{:S(2)}) collective-permute-start(bf16[4,1,576,512]{3,2,1,0:T(8,128)(2,1)} %get-tuple-element.215), channel_id=1, source_target_pairs={{0,4},{4,0},{8,12},{12,8},{16,20},{20,16},{24,28},{28,24},{1,5},{5... | collective-permute-start | bytes 7077896 | tf_op jit(solution)/shard_map/ppermute | solution.py:616
  203.4 16.8 %all-to-all-start.1 = ((bf16[4,128,384]{2,1,0:T(8,128)(2,1)}), bf16[4,128,384]{2,1,0:T(8,128)(2,1)S(1)}, u32[]{:S(2)}, u32[]{:S(2)}) async-start(bf16[4,128,384]{2,1,0:T(8,128)(2,1)} %copy-done.23), calls=%async_computation.1 | async-start | bytes 786432 | tf_op jit(solution)/shard_map/all_to_all | solution.py:830
  220.2 29.3 %all-to-all-start.2 = ((bf16[4,128,640]{2,1,0:T(8,128)(2,1)}), bf16[4,128,640]{2,1,0:T(8,128)(2,1)}, u32[]{:S(2)}, u32[]{:S(2)}) async-start(bf16[4,128,640]{2,1,0:T(8,128)(2,1)} %get-tuple-element.224), calls=%async_computation.2 | async-start | bytes 1310720 | tf_op jit(solution)/shard_map/all_to_all | solution.py:830
  224.4 20.6 %collective-permute-start.19 = (bf16[128,1536]{1,0:T(8,128)(2,1)}, bf16[128,1536]{1,0:T(8,128)(2,1)S(1)}, u32[]{:S(2)}, u32[]{:S(2)}) collective-permute-start(bf16[128,1536]{1,0:T(8,128)(2,1)} %collective-permute-done.16.refs_2_), channel_id=1, source_target_pairs={{0,1},{1,0},{2,3},{3,2},{4,5},{5,4},{6,7},{7,6},{8,9},{9,8},{10,11... | collective-permute-start | bytes 1179656 | tf_op jit(solution)/shard_map/ppermute | solution.py:616
  259.4 13.8 %collective-permute-start.22 = (bf16[2,1,192,512]{3,2,1,0:T(8,128)(2,1)S(1)}, bf16[2,1,192,512]{3,2,1,0:T(8,128)(2,1)S(1)}, u32[]{:S(2)}, u32[]{:S(2)}) collective-permute-start(bf16[2,1,192,512]{3,2,1,0:T(8,128)(2,1)S(1)} %get-tuple-element.247), channel_id=1, source_target_pairs={{0,8},{4,12},{8,0},{12,4},{16,24},{20,28},{24,16},{28,20},{1,9},{5... | collective-permute-start | bytes 1179656 | tf_op jit(solution)/shard_map/ppermute | solution.py:616
  260.2 20.0 %collective-permute-start.24 = (bf16[128,1536]{1,0:T(8,128)(2,1)S(1)}, bf16[128,1536]{1,0:T(8,128)(2,1)S(1)}, u32[]{:S(2)}, u32[]{:S(2)}) collective-permute-start(bf16[128,1536]{1,0:T(8,128)(2,1)S(1)} %bitcast.37), channel_id=1, source_target_pairs={{0,2},{1,3},{2,0},{3,1},{4,6},{5,7},{6,4},{7,5},{8,10},{9,11},{10,... | collective-permute-start | bytes 1179656 | tf_op jit(solution)/shard_map/ppermute | solution.py:616
  262.3 13.2 %collective-permute-start.23 = (bf16[2,1,192,640]{3,2,1,0:T(8,128)(2,1)S(1)}, bf16[2,1,192,640]{3,2,1,0:T(8,128)(2,1)S(1)}, u32[]{:S(2)}, u32[]{:S(2)}) collective-permute-start(bf16[2,1,192,640]{3,2,1,0:T(8,128)(2,1)S(1)} %get-tuple-element.249), channel_id=1, source_target_pairs={{0,16},{4,20},{8,24},{12,28},{16,0},{20,4},{24,8},{28,12},{1,17},{... | collective-permute-start | bytes 1474568 | tf_op jit(solution)/shard_map/ppermute | solution.py:616
  280.2 11.6 %collective-permute-start.25 = (bf16[1,192,512]{2,1,0:T(8,128)(2,1)S(1)}, bf16[1,192,512]{2,1,0:T(8,128)(2,1)S(1)}, u32[]{:S(2)}, u32[]{:S(2)}) collective-permute-start(bf16[1,192,512]{2,1,0:T(8,128)(2,1)S(1)} %get-tuple-element.258), channel_id=1, source_target_pairs={{0,16},{4,20},{8,24},{12,28},{16,0},{20,4},{24,8},{28,12},{1,17},{... | collective-permute-start | bytes 589832 | tf_op jit(solution)/shard_map/ppermute | solution.py:616
  280.8 13.7 %collective-permute-start.26 = (bf16[1,192,640]{2,1,0:T(8,128)(2,1)S(1)}, bf16[1,192,640]{2,1,0:T(8,128)(2,1)S(1)}, u32[]{:S(2)}, u32[]{:S(2)}) collective-permute-start(bf16[1,192,640]{2,1,0:T(8,128)(2,1)S(1)} %get-tuple-element.260), channel_id=1, source_target_pairs={{0,8},{4,12},{8,0},{12,4},{16,24},{20,28},{24,16},{28,20},{1,9},{5... | collective-permute-start | bytes 737288 | tf_op jit(solution)/shard_map/ppermute | solution.py:616
  294.6 26.7 %collective-permute-start.30 = (bf16[2,1,576,256]{3,2,1,0:T(8,128)(2,1)S(1)}, bf16[2,1,576,256]{3,2,1,0:T(8,128)(2,1)S(1)}, u32[]{:S(2)}, u32[]{:S(2)}) collective-permute-start(bf16[2,1,576,256]{3,2,1,0:T(8,128)(2,1)S(1)} %copy-done.33), channel_id=1, source_target_pairs={{0,8},{4,12},{8,0},{12,4},{16,24},{20,28},{24,16},{28,20},{1,9},{5... | collective-permute-start | bytes 1769480 | tf_op jit(solution)/shard_map/ppermute | solution.py:616
  295.9 20.4 %collective-permute-start.28 = (bf16[192,1152]{1,0:T(8,128)(2,1)S(1)}, bf16[192,1152]{1,0:T(8,128)(2,1)S(1)}, u32[]{:S(2)}, u32[]{:S(2)}) collective-permute-start(bf16[192,1152]{1,0:T(8,128)(2,1)S(1)} %maximum_bitcast_fusion.refs_0_), channel_id=1, source_target_pairs={{0,2},{1,3},{2,0},{3,1},{4,6},{5,7},{6,4},{7,5},{8,10},{9,11},{10,... | collective-permute-start | bytes 1327112 | tf_op jit(solution)/shard_map/ppermute | solution.py:616
  295.9 27.2 %collective-permute-start.32 = (bf16[2,1,576,256]{3,2,1,0:T(8,128)(2,1)S(1)}, bf16[2,1,576,256]{3,2,1,0:T(8,128)(2,1)S(1)}, u32[]{:S(2)}, u32[]{:S(2)}) collective-permute-start(bf16[2,1,576,256]{3,2,1,0:T(8,128)(2,1)S(1)} %copy-done.31), channel_id=1, source_target_pairs={{0,16},{4,20},{8,24},{12,28},{16,0},{20,4},{24,8},{28,12},{1,17},{... | collective-permute-start | bytes 1769480 | tf_op jit(solution)/shard_map/ppermute | solution.py:616
  297.4 32.2 %collective-permute-start.27 = (bf16[192,1152]{1,0:T(8,128)(2,1)S(1)}, bf16[192,1152]{1,0:T(8,128)(2,1)S(1)}, u32[]{:S(2)}, u32[]{:S(2)}) collective-permute-start(bf16[192,1152]{1,0:T(8,128)(2,1)S(1)} %maximum_bitcast_fusion.refs_0_), channel_id=1, source_target_pairs={{0,1},{1,0},{2,3},{3,2},{4,5},{5,4},{6,7},{7,6},{8,9},{9,8},{10,11... | collective-permute-start | bytes 1327112 | tf_op jit(solution)/shard_map/ppermute | solution.py:616
  316.2 13.3 %collective-permute-start.29 = (bf16[192,1152]{1,0:T(8,128)(2,1)S(1)}, bf16[192,1152]{1,0:T(8,128)(2,1)S(1)}, u32[]{:S(2)}, u32[]{:S(2)}) collective-permute-start(bf16[192,1152]{1,0:T(8,128)(2,1)S(1)} %collective-permute-done.28.refs_2_), channel_id=1, source_target_pairs={{0,1},{1,0},{2,3},{3,2},{4,5},{5,4},{6,7},{7,6},{8,9},{9,8},{10,11... | collective-permute-start | bytes 1327112 | tf_op jit(solution)/shard_map/ppermute | solution.py:616
  321.5 12.0 %collective-permute-start.31 = (bf16[1,576,256]{2,1,0:T(8,128)(2,1)S(1)}, bf16[1,576,256]{2,1,0:T(8,128)(2,1)S(1)}, u32[]{:S(2)}, u32[]{:S(2)}) collective-permute-start(bf16[1,576,256]{2,1,0:T(8,128)(2,1)S(1)} %get-tuple-element.336), channel_id=1, source_target_pairs={{0,16},{4,20},{8,24},{12,28},{16,0},{20,4},{24,8},{28,12},{1,17},{... | collective-permute-start | bytes 884744 | tf_op jit(solution)/shard_map/ppermute | solution.py:616
  (56 other events, 548.3 us)
Sparse Core Ops, SparseCore 0:
  9.9 54.3 all-gather.1
  172.5 149.6 reduce-scatter.1

commit v6 on v5

--- a/solution.py
+++ b/solution.py
@@ -312,22 +312,25 @@
 
 def forward_kernel(places, kv, experts, dev_ref, tok_ref, cos_ref, sin_ref, segr_ref, segc_ref, q_hbm, *refs):
     pieces, refs = refs[:len(places)], refs[len(places):]
-    qkv_ref, mix_ref, resid_ref, n2_ref, gains_ref, router_ref, kv_ref, wq, wo, sems = refs
+    qkv_ref, mix_ref, resid_ref, n2_ref, gains_ref, router_ref, kv_ref, wq, wkv, wsm, wo, sems = refs
     T, W = tok_ref.shape
     C = 512
     chunks = W // C
-    fetched = fetch(places, pieces, dev_ref[1], wo, sems, chunks, 0, wo.shape[1])
+    some = len(places)
+    fetched = fetch(places, pieces, dev_ref[1], wkv, sems, chunks, 0, 2 * kv)
+    fetched += fetch(places, pieces, dev_ref[1], wsm, sems, chunks + some, 2 * kv + W, 2 * kv + W + 128)
     copies = []
     for j in range(chunks):
         copies.append(pltpu.make_async_copy(q_hbm.at[:, j * C:(j + 1) * C], wq.at[j], sems.at[j]))
         copies[-1].start()
+    late = fetch(places, pieces, dev_ref[1], wo, sems, chunks + 2 * some, 2 * kv, 2 * kv + W)
     x = tok_ref[...].astype(F32)
     inverse = lax.rsqrt(jnp.mean(x * x, axis=1, keepdims=True) + EPSILON)
     for copy in fetched:
         copy.wait()
-    keep = pltpu.make_async_copy(wo.at[:, :2 * kv], kv_ref, sems.at[chunks + len(places)])
+    keep = pltpu.make_async_copy(wkv, kv_ref, sems.at[chunks + 3 * some])
     keep.start()
-    small = wo[:, 2 * kv + W:]
+    small = wsm[...]
     router_ref[...] = small
     turned = small.astype(F32).T
     gain1, gain2 = turned[experts:experts + 1, :], turned[experts + 1:experts + 2, :]
@@ -338,7 +341,7 @@
     cosine, sine = cos_ref[...], sin_ref[...]
     q_tiles = W // 128
     k_tiles = kv // 128
-    side = dot_nn(n1, wo[:, :2 * kv])
+    side = dot_nn(n1, wkv[...])
     others = [side[:, t * 128:(t + 1) * 128] for t in range(2 * k_tiles)]
     others = [rope_tile(t, cosine, sine).astype(BF) for t in others[:k_tiles]] + [t.astype(BF) for t in others[k_tiles:]]
     tiles = []
@@ -361,10 +364,12 @@
         unstacked(dot_nn(p.astype(BF), v_tile), g, per, T, mixed)
     for t in range(q_tiles):
         mix_ref[:, t * 128:(t + 1) * 128] = mixed[t].astype(BF)
+    for copy in late:
+        copy.wait()
     total = jnp.zeros((T, 1), F32)
     for j in range(chunks):
         cols = slice(j * C, (j + 1) * C)
-        r = tok_ref[:, cols].astype(F32) + dot_nn(mix_ref[...], wo[:, 2 * kv + j * C:2 * kv + (j + 1) * C])
+        r = tok_ref[:, cols].astype(F32) + dot_nn(mix_ref[...], wo[:, cols])
         resid_ref[:, cols] = r
         total = total + jnp.sum(r * r, axis=1, keepdims=True)
     inverse = lax.rsqrt(total / W + EPSILON)
@@ -383,8 +388,8 @@
         out_shape=(S((T, N), BF), S((T, W), BF), S((T, W), F32), S((T, W), BF), S((8, W), F32), S((W, 128), BF), S((W, 2 * kv), BF)),
         in_specs=[pl.BlockSpec(memory_space=pltpu.SMEM)] + [v] * 5 + [hbm] * (1 + len(places)),
         out_specs=(v,) * 6 + (hbm,),
-        scratch_shapes=[pltpu.VMEM((W // 512, W, 512), BF), pltpu.VMEM((W, N + 128), BF),
-                        pltpu.SemaphoreType.DMA((W // 512 + len(places) + 1,))],
+        scratch_shapes=[pltpu.VMEM((W // 512, W, 512), BF), pltpu.VMEM((W, 2 * kv), BF), pltpu.VMEM((W, 128), BF), pltpu.VMEM((W, W), BF),
+                        pltpu.SemaphoreType.DMA((W // 512 + 3 * len(places) + 1,))],
         compiler_params=pltpu.CompilerParams(vmem_limit_bytes=60 << 20),
         cost_estimate=pl.CostEstimate(flops=0, bytes_accessed=0, transcendentals=0),
     )(where, tokens, cosine, sine, segr, segc, q_w, *pieces)

time: 343 us -> 342 us (level)
  no operation moved by 1% of the time
where the time goes in v6:
time: 342 us; the launch traced here: 341 us
  waiting for transfers between devices  119 us (35%)
  Pallas kernels  119 us (35%)
  starting transfers between devices  48.7 us (14%)
  local copies, waits for them, and re-layouts  32.9 us (10%)
  between operations  14.7 us (4%)
  other arithmetic  6.45 us (2%)
    ppermute x34, waiting for transfers between devices, flip(): return lax.ppermute(x, axis, [(i, i ^ mask) for i in range(size)])  114 us
    ppermute x34, starting transfers between devices, flip(): return lax.ppermute(x, axis, [(i, i ^ mask) for i in range(size)])  37.1 us
    pallas_call x1, Pallas kernels, expert_rows(): pl.pallas_call(functools.partial(expert_kernel, blocks, choices), out_sha...  26.6 us
    pallas_call x2, Pallas kernels, expert_grads(): pl.pallas_call(functools.partial(grad_kernel, blocks, apart), out_shape=(...  25.5 us
    unnamed x100, local copies, waits for them, and re-layouts  19.9 us
    all_to_all x3, starting transfers between devices, local(): lax.all_to_all(x, 'expert', split_axis=0, concat_axis=0, tiled=True)  11.5 us
    pallas_call x1, Pallas kernels, backward(): pl.pallas_call(functools.partial(backward_kernel, places), out_shape=(S((...  11.1 us
    pallas_call x1, Pallas kernels, combine(): pl.pallas_call(combine_kernel, out_shape=(jax.ShapeDtypeStruct((blocks //...  11 us
  transfers between devices with their start and end apart: 39, of which 20 were waited for; matrix products, arithmetic and copies ran while one was open for 6% of the time, Pallas kernels for 31%

profile of v6, /device:TPU:0, one launch (start us, length us, event | category | flops | bytes accessed | tf_op | source)
XLA Modules:
  0.0 340.7 jit_solution(48551743355323305)
XLA Ops:
  12.6 3.0 collective-permute-start.1
  26.6 21.0 %collective-permute-done.1.refs_4_ = bf16[192,2688]{1,0:T(8,128)(2,1)} collective-permute-done((bf16[192,2688]{1,0:T(8,128)(2,1)S(1)}, bf16[192,2688]{1,0:T(8,128)(2,1)}, u32[]{:S(2)}, u32[]{:S(2)}) %collective-permute-start.1) | collective-permute-done | bytes 1032224 | tf_op jit(solution)/shard_map/ppermute | solution.py:621
  47.5 2.7 collective-permute-done.refs_2_
  52.1 3.2 collective-permute-done.3.refs_2_.refs_6_
  58.1 9.9 %collective-permute-done.8.refs_6_ = bf16[192,1280]{1,0:T(8,128)(2,1)} collective-permute-done((bf16[192,1280]{1,0:T(8,128)(2,1)S(1)}, bf16[192,1280]{1,0:T(8,128)(2,1)}, u32[]{:S(2)}, u32[]{:S(2)}) %collective-permute-start.8) | collective-permute-done | bytes 491552 | tf_op jit(solution)/shard_map/ppermute | solution.py:621
  68.0 3.1 collective-permute-done.9.refs_7_
  71.1 3.3 collective-permute-done.4.refs_3_.refs_7_
  76.7 10.7 %shard_map.229 = (bf16[128,2560]{1,0:T(8,128)(2,1)}, bf16[128,1536]{1,0:T(8,128)(2,1)}, f32[128,1536]{1,0:T(8,128)}, bf16[128,1536]{1,0:T(8,128)(2,1)}, f32[8,15...) custom-call(s32[4]{0:T(128)} %pad_add_fusion.dev_ref.where_ref, bf16[128,1536]{1,0:T(8,128)(2,1)} %tok_ref.3, ...), custom_call_target="tpu_custom_call" | custom-call | tf_op jit(solution)/shard_map/pallas_call | solution.py:386
  87.5 3.4 %collective-permute-start.13 = (bf16[128,1536]{1,0:T(8,128)(2,1)}, bf16[128,1536]{1,0:T(8,128)(2,1)}, u32[]{:S(2)}, u32[]{:S(2)}) collective-permute-start(bf16[128,1536]{1,0:T(8,128)(2,1)} %get-tuple-element.177.refs_0_.refs_3_), channel_id=1, source_target_pairs={{0,2},{1,3},{2,0},{3,1},{4,6},{5,7},{6,4},{7,5},{8,10},{9,11},{10,... | collective-permute-start | bytes 1179656 | tf_op jit(solution)/shard_map/ppermute | solution.py:621
  92.7 9.6 %shard_map.230.refs_11_ = f32[5,512,512]{2,1,0:T(8,128)} custom-call(bf16[128,3200]{1,0:T(8,128)(2,1)} %copy-done, bf16[128,3200]{1,0:T(8,128)(2,1)} %copy-done.5, bf16[128,3200]{1,0:T(8,128)(2,1)} %copy-done.3, bf16[128,3200]{1,0:T(8,128)(2,1)} %copy-done.7, bf16[5,512,1536]{2,1,0:T(8,128)(2,1)} %down_ref.1), custom_call_target="tpu_custom_call" | custom-call | tf_op jit(solution)/shard_map/pallas_call | solution.py:219
  104.8 4.6 %collective-permute-done.13.refs_2_ = bf16[128,1536]{1,0:T(8,128)(2,1)} collective-permute-done((bf16[128,1536]{1,0:T(8,128)(2,1)}, bf16[128,1536]{1,0:T(8,128)(2,1)}, u32[]{:S(2)}, u32[]{:S(2)}) %collective-permute-start.13) | collective-permute-done | bytes 393248 | tf_op jit(solution)/shard_map/ppermute | solution.py:621
  111.1 9.3 %collective-permute-done.14.refs_3_ = bf16[128,1536]{1,0:T(8,128)(2,1)S(1)} collective-permute-done((bf16[128,1536]{1,0:T(8,128)(2,1)}, bf16[128,1536]{1,0:T(8,128)(2,1)S(1)}, u32[]{:S(2)}, u32[]{:S(2)}) %collective-permute-start.14) | collective-permute-done | bytes 393248 | tf_op jit(solution)/shard_map/ppermute | solution.py:621
  124.7 26.6 %shard_map.232 = (bf16[4,128,1664]{2,1,0:T(8,128)(2,1)}, f32[512,128]{1,0:T(8,128)}, bf16[1536,512]{1,0:T(8,128)(2,1)}, bf16[5,512,512]{2,1,0:T(8,128)(2,1)}, bf...) custom-call(s32[4]{0:T(128)} %pad_add_fusion.dev_ref.where_ref, ...), custom_call_target="tpu_custom_call" | custom-call | flops 16106127360 | bytes 33030144 | tf_op jit(solution)/shard_map/pallas_call | solution.py:97
  152.0 3.6 %all-to-all-start = ((bf16[4,128,1664]{2,1,0:T(8,128)(2,1)}), bf16[4,128,1664]{2,1,0:T(8,128)(2,1)S(1)}, u32[]{:S(2)}, u32[]{:S(2)}) async-start(bf16[4,128,1664]{2,1,0:T(8,128)(2,1)} %get-tuple-element.191), calls=%async_computation | async-start | bytes 3407872 | tf_op jit(solution)/shard_map/all_to_all | solution.py:835
  155.7 16.0 %shard_map.233 = bf16[8,4,576,512]{3,2,1,0:T(8,128)(2,1)} custom-call(s32[4]{0:T(128)} %pad_add_fusion.dev_ref.where_ref, bf16[128,3200]{1,0:T(8,128)(2,1)} %copy-done, bf16[128,3200]{1,0:T(8,128)(2,1)} %copy-done.5, bf16[128,3200]{1,0:T(8,128)(2,1)} %copy-done.3, bf16[128,3200]{1,0:T(8,128)(2,1)} %copy-done.7, ...), custom_call_target="tpu_custom_call" | custom-call | tf_op jit(solution)/shard_map/pallas_call | solution.py:151
  171.7 9.5 %shard_map.234 = (bf16[4,1,576,512]{3,2,1,0:T(8,128)(2,1)}, bf16[4,1,576,512]{3,2,1,0:T(8,128)(2,1)}) custom-call(s32[4]{0:T(128)} %pad_add_fusion.dev_ref.where_ref, bf16[128,3200]{1,0:T(8,128)(2,1)} %copy-done, bf16[128,3200]{1,0:T(8,128)(2,1)} %copy-done.5, bf16[128,3200]{1,0:T(8,128)(2,1)} %copy-done.3, bf16[128,3200]{1,0:T(8,128)(2,1)} %copy-done.7, ...), custom_call_target="tpu_custom_call" | custom-call | tf_op jit(solution)/shard_map/pallas_call | solution.py:151
  181.2 11.0 %shard_map.235 = (bf16[2,128,1536]{2,1,0:T(8,128)(2,1)}, bf16[2,128,1536]{2,1,0:T(8,128)(2,1)}) custom-call(bf16[5,512,512]{2,1,0:T(8,128)(2,1)} %get-tuple-element.200.weighed_ref, bf16[5,512,1536]{2,1,0:T(8,128)(2,1)} %down_ref.1), custom_call_target="tpu_custom_call" | custom-call | tf_op jit(solution)/shard_map/pallas_call | solution.py:190
  202.7 3.7 %all-to-all-start.1 = ((bf16[4,128,384]{2,1,0:T(8,128)(2,1)}), bf16[4,128,384]{2,1,0:T(8,128)(2,1)S(1)}, u32[]{:S(2)}, u32[]{:S(2)}) async-start(bf16[4,128,384]{2,1,0:T(8,128)(2,1)} %copy-done.23), calls=%async_computation.1 | async-start | bytes 786432 | tf_op jit(solution)/shard_map/all_to_all | solution.py:835
  206.4 11.1 %shard_map.237 = (bf16[128,2560]{1,0:T(8,128)(2,1)}, bf16[4,128,640]{2,1,0:T(8,128)(2,1)}) custom-call(s32[4]{0:T(128)} %pad_add_fusion.dev_ref.where_ref, bf16[128,1536]{1,0:T(8,128)(2,1)} %copy-done.22, bf16[128,2560]{1,0:T(8,128)(2,1)} %get-tuple-element.211.qkv_ref, f32[128,128]{1,0:T(8,128)} %copy.60.cos_ref, f32[128,128]{1,0:T(8,128)} %pad_maximum_fusion.sin_ref, ...), custom_call_target="tpu_custom_call" | custom-call | tf_op jit(solution)/shard_map/pallas_call | solution.py:501
  219.5 4.2 %all-to-all-start.2 = ((bf16[4,128,640]{2,1,0:T(8,128)(2,1)}), bf16[4,128,640]{2,1,0:T(8,128)(2,1)}, u32[]{:S(2)}, u32[]{:S(2)}) async-start(bf16[4,128,640]{2,1,0:T(8,128)(2,1)} %get-tuple-element.224), calls=%async_computation.2 | async-start | bytes 1310720 | tf_op jit(solution)/shard_map/all_to_all | solution.py:835
  232.4 2.8 copy-done.2
  235.2 4.4 %shard_map.239 = (f32[128,1536]{1,0:T(8,128)}, f32[1536,128]{1,0:T(8,128)S(1)}) custom-call(bf16[128,2560]{1,0:T(8,128)(2,1)S(1)} %copy-done.18, bf16[128,1536]{1,0:T(8,128)(2,1)S(1)} %copy-done.10, f32[8,1536]{1,0:T(8,128)S(1)} %copy-done.26, f32[128,1536]{1,0:T(8,128)S(1)} %get-tuple-element.226.resid_back_ref, ...), custom_call_target="tpu_custom_call" | custom-call | tf_op jit(solution)/shard_map/pallas_call | solution.py:537
  240.5 3.8 %collective-permute-done.19.refs_3_ = bf16[128,1536]{1,0:T(8,128)(2,1)S(1)} collective-permute-done((bf16[128,1536]{1,0:T(8,128)(2,1)}, bf16[128,1536]{1,0:T(8,128)(2,1)S(1)}, u32[]{:S(2)}, u32[]{:S(2)}) %collective-permute-start.19) | collective-permute-done | bytes 393248 | tf_op jit(solution)/shard_map/ppermute | solution.py:621
  245.1 3.7 %shard_map.240 = (bf16[4,1,192,384]{3,2,1,0:T(8,128)(2,1)}, bf16[4,1,192,384]{3,2,1,0:T(8,128)(2,1)}) custom-call(s32[4]{0:T(128)} %pad_add_fusion.dev_ref.where_ref, bf16[128,1536]{1,0:T(8,128)(2,1)} %get-tuple-element.230.refs_0_, bf16[128,1536]{1,0:T(8,128)(2,1)} %copy-done.44, bf16[128,1536]{1,0:T(8,128)(2,1)} %collective-permute-done.16.refs_2_, ...), custom_call_target="tpu_custom_call" | custom-call | tf_op jit(solution)/shard_map/pallas_call | solution.py:572
  248.9 5.1 %shard_map.241 = (bf16[4,1,192,768]{3,2,1,0:T(8,128)(2,1)}, bf16[4,1,192,768]{3,2,1,0:T(8,128)(2,1)}) custom-call(s32[4]{0:T(128)} %pad_add_fusion.dev_ref.where_ref, bf16[2,4,192,512]{3,2,1,0:T(8,128)(2,1)} %copy-done.14, bf16[4,128,640]{2,1,0:T(8,128)(2,1)} %all-to-all-done.2.qkv_ref, f32[1536,128]{1,0:T(8,128)} %copy-done.29), custom_call_target="tpu_custom_call" | custom-call | flops 1207959552 | bytes 4718592 | tf_op jit(solution)/shard_map/pallas_call | solution.py:610
  254.3 2.7 collective-permute-done.21.refs_3_
  262.3 10.2 %collective-permute-done.22 = bf16[2,1,192,512]{3,2,1,0:T(8,128)(2,1)S(1)} collective-permute-done((bf16[2,1,192,512]{3,2,1,0:T(8,128)(2,1)S(1)}, bf16[2,1,192,512]{3,2,1,0:T(8,128)(2,1)S(1)}, u32[]{:S(2)}, u32[]{:S(2)}) %collective-permute-start.22) | collective-permute-done | bytes 393248 | tf_op jit(solution)/shard_map/ppermute | solution.py:621
  275.0 4.6 %collective-permute-done.24 = bf16[128,1536]{1,0:T(8,128)(2,1)S(1)} collective-permute-done((bf16[128,1536]{1,0:T(8,128)(2,1)S(1)}, bf16[128,1536]{1,0:T(8,128)(2,1)S(1)}, u32[]{:S(2)}, u32[]{:S(2)}) %collective-permute-start.24) | collective-permute-done | bytes 393248 | tf_op jit(solution)/shard_map/ppermute | solution.py:621
  281.4 9.8 %collective-permute-done.25 = bf16[1,192,512]{2,1,0:T(8,128)(2,1)S(1)} collective-permute-done((bf16[1,192,512]{2,1,0:T(8,128)(2,1)S(1)}, bf16[1,192,512]{2,1,0:T(8,128)(2,1)S(1)}, u32[]{:S(2)}, u32[]{:S(2)}) %collective-permute-start.25) | collective-permute-done | bytes 196640 | tf_op jit(solution)/shard_map/ppermute | solution.py:621
  296.7 2.9 collective-permute-start.27
  299.6 15.9 %collective-permute-done.28.refs_2_ = bf16[192,1152]{1,0:T(8,128)(2,1)S(1)} collective-permute-done((bf16[192,1152]{1,0:T(8,128)(2,1)S(1)}, bf16[192,1152]{1,0:T(8,128)(2,1)S(1)}, u32[]{:S(2)}, u32[]{:S(2)}) %collective-permute-start.28) | collective-permute-done | bytes 442400 | tf_op jit(solution)/shard_map/ppermute | solution.py:621
  315.6 5.1 %collective-permute-done.30 = bf16[2,1,576,256]{3,2,1,0:T(8,128)(2,1)S(1)} collective-permute-done((bf16[2,1,576,256]{3,2,1,0:T(8,128)(2,1)S(1)}, bf16[2,1,576,256]{3,2,1,0:T(8,128)(2,1)S(1)}, u32[]{:S(2)}, u32[]{:S(2)}) %collective-permute-start.30) | collective-permute-done | bytes 589856 | tf_op jit(solution)/shard_map/ppermute | solution.py:621
  (199 shorter events, 85.5 us)
Async XLA Ops:
  7.2 69.5 %all-gather.2.cloned.1.call-start = ((), (), s32[]{:S(2)}) async-start(), calls=%async_computation.4 | async-start | bytes 5308416 | tf_op jit(solution)/shard_map/all_gather | solution.py:818
  12.6 35.0 %collective-permute-start.1 = (bf16[192,2688]{1,0:T(8,128)(2,1)S(1)}, bf16[192,2688]{1,0:T(8,128)(2,1)}, u32[]{:S(2)}, u32[]{:S(2)}) collective-permute-start(bf16[192,2688]{1,0:T(8,128)(2,1)S(1)} %concatenate.13.refs_0_), channel_id=1, source_target_pairs={{0,16},{4,20},{8,24},{12,28},{16,0},{20,4},{24,8},{28,12},{1,17},{... | collective-permute-start | bytes 3096584 | tf_op jit(solution)/shard_map/ppermute | solution.py:621
  15.6 34.7 %collective-permute-start = (bf16[192,2688]{1,0:T(8,128)(2,1)S(1)}, bf16[192,2688]{1,0:T(8,128)(2,1)}, u32[]{:S(2)}, u32[]{:S(2)}) collective-permute-start(bf16[192,2688]{1,0:T(8,128)(2,1)S(1)} %concatenate.13.refs_0_), channel_id=1, source_target_pairs={{0,8},{4,12},{8,0},{12,4},{16,24},{20,28},{24,16},{28,20},{1,9},{5... | collective-permute-start | bytes 3096584 | tf_op jit(solution)/shard_map/ppermute | solution.py:621
  17.3 38.0 %collective-permute-start.3 = (bf16[128,3200]{1,0:T(8,128)(2,1)S(1)}, bf16[128,3200]{1,0:T(8,128)(2,1)S(1)}, u32[]{:S(2)}, u32[]{:S(2)}) collective-permute-start(bf16[128,3200]{1,0:T(8,128)(2,1)S(1)} %fusion.3.refs_0_.refs_4_), channel_id=1, source_target_pairs={{0,2},{1,3},{2,0},{3,1},{4,6},{5,7},{6,4},{7,5},{8,10},{9,11},{10,... | collective-permute-start | bytes 2457608 | tf_op jit(solution)/shard_map/ppermute | solution.py:621
  20.0 37.7 %collective-permute-start.2 = (bf16[128,3200]{1,0:T(8,128)(2,1)S(1)}, bf16[128,3200]{1,0:T(8,128)(2,1)S(1)}, u32[]{:S(2)}, u32[]{:S(2)}) collective-permute-start(bf16[128,3200]{1,0:T(8,128)(2,1)S(1)} %fusion.3.refs_0_.refs_4_), channel_id=1, source_target_pairs={{0,1},{1,0},{2,3},{3,2},{4,5},{5,4},{6,7},{7,6},{8,9},{9,8},{10,11... | collective-permute-start | bytes 2457608 | tf_op jit(solution)/shard_map/ppermute | solution.py:621
  52.0 16.0 %collective-permute-start.8 = (bf16[192,1280]{1,0:T(8,128)(2,1)S(1)}, bf16[192,1280]{1,0:T(8,128)(2,1)}, u32[]{:S(2)}, u32[]{:S(2)}) collective-permute-start(bf16[192,1280]{1,0:T(8,128)(2,1)S(1)} %slice.46), channel_id=1, source_target_pairs={{0,16},{4,20},{8,24},{12,28},{16,0},{20,4},{24,8},{28,12},{1,17},{... | collective-permute-start | bytes 1474568 | tf_op jit(solution)/shard_map/ppermute | solution.py:621
  55.4 19.0 %collective-permute-start.4 = (bf16[128,3200]{1,0:T(8,128)(2,1)S(1)}, bf16[128,3200]{1,0:T(8,128)(2,1)S(1)}, u32[]{:S(2)}, u32[]{:S(2)}) collective-permute-start(bf16[128,3200]{1,0:T(8,128)(2,1)S(1)} %collective-permute-done.3.refs_2_.refs_6_), channel_id=1, source_target_pairs={{0,1},{1,0},{2,3},{3,2},{4,5},{5,4},{6,7},{7,6},{8,9},{9,8},{10,11... | collective-permute-start | bytes 2457608 | tf_op jit(solution)/shard_map/ppermute | solution.py:621
  57.0 14.1 %collective-permute-start.9 = (bf16[192,1408]{1,0:T(8,128)(2,1)S(1)}, bf16[192,1408]{1,0:T(8,128)(2,1)}, u32[]{:S(2)}, u32[]{:S(2)}) collective-permute-start(bf16[192,1408]{1,0:T(8,128)(2,1)S(1)} %slice.47), channel_id=1, source_target_pairs={{0,8},{4,12},{8,0},{12,4},{16,24},{20,28},{24,16},{28,20},{1,9},{5... | collective-permute-start | bytes 1622024 | tf_op jit(solution)/shard_map/ppermute | solution.py:621
  57.6 19.0 %collective-permute-start.6 = (bf16[192,2688]{1,0:T(8,128)(2,1)}, bf16[192,2688]{1,0:T(8,128)(2,1)}, u32[]{:S(2)}, u32[]{:S(2)}) collective-permute-start(bf16[192,2688]{1,0:T(8,128)(2,1)} %collective-permute-done.refs_2_), channel_id=1, source_target_pairs={{0,4},{4,0},{8,12},{12,8},{16,20},{20,16},{24,28},{28,24},{1,5},{5... | collective-permute-start | bytes 3096584 | tf_op jit(solution)/shard_map/ppermute | solution.py:621
  57.6 19.0 %collective-permute-start.5 = (bf16[192,2688]{1,0:T(8,128)(2,1)}, bf16[192,2688]{1,0:T(8,128)(2,1)}, u32[]{:S(2)}, u32[]{:S(2)}) collective-permute-start(bf16[192,2688]{1,0:T(8,128)(2,1)} %copy-done.37), channel_id=1, source_target_pairs={{0,4},{4,0},{8,12},{12,8},{16,20},{20,16},{24,28},{28,24},{1,5},{5... | collective-permute-start | bytes 3096584 | tf_op jit(solution)/shard_map/ppermute | solution.py:621
  87.5 21.9 %collective-permute-start.13 = (bf16[128,1536]{1,0:T(8,128)(2,1)}, bf16[128,1536]{1,0:T(8,128)(2,1)}, u32[]{:S(2)}, u32[]{:S(2)}) collective-permute-start(bf16[128,1536]{1,0:T(8,128)(2,1)} %get-tuple-element.177.refs_0_.refs_3_), channel_id=1, source_target_pairs={{0,2},{1,3},{2,0},{3,1},{4,6},{5,7},{6,4},{7,5},{8,10},{9,11},{10,... | collective-permute-start | bytes 1179656 | tf_op jit(solution)/shard_map/ppermute | solution.py:621
  90.9 18.6 %collective-permute-start.12 = (bf16[128,1536]{1,0:T(8,128)(2,1)}, bf16[128,1536]{1,0:T(8,128)(2,1)}, u32[]{:S(2)}, u32[]{:S(2)}) collective-permute-start(bf16[128,1536]{1,0:T(8,128)(2,1)} %get-tuple-element.177.refs_0_.refs_3_), channel_id=1, source_target_pairs={{0,1},{1,0},{2,3},{3,2},{4,5},{5,4},{6,7},{7,6},{8,9},{9,8},{10,11... | collective-permute-start | bytes 1179656 | tf_op jit(solution)/shard_map/ppermute | solution.py:621
  120.4 30.9 %collective-permute-start.16 = (bf16[128,1536]{1,0:T(8,128)(2,1)S(1)}, bf16[128,1536]{1,0:T(8,128)(2,1)}, u32[]{:S(2)}, u32[]{:S(2)}) collective-permute-start(bf16[128,1536]{1,0:T(8,128)(2,1)S(1)} %copy-done.43), channel_id=1, source_target_pairs={{0,2},{1,3},{2,0},{3,1},{4,6},{5,7},{6,4},{7,5},{8,10},{9,11},{10,... | collective-permute-start | bytes 1179656 | tf_op jit(solution)/shard_map/ppermute | solution.py:621
  122.9 28.4 %collective-permute-start.15 = (bf16[128,1536]{1,0:T(8,128)(2,1)S(1)}, bf16[128,1536]{1,0:T(8,128)(2,1)S(1)}, u32[]{:S(2)}, u32[]{:S(2)}) collective-permute-start(bf16[128,1536]{1,0:T(8,128)(2,1)S(1)} %copy-done.43), channel_id=1, source_target_pairs={{0,1},{1,0},{2,3},{3,2},{4,5},{5,4},{6,7},{7,6},{8,9},{9,8},{10,11... | collective-permute-start | bytes 1179656 | tf_op jit(solution)/shard_map/ppermute | solution.py:621
  152.0 42.4 %all-to-all-start = ((bf16[4,128,1664]{2,1,0:T(8,128)(2,1)}), bf16[4,128,1664]{2,1,0:T(8,128)(2,1)S(1)}, u32[]{:S(2)}, u32[]{:S(2)}) async-start(bf16[4,128,1664]{2,1,0:T(8,128)(2,1)} %get-tuple-element.191), calls=%async_computation | async-start | bytes 3407872 | tf_op jit(solution)/shard_map/all_to_all | solution.py:835
  155.6 169.1 %reduce-scatter.2.cloned.1.call-start = ((), (), s32[]{:S(2)}) async-start(), calls=%async_computation.5 | async-start | bytes 21233664 | tf_op jit(solution)/shard_map/reduce_scatter | solution.py:849
  194.5 25.0 %collective-permute-start.18 = (bf16[2,128,1536]{2,1,0:T(8,128)(2,1)}, bf16[2,128,1536]{2,1,0:T(8,128)(2,1)}, u32[]{:S(2)}, u32[]{:S(2)}) collective-permute-start(bf16[2,128,1536]{2,1,0:T(8,128)(2,1)} %get-tuple-element.216), channel_id=1, source_target_pairs={{0,1},{1,0},{2,3},{3,2},{4,5},{5,4},{6,7},{7,6},{8,9},{9,8},{10,11... | collective-permute-start | bytes 2359304 | tf_op jit(solution)/shard_map/ppermute | solution.py:621
  194.5 25.0 %collective-permute-start.17 = (bf16[4,1,576,512]{3,2,1,0:T(8,128)(2,1)}, bf16[4,1,576,512]{3,2,1,0:T(8,128)(2,1)}, u32[]{:S(2)}, u32[]{:S(2)}) collective-permute-start(bf16[4,1,576,512]{3,2,1,0:T(8,128)(2,1)} %get-tuple-element.215), channel_id=1, source_target_pairs={{0,4},{4,0},{8,12},{12,8},{16,20},{20,16},{24,28},{28,24},{1,5},{5... | collective-permute-start | bytes 7077896 | tf_op jit(solution)/shard_map/ppermute | solution.py:621
  202.7 16.8 %all-to-all-start.1 = ((bf16[4,128,384]{2,1,0:T(8,128)(2,1)}), bf16[4,128,384]{2,1,0:T(8,128)(2,1)S(1)}, u32[]{:S(2)}, u32[]{:S(2)}) async-start(bf16[4,128,384]{2,1,0:T(8,128)(2,1)} %copy-done.23), calls=%async_computation.1 | async-start | bytes 786432 | tf_op jit(solution)/shard_map/all_to_all | solution.py:835
  219.5 29.3 %all-to-all-start.2 = ((bf16[4,128,640]{2,1,0:T(8,128)(2,1)}), bf16[4,128,640]{2,1,0:T(8,128)(2,1)}, u32[]{:S(2)}, u32[]{:S(2)}) async-start(bf16[4,128,640]{2,1,0:T(8,128)(2,1)} %get-tuple-element.224), calls=%async_computation.2 | async-start | bytes 1310720 | tf_op jit(solution)/shard_map/all_to_all | solution.py:835
  223.7 20.6 %collective-permute-start.19 = (bf16[128,1536]{1,0:T(8,128)(2,1)}, bf16[128,1536]{1,0:T(8,128)(2,1)S(1)}, u32[]{:S(2)}, u32[]{:S(2)}) collective-permute-start(bf16[128,1536]{1,0:T(8,128)(2,1)} %collective-permute-done.16.refs_2_), channel_id=1, source_target_pairs={{0,1},{1,0},{2,3},{3,2},{4,5},{5,4},{6,7},{7,6},{8,9},{9,8},{10,11... | collective-permute-start | bytes 1179656 | tf_op jit(solution)/shard_map/ppermute | solution.py:621
  258.7 13.8 %collective-permute-start.22 = (bf16[2,1,192,512]{3,2,1,0:T(8,128)(2,1)S(1)}, bf16[2,1,192,512]{3,2,1,0:T(8,128)(2,1)S(1)}, u32[]{:S(2)}, u32[]{:S(2)}) collective-permute-start(bf16[2,1,192,512]{3,2,1,0:T(8,128)(2,1)S(1)} %get-tuple-element.247), channel_id=1, source_target_pairs={{0,8},{4,12},{8,0},{12,4},{16,24},{20,28},{24,16},{28,20},{1,9},{5... | collective-permute-start | bytes 1179656 | tf_op jit(solution)/shard_map/ppermute | solution.py:621
  259.5 20.0 %collective-permute-start.24 = (bf16[128,1536]{1,0:T(8,128)(2,1)S(1)}, bf16[128,1536]{1,0:T(8,128)(2,1)S(1)}, u32[]{:S(2)}, u32[]{:S(2)}) collective-permute-start(bf16[128,1536]{1,0:T(8,128)(2,1)S(1)} %bitcast.37), channel_id=1, source_target_pairs={{0,2},{1,3},{2,0},{3,1},{4,6},{5,7},{6,4},{7,5},{8,10},{9,11},{10,... | collective-permute-start | bytes 1179656 | tf_op jit(solution)/shard_map/ppermute | solution.py:621
  261.6 13.2 %collective-permute-start.23 = (bf16[2,1,192,640]{3,2,1,0:T(8,128)(2,1)S(1)}, bf16[2,1,192,640]{3,2,1,0:T(8,128)(2,1)S(1)}, u32[]{:S(2)}, u32[]{:S(2)}) collective-permute-start(bf16[2,1,192,640]{3,2,1,0:T(8,128)(2,1)S(1)} %get-tuple-element.249), channel_id=1, source_target_pairs={{0,16},{4,20},{8,24},{12,28},{16,0},{20,4},{24,8},{28,12},{1,17},{... | collective-permute-start | bytes 1474568 | tf_op jit(solution)/shard_map/ppermute | solution.py:621
  279.6 11.6 %collective-permute-start.25 = (bf16[1,192,512]{2,1,0:T(8,128)(2,1)S(1)}, bf16[1,192,512]{2,1,0:T(8,128)(2,1)S(1)}, u32[]{:S(2)}, u32[]{:S(2)}) collective-permute-start(bf16[1,192,512]{2,1,0:T(8,128)(2,1)S(1)} %get-tuple-element.258), channel_id=1, source_target_pairs={{0,16},{4,20},{8,24},{12,28},{16,0},{20,4},{24,8},{28,12},{1,17},{... | collective-permute-start | bytes 589832 | tf_op jit(solution)/shard_map/ppermute | solution.py:621
  280.1 13.7 %collective-permute-start.26 = (bf16[1,192,640]{2,1,0:T(8,128)(2,1)S(1)}, bf16[1,192,640]{2,1,0:T(8,128)(2,1)S(1)}, u32[]{:S(2)}, u32[]{:S(2)}) collective-permute-start(bf16[1,192,640]{2,1,0:T(8,128)(2,1)S(1)} %get-tuple-element.260), channel_id=1, source_target_pairs={{0,8},{4,12},{8,0},{12,4},{16,24},{20,28},{24,16},{28,20},{1,9},{5... | collective-permute-start | bytes 737288 | tf_op jit(solution)/shard_map/ppermute | solution.py:621
  293.9 26.7 %collective-permute-start.30 = (bf16[2,1,576,256]{3,2,1,0:T(8,128)(2,1)S(1)}, bf16[2,1,576,256]{3,2,1,0:T(8,128)(2,1)S(1)}, u32[]{:S(2)}, u32[]{:S(2)}) collective-permute-start(bf16[2,1,576,256]{3,2,1,0:T(8,128)(2,1)S(1)} %copy-done.33), channel_id=1, source_target_pairs={{0,8},{4,12},{8,0},{12,4},{16,24},{20,28},{24,16},{28,20},{1,9},{5... | collective-permute-start | bytes 1769480 | tf_op jit(solution)/shard_map/ppermute | solution.py:621
  295.2 20.4 %collective-permute-start.28 = (bf16[192,1152]{1,0:T(8,128)(2,1)S(1)}, bf16[192,1152]{1,0:T(8,128)(2,1)S(1)}, u32[]{:S(2)}, u32[]{:S(2)}) collective-permute-start(bf16[192,1152]{1,0:T(8,128)(2,1)S(1)} %maximum_bitcast_fusion.refs_0_), channel_id=1, source_target_pairs={{0,2},{1,3},{2,0},{3,1},{4,6},{5,7},{6,4},{7,5},{8,10},{9,11},{10,... | collective-permute-start | bytes 1327112 | tf_op jit(solution)/shard_map/ppermute | solution.py:621
  295.2 27.2 %collective-permute-start.32 = (bf16[2,1,576,256]{3,2,1,0:T(8,128)(2,1)S(1)}, bf16[2,1,576,256]{3,2,1,0:T(8,128)(2,1)S(1)}, u32[]{:S(2)}, u32[]{:S(2)}) collective-permute-start(bf16[2,1,576,256]{3,2,1,0:T(8,128)(2,1)S(1)} %copy-done.31), channel_id=1, source_target_pairs={{0,16},{4,20},{8,24},{12,28},{16,0},{20,4},{24,8},{28,12},{1,17},{... | collective-permute-start | bytes 1769480 | tf_op jit(solution)/shard_map/ppermute | solution.py:621
  296.7 32.2 %collective-permute-start.27 = (bf16[192,1152]{1,0:T(8,128)(2,1)S(1)}, bf16[192,1152]{1,0:T(8,128)(2,1)S(1)}, u32[]{:S(2)}, u32[]{:S(2)}) collective-permute-start(bf16[192,1152]{1,0:T(8,128)(2,1)S(1)} %maximum_bitcast_fusion.refs_0_), channel_id=1, source_target_pairs={{0,1},{1,0},{2,3},{3,2},{4,5},{5,4},{6,7},{7,6},{8,9},{9,8},{10,11... | collective-permute-start | bytes 1327112 | tf_op jit(solution)/shard_map/ppermute | solution.py:621
  315.6 13.4 %collective-permute-start.29 = (bf16[192,1152]{1,0:T(8,128)(2,1)S(1)}, bf16[192,1152]{1,0:T(8,128)(2,1)S(1)}, u32[]{:S(2)}, u32[]{:S(2)}) collective-permute-start(bf16[192,1152]{1,0:T(8,128)(2,1)S(1)} %collective-permute-done.28.refs_2_), channel_id=1, source_target_pairs={{0,1},{1,0},{2,3},{3,2},{4,5},{5,4},{6,7},{7,6},{8,9},{9,8},{10,11... | collective-permute-start | bytes 1327112 | tf_op jit(solution)/shard_map/ppermute | solution.py:621
  320.9 12.0 %collective-permute-start.31 = (bf16[1,576,256]{2,1,0:T(8,128)(2,1)S(1)}, bf16[1,576,256]{2,1,0:T(8,128)(2,1)S(1)}, u32[]{:S(2)}, u32[]{:S(2)}) collective-permute-start(bf16[1,576,256]{2,1,0:T(8,128)(2,1)S(1)} %get-tuple-element.336), channel_id=1, source_target_pairs={{0,16},{4,20},{8,24},{12,28},{16,0},{20,4},{24,8},{28,12},{1,17},{... | collective-permute-start | bytes 884744 | tf_op jit(solution)/shard_map/ppermute | solution.py:621
  (56 other events, 545.6 us)
Sparse Core Ops, SparseCore 0:
  9.9 54.3 all-gather.1
  171.8 149.6 reduce-scatter.1
